TPU v7x, 32 devices: a whole 2x2x4 slice. The times are simulated.
32 devices in a mesh: dp: 8 (over y, x, core), mp: 4 (over z).
Axes of the slice: x: 2, y: 2, z: 4, core: 2. Of those that a mesh axis runs over, the one named last changes fastest.
Arguments:
- inputs: bfloat16 [8192, 2048], P(('dp', 'mp')), may hold values from -6 to 6
- w_query: bfloat16 [2048, 2048], P('dp', 'mp'), may hold values from -0.125 to 0.125
- w_key: bfloat16 [2048, 2048], P('dp', 'mp'), may hold values from -0.125 to 0.125
- w_value: bfloat16 [2048, 2048], P('dp', 'mp'), may hold values from -0.125 to 0.125
- q_gain: bfloat16 [16, 128], P('mp', 'dp'), may hold values from 1 to 8
- k_gain: bfloat16 [16, 128], P('mp', 'dp'), may hold values from 1 to 8
- w_out: bfloat16 [2048, 2048], P('mp', 'dp'), may hold values from -0.125 to 0.125
- attn_gain: bfloat16 [2048], P('dp'), may hold values from 0.099609375 to 1.8984375
- w_gate: bfloat16 [2048, 8192], P('dp', 'mp'), may hold values from -0.125 to 0.125
- w_up: bfloat16 [2048, 8192], P('dp', 'mp'), may hold values from -0.125 to 0.125
- w_down: bfloat16 [8192, 2048], P('mp', 'dp'), may hold values from -0.0625 to 0.0625
- mlp_gain: bfloat16 [2048], P('dp'), may hold values from 0.099609375 to 1.8984375
- cotangent: bfloat16 [8192, 2048], P(('dp', 'mp')), may hold values from -6 to 6
Outputs:
- output: float32 [8192, 2048], P(('dp', 'mp'))
- input_grad: float32 [8192, 2048], P(('dp', 'mp'))
- grad_w_query: float32 [2048, 2048], P('dp', 'mp')
- grad_w_key: float32 [2048, 2048], P('dp', 'mp')
- grad_w_value: float32 [2048, 2048], P('dp', 'mp')
- grad_q_gain: float32 [16, 128], P('mp', 'dp')
- grad_k_gain: float32 [16, 128], P('mp', 'dp')
- grad_w_out: float32 [2048, 2048], P('mp', 'dp')
- grad_attn_gain: float32 [2048], P('dp')
- grad_w_gate: float32 [2048, 8192], P('dp', 'mp')
- grad_w_up: float32 [2048, 8192], P('dp', 'mp')
- grad_w_down: float32 [8192, 2048], P('mp', 'dp')
- grad_mlp_gain: float32 [2048], P('dp')
All inputs are finite; a program needn't handle non-finite values.
Results may differ from a plain program's by a relative error of at most 0.02.
The roundings to bfloat16 on the way count: a program that leaves them out, or rounds other values in their place, can miss the bound.
Values may be sent and summed in bfloat16 or wider, within the bound.
No kernel may reach another device: no remote copies, remote signals or barrier semaphores. Data moves between devices by JAX's collectives and lax.ppermute only.
A program may use at most 320 MiB of HBM per device.

v0:
```python
import functools

import jax
import jax.numpy as jnp
from jax import lax
from jax.experimental import pallas as pl
from jax.experimental.layout import Layout, with_layout_constraint
from jax.experimental.pallas import tpu as pltpu
from jax.sharding import PartitionSpec as P


HD = 128
L = 1024

epsilon = 1e-06
rope_base = 500000.0

BF = jnp.bfloat16
F32 = jnp.float32


def dot_plain(left, right):
    return jnp.dot(left, right, preferred_element_type=F32)


def dot_right_t(left, right):
    return lax.dot_general(left, right, (((1,), (1,)), ((), ())), preferred_element_type=F32)


def dot_left_t(left, right):
    return lax.dot_general(left, right, (((0,), (0,)), ((), ())), preferred_element_type=F32)


def row_major(value):
    return with_layout_constraint(value, Layout(major_to_minor=(0, 1)))


def rope_tables():
    half = HD // 2
    freqs = rope_base ** (-2.0 * jnp.arange(half, dtype=F32) / HD)
    angles = jnp.arange(L).astype(F32)[:, None] * freqs[None, :]
    cosine, sine = jnp.cos(angles), jnp.sin(angles)
    return (
        jnp.concatenate([cosine, cosine], axis=1),
        jnp.concatenate([-sine, sine], axis=1),
    )


def masked_scores(queries, keys, rows, last):
    scores = dot_right_t(queries, keys) * (HD ** (-0.5))
    row = lax.broadcasted_iota(jnp.int32, (rows, last), 0) + (last - rows)
    col = lax.broadcasted_iota(jnp.int32, (rows, last), 1)
    return jnp.where(col <= row, scores, -1e30)


def forward_kernel(n, rows, me_ref, *refs):
    q_in, k_in, v_in = refs[:n], refs[n : 2 * n], refs[2 * n : 3 * n]
    rate_q, rate_k, gain_q, gain_k, cosine, sine = refs[3 * n : 3 * n + 6]
    attn, q_out, k_out, v_out, lse = refs[3 * n + 6 :]
    me = me_ref[0]

    def place(s):
        return pl.multiple_of(lax.rem(me - s + n, n) * rows, rows)

    for s in range(n):
        at = pl.ds(place(s), rows)
        c, d = cosine[at, :], sine[at, :]
        for src, rate, gain, dst in (
            (q_in[s], rate_q, gain_q, q_out),
            (k_in[s], rate_k, gain_k, k_out),
        ):
            normed = src[...] * rate[at, :] * gain[0]
            turned = normed * c + pltpu.roll(normed, HD // 2, 1) * d
            dst[at, :] = turned.astype(BF)
        v_out[at, :] = v_in[s][...].astype(BF)
    for piece in range(n):
        first, last = piece * rows, (piece + 1) * rows
        scores = masked_scores(q_out[first:last, :], k_out[:last, :], rows, last)
        peak = jnp.max(scores, axis=1, keepdims=True)
        grown = jnp.exp(scores - peak)
        total = jnp.sum(grown, axis=1, keepdims=True)
        lse[0, first:last, :] = peak + jnp.log(total)
        probs = (grown * (1.0 / total)).astype(BF)
        attn[pl.ds(place(piece), rows), :] = dot_plain(probs, v_out[:last, :]).astype(BF)


def backward_kernel(n, rows, me_ref, *refs):
    q_in, k_in, g_in = refs[:n], refs[n : 2 * n], refs[2 * n : 3 * n]
    (rate_q, rate_k, gain_q, gain_k, cosine, sine, q_rot, k_rot, value, lse) = refs[
        3 * n : 3 * n + 10
    ]
    t_q, t_k, d_v, sums, gains = refs[3 * n + 10 : 3 * n + 15]
    grads, acc_q, acc_k, acc_v = refs[3 * n + 15 :]
    me = me_ref[0]
    scale = HD ** (-0.5)

    def place(s):
        return pl.multiple_of(lax.rem(me - s + n, n) * rows, rows)

    for s in range(n):
        grads[pl.ds(place(s), rows), :] = g_in[s][...]
    acc_k[...] = jnp.zeros_like(acc_k)
    acc_v[...] = jnp.zeros_like(acc_v)
    for piece in range(n):
        first, last = piece * rows, (piece + 1) * rows
        queries, keys = q_rot[first:last, :], k_rot[:last, :]
        grad = grads[first:last, :]
        scores = masked_scores(queries, keys, rows, last)
        probs = jnp.exp(scores - lse[0, first:last, :])
        d_probs = dot_right_t(grad, value[:last, :])
        delta = jnp.sum(probs * d_probs, axis=1, keepdims=True)
        d_scores = (probs * (d_probs - delta) * scale).astype(BF)
        acc_v[:last, :] += dot_left_t(probs.astype(BF), grad)
        acc_q[first:last, :] = dot_plain(d_scores, keys)
        acc_k[:last, :] += dot_left_t(d_scores, queries)
    ones = jnp.ones((8, HD), F32)
    head = pl.program_id(0)
    for which, (acc, src, rate, gain, out) in enumerate(
        ((acc_q, q_in, rate_q, gain_q, t_q), (acc_k, k_in, rate_k, gain_k, t_k))
    ):
        column = jnp.zeros((1, HD), F32)
        for s in range(n):
            at = pl.ds(place(s), rows)
            grad = acc[at, :]
            normed = grad * cosine[at, :] - pltpu.roll(grad, HD // 2, 1) * sine[at, :]
            hat = src[s][...] * rate[at, :]
            column = column + jnp.sum(normed * hat, axis=0, keepdims=True)
            scaled = normed * gain[0]
            out[s * rows : (s + 1) * rows, :] = scaled
            line = lax.dot_general(
                ones,
                scaled * hat,
                (((1,), (1,)), ((), ())),
                precision=lax.Precision.HIGHEST,
                preferred_element_type=F32,
            )
            here = (which, slice(None), slice(s * rows, (s + 1) * rows))

            @pl.when(head == 0)
            def _():
                sums[here] = line

            @pl.when(head > 0)
            def _():
                sums[here] += line

        gains[0, which : which + 1, :] = column
    for s in range(n):
        d_v[s * rows : (s + 1) * rows, :] = acc_v[pl.ds(place(s), rows), :].astype(BF)


def attention_forward(me, pieces, rate_q, rate_k, gain_q, gain_k, cosine, sine):
    n, rows = len(pieces), pieces[0].shape[0]
    heads = gain_q.shape[0]

    def part(offset):
        return [pl.BlockSpec((rows, HD), lambda h, m, o=offset: (0, o * heads + h))] * n

    whole = pl.BlockSpec((L, HD), lambda h, m: (0, 0))
    gain = pl.BlockSpec((1, 1, HD), lambda h, m: (h, 0, 0))
    column = pl.BlockSpec((L, HD), lambda h, m: (0, h))
    low = jax.ShapeDtypeStruct((L, heads * HD), BF)
    return pl.pallas_call(
        functools.partial(forward_kernel, n, rows),
        grid_spec=pltpu.PrefetchScalarGridSpec(
            num_scalar_prefetch=1,
            grid=(heads,),
            in_specs=part(0) + part(1) + part(2) + [whole, whole, gain, gain, whole, whole],
            out_specs=[column] * 4 + [pl.BlockSpec((1, L, 1), lambda h, m: (h, 0, 0))],
        ),
        out_shape=[low] * 4 + [jax.ShapeDtypeStruct((heads, L, 1), F32)],
        compiler_params=pltpu.CompilerParams(vmem_limit_bytes=48 << 20),
        cost_estimate=pl.CostEstimate(
            flops=2 * heads * L * L * HD,
            bytes_accessed=12 * heads * L * HD + 10 * heads * L * HD,
            transcendentals=heads * L * L // 2,
        ),
        name="attention_forward",
    )(
        me,
        *pieces,
        *pieces,
        *pieces,
        rate_q,
        rate_k,
        gain_q[:, None, :],
        gain_k[:, None, :],
        cosine,
        sine,
    )


def attention_backward(
    me, pieces, grads, rate_q, rate_k, gain_q, gain_k, cosine, sine, q_rot, k_rot, value, lse
):
    n, rows = len(pieces), pieces[0].shape[0]
    heads = gain_q.shape[0]

    def part(offset):
        return [pl.BlockSpec((rows, HD), lambda h, m, o=offset: (0, o * heads + h))] * n

    whole = pl.BlockSpec((L, HD), lambda h, m: (0, 0))
    gain = pl.BlockSpec((1, 1, HD), lambda h, m: (h, 0, 0))
    column = pl.BlockSpec((L, HD), lambda h, m: (0, h))
    wide = jax.ShapeDtypeStruct((L, heads * HD), F32)
    return pl.pallas_call(
        functools.partial(backward_kernel, n, rows),
        grid_spec=pltpu.PrefetchScalarGridSpec(
            num_scalar_prefetch=1,
            grid=(heads,),
            in_specs=part(0)
            + part(1)
            + part(0)
            + [whole, whole, gain, gain, whole, whole]
            + [column] * 3
            + [pl.BlockSpec((1, L, 1), lambda h, m: (h, 0, 0))],
            out_specs=[column] * 3
            + [
                pl.BlockSpec((2, 8, L), lambda h, m: (0, 0, 0)),
                pl.BlockSpec((1, 2, HD), lambda h, m: (h, 0, 0)),
            ],
            scratch_shapes=[
                pltpu.VMEM((L, HD), BF),
                pltpu.VMEM((L, HD), F32),
                pltpu.VMEM((L, HD), F32),
                pltpu.VMEM((L, HD), F32),
            ],
        ),
        out_shape=[
            wide,
            wide,
            jax.ShapeDtypeStruct((L, heads * HD), BF),
            jax.ShapeDtypeStruct((2, 8, L), F32),
            jax.ShapeDtypeStruct((heads, 2, HD), F32),
        ],
        compiler_params=pltpu.CompilerParams(vmem_limit_bytes=48 << 20),
        cost_estimate=pl.CostEstimate(
            flops=5 * heads * L * L * HD,
            bytes_accessed=26 * heads * L * HD,
            transcendentals=heads * L * L // 2,
        ),
        name="attention_backward",
    )(
        me,
        *pieces,
        *pieces,
        *grads,
        rate_q,
        rate_k,
        gain_q[:, None, :],
        gain_k[:, None, :],
        cosine,
        sine,
        q_rot,
        k_rot,
        value,
        lse,
    )


def local(
    n,
    groups,
    inputs,
    w_query,
    w_key,
    w_value,
    q_gain,
    k_gain,
    w_out,
    attn_gain,
    w_gate,
    w_up,
    w_down,
    mlp_gain,
    cotangent,
):
    rows, width = inputs.shape
    heads, slice_q = q_gain.shape
    head_cols = heads * HD
    units = w_gate.shape[1]
    me = lax.axis_index("mp").astype(jnp.int32)
    me_ref = me.reshape(1)
    ring = [(i, (i + 1) % n) for i in range(n)]

    def shift(value):
        return lax.ppermute(value, "mp", ring)

    def reorder(stacked):
        turned = stacked[::-1]
        return lax.dynamic_slice_in_dim(
            jnp.concatenate([turned, turned], axis=0), n - 1 - me, n, axis=0
        )

    def gather_ring(own, first=1, last=n - 1, after={}):
        held = [own]
        for s in range(first, last + 1):
            sent = held[-1]
            if s in after:
                sent = lax.optimization_barrier((sent, after[s]))[0]
            held.append(shift(sent))
        return held

    def scatter_ring(partial_of, after={}):
        running = None
        for s in range(1, n):
            term = partial_of(s)
            if running is not None:
                term = term + running.astype(F32)
            term = term.astype(BF)
            if s in after:
                term = lax.optimization_barrier((term, after[s]))[0]
            running = shift(term)
        return partial_of(0) + running.astype(F32)

    w_attn = lax.all_gather(
        row_major(jnp.concatenate([w_query, w_key, w_value, row_major(w_out.T)], axis=1)),
        "dp",
        axis=0,
        tiled=True,
    )
    w_qkv = w_attn[:, : 3 * head_cols]
    out_t = w_attn[:, 3 * head_cols :]
    small = jnp.concatenate(
        [q_gain.reshape(-1), k_gain.reshape(-1), attn_gain, mlp_gain], axis=0
    )
    small = lax.all_gather(small, "dp", axis=0, tiled=False).astype(F32)
    count = heads * slice_q
    gain_q = small[:, :count].reshape(groups, heads, slice_q).transpose(1, 0, 2).reshape(heads, HD)
    gain_k = (
        small[:, count : 2 * count]
        .reshape(groups, heads, slice_q)
        .transpose(1, 0, 2)
        .reshape(heads, HD)
    )
    own_cols = attn_gain.shape[0]
    gain_a = small[:, 2 * count : 2 * count + own_cols].reshape(width)
    gain_m = small[:, 2 * count + own_cols :].reshape(width)
    full_gate = lax.all_gather(w_gate, "dp", axis=0, tiled=True)
    full_up = lax.all_gather(w_up, "dp", axis=0, tiled=True)
    full_down = lax.all_gather(w_down, "dp", axis=1, tiled=True)
    cosine, sine = rope_tables()

    held_x = gather_ring(inputs, 1, n - 2)
    pieces = [dot_plain(x, w_qkv) for x in held_x]
    last, pieces[0] = lax.optimization_barrier((held_x[-1], pieces[0]))
    held_x.append(gather_ring(last, n - 1)[1])
    pieces.append(dot_plain(held_x[-1], w_qkv))
    squares = jnp.stack(
        [
            jnp.stack(
                [
                    jnp.sum(jnp.square(p[:, :head_cols]), axis=1),
                    jnp.sum(jnp.square(p[:, head_cols : 2 * head_cols]), axis=1),
                ]
            )
            for p in pieces
        ]
    )
    squares = lax.psum(reorder(squares), "mp")
    rates = lax.rsqrt(squares / width + epsilon)
    rate_q = jnp.broadcast_to(rates[:, 0].reshape(L, 1), (L, HD))
    rate_k = jnp.broadcast_to(rates[:, 1].reshape(L, 1), (L, HD))
    attn, q_rot, k_rot, value, lse = attention_forward(
        me_ref, pieces, rate_q, rate_k, gain_q, gain_k, cosine, sine
    )
    attn_proj = scatter_ring(lambda s: dot_right_t(attn[s * rows : (s + 1) * rows], out_t))
    rate_a = lax.rsqrt(jnp.mean(attn_proj * attn_proj, axis=1, keepdims=True) + epsilon)
    hat_a = attn_proj * rate_a
    resid = inputs.astype(F32) + hat_a * gain_a
    resid_low = resid.astype(BF)

    held_r = gather_ring(resid_low)
    gates, ups, hiddens = [], [], []
    for r in held_r:
        gate = dot_plain(r, full_gate)
        up = dot_plain(r, full_up)
        gates.append(gate)
        ups.append(up)
        hiddens.append((gate * jax.nn.sigmoid(gate) * up).astype(BF))
    mlp_proj = scatter_ring(lambda s: dot_plain(hiddens[s], full_down))
    rate_m = lax.rsqrt(jnp.mean(mlp_proj * mlp_proj, axis=1, keepdims=True) + epsilon)
    hat_m = mlp_proj * rate_m
    output = resid + hat_m * gain_m

    upstream = cotangent.astype(F32)
    grad_gain_m = jnp.sum(upstream * hat_m, axis=0)
    scaled_m = upstream * gain_m
    d_mlp = (
        rate_m * (scaled_m - hat_m * jnp.mean(scaled_m * hat_m, axis=1, keepdims=True))
    ).astype(BF)
    held_m = gather_ring(d_mlp)
    d_gates, d_ups = [], []
    for s in range(n):
        gate, up = gates[s], ups[s]
        sigma = jax.nn.sigmoid(gate)
        d_hidden = dot_right_t(held_m[s], full_down)
        d_gates.append((d_hidden * up * sigma * (1.0 + gate * (1.0 - sigma))).astype(BF))
        d_ups.append((d_hidden * (gate * sigma)).astype(BF))
    down = dot_left_t(jnp.concatenate(hiddens, axis=0), jnp.concatenate(held_m, axis=0)).astype(BF)
    d_resid = upstream + scatter_ring(
        lambda s: dot_right_t(d_gates[s], full_gate) + dot_right_t(d_ups[s], full_up),
        {1: held_m[-1]},
    )
    grad_down = lax.psum_scatter(down, "dp", scatter_dimension=1, tiled=True)
    d_gate_up = jnp.concatenate(
        [jnp.concatenate(d_gates, axis=0), jnp.concatenate(d_ups, axis=0)], axis=1
    )
    all_r = jnp.concatenate(held_r, axis=0)
    gate_up = dot_left_t(all_r, d_gate_up).astype(BF)

    grad_gain_a = jnp.sum(d_resid * hat_a, axis=0)
    scaled_a = d_resid * gain_a
    d_attn_proj = (
        rate_a * (scaled_a - hat_a * jnp.mean(scaled_a * hat_a, axis=1, keepdims=True))
    ).astype(BF)
    held_a = gather_ring(d_attn_proj, after={n - 1: grad_down})
    grad_gate_up = lax.psum_scatter(gate_up, "dp", scatter_dimension=0, tiled=True)
    d_attn = [dot_plain(a, out_t).astype(BF) for a in held_a]
    t_q, t_k, d_value, sums, head_gains = attention_backward(
        me_ref,
        pieces,
        d_attn,
        rate_q,
        rate_k,
        gain_q,
        gain_k,
        cosine,
        sine,
        q_rot,
        k_rot,
        value,
        lse,
    )
    sums = reorder(sums[:, 0, :].reshape(2, n, rows).transpose(1, 0, 2))
    sums = lax.psum(sums, "mp")
    back = reorder(jnp.concatenate([rates, sums / width], axis=1))
    d_qkv = []
    for s in range(n):
        at = slice(s * rows, (s + 1) * rows)
        parts = []
        for which, t in enumerate((t_q, t_k)):
            rate = back[s, which][:, None]
            raw = pieces[s][:, which * head_cols : (which + 1) * head_cols]
            parts.append((rate * (t[at] - raw * (rate * back[s, 2 + which][:, None]))).astype(BF))
        parts.append(d_value[at])
        d_qkv.append(jnp.concatenate(parts, axis=1))
    all_x, all_d = jnp.concatenate(held_x, axis=0), jnp.concatenate(d_qkv, axis=0)
    dw_qkv = dot_left_t(all_x, all_d).astype(BF)
    all_a = jnp.concatenate(held_a, axis=0)
    dw_out = dot_left_t(all_a, attn).astype(BF)
    grad_attn = lax.psum_scatter(
        jnp.concatenate([dw_qkv, dw_out], axis=1), "dp", scatter_dimension=0, tiled=True
    )
    grad_query = grad_attn[:, :head_cols].astype(F32)
    grad_key = grad_attn[:, head_cols : 2 * head_cols].astype(F32)
    grad_value = grad_attn[:, 2 * head_cols : 3 * head_cols].astype(F32)
    grad_out = grad_attn[:, 3 * head_cols :].astype(F32).T
    input_grad = d_resid + scatter_ring(
        lambda s: dot_right_t(d_qkv[s], w_qkv), {n - 1: grad_gate_up}
    )

    grad_gate = grad_gate_up[:, :units].astype(F32)
    grad_up = grad_gate_up[:, units:].astype(F32)

    post = lax.psum(jnp.stack([grad_gain_a, grad_gain_m]), "mp")
    post = post.reshape(2, groups, own_cols).transpose(1, 0, 2).reshape(groups, 2 * own_cols)
    own = head_gains.transpose(1, 0, 2).reshape(2, heads, groups, slice_q)
    own = own.transpose(2, 0, 1, 3).reshape(groups, 2 * count)
    totals = lax.psum(jnp.concatenate([own, post], axis=1), "dp")
    mine = lax.dynamic_index_in_dim(totals, lax.axis_index("dp"), 0, keepdims=False)
    return (
        output,
        input_grad,
        grad_query,
        grad_key,
        grad_value,
        mine[:count].reshape(heads, slice_q),
        mine[count : 2 * count].reshape(heads, slice_q),
        grad_out,
        mine[2 * count : 2 * count + own_cols],
        grad_gate,
        grad_up,
        grad_down.astype(F32),
        mine[2 * count + own_cols :],
    )


def solution(mesh):
    in_specs = (
        P(("dp", "mp"), None),
        P("dp", "mp"),
        P("dp", "mp"),
        P("dp", "mp"),
        P("mp", "dp"),
        P("mp", "dp"),
        P("mp", "dp"),
        P("dp"),
        P("dp", "mp"),
        P("dp", "mp"),
        P("mp", "dp"),
        P("dp"),
        P(("dp", "mp"), None),
    )
    out_specs = (
        P(("dp", "mp"), None),
        P(("dp", "mp"), None),
        P("dp", "mp"),
        P("dp", "mp"),
        P("dp", "mp"),
        P("mp", "dp"),
        P("mp", "dp"),
        P("mp", "dp"),
        P("dp"),
        P("dp", "mp"),
        P("dp", "mp"),
        P("mp", "dp"),
        P("dp"),
    )

    def body(*args):
        return local(mesh.shape["mp"], mesh.shape["dp"], *args)

    return jax.shard_map(body, mesh=mesh, in_specs=in_specs, out_specs=out_specs, check_vma=False)
```

profile of v0, /device:TPU:0, one launch (start us, length us, event | category | flops | bytes accessed | tf_op | source)
XLA Modules:
  0.0 829.3 jit_solution(12338609347430726596)
XLA Ops:
  15.8 25.3 %collective-permute-done = bf16[256,2048]{1,0:T(8,128)(2,1)} collective-permute-done((bf16[256,2048]{1,0:T(8,128)(2,1)S(1)}, bf16[256,2048]{1,0:T(8,128)(2,1)}, u32[]{:S(2)}, u32[]{:S(2)}) %collective-permute-start) | collective-permute-done | bytes 1048608 | tf_op jit(solution)/shard_map/ppermute | solution.py:287
  41.4 9.4 %all-gather.1 = bf16[8,1,640]{2,1,0:T(2,128)(2,1)S(1)} all-gather(bf16[1,1,640]{2,1,0:T(2,128)(2,1)S(1)} %reshape.219), channel_id=2, replica_groups=mesh['dp'=8,'mp'=4] {'dp'}, dimensions={0}, use_global_device_ids=true | all-gather | bytes 11520 | tf_op jit(solution)/shard_map/all_gather | solution.py:327
  53.5 14.0 %collective-permute-done.1 = bf16[256,2048]{1,0:T(8,128)(2,1)} collective-permute-done((bf16[256,2048]{1,0:T(8,128)(2,1)}, bf16[256,2048]{1,0:T(8,128)(2,1)}, u32[]{:S(2)}, u32[]{:S(2)}) %collective-permute-start.1) | collective-permute-done | bytes 1048608 | tf_op jit(solution)/shard_map/ppermute | solution.py:287
  80.3 22.2 %collective-permute-done.2 = bf16[256,2048]{1,0:T(8,128)(2,1)S(1)} collective-permute-done((bf16[256,2048]{1,0:T(8,128)(2,1)}, bf16[256,2048]{1,0:T(8,128)(2,1)S(1)}, u32[]{:S(2)}, u32[]{:S(2)}) %collective-permute-start.2) | collective-permute-done | bytes 1048608 | tf_op jit(solution)/shard_map/ppermute | solution.py:287
  105.7 10.6 %psum.28 = f32[4,2,256]{2,0,1:T(4,128)S(1)} all-reduce(f32[4,2,256]{2,0,1:T(4,128)S(1)} %fusion.143), channel_id=1, replica_groups=mesh['dp'=8,'mp'=4] {'mp'}, use_global_device_ids=true, to_apply=%region_8.0 | all-reduce | flops 2048 | bytes 16384 | tf_op jit(solution)/shard_map/psum | solution.py:360
  117.1 14.4 %attention_forward.1 = (bf16[1024,512]{1,0:T(8,128)(2,1)S(1)}, bf16[1024,512]{1,0:T(8,128)(2,1)S(1)}, bf16[1024,512]{1,0:T(8,128)(2,1)S(1)}, bf16[1024,512]{1,0:T(8,128)(2,1)}, f32[4,1024,1]{2,1,0:T(8,128)}) custom-call(s32[1]{0:T(128)} %bitcast.me_ref, f32[256,1536]{1,0:T(8,128)} %copy-done.13, f32[256,1536]{1,0:T(8,128)} %copy-done.14, ...), custom_call_target="tpu_custom_call" | custom-call | flops 1073741824 | bytes 11534336 | tf_op jit(solution)/shard_map/attention_forward/pallas_call | solution.py:163
  132.9 23.7 %collective-permute-done.3 = bf16[256,2048]{1,0:T(8,128)(2,1)S(1)} collective-permute-done((bf16[256,2048]{1,0:T(8,128)(2,1)S(1)}, bf16[256,2048]{1,0:T(8,128)(2,1)S(1)}, u32[]{:S(2)}, u32[]{:S(2)}) %collective-permute-start.3) | collective-permute-done | bytes 1048608 | tf_op jit(solution)/shard_map/ppermute | solution.py:287
  158.2 22.6 %collective-permute-done.4 = bf16[256,2048]{1,0:T(8,128)(2,1)S(1)} collective-permute-done((bf16[256,2048]{1,0:T(8,128)(2,1)S(1)}, bf16[256,2048]{1,0:T(8,128)(2,1)S(1)}, u32[]{:S(2)}, u32[]{:S(2)}) %collective-permute-start.4) | collective-permute-done | bytes 1048608 | tf_op jit(solution)/shard_map/ppermute | solution.py:287
  182.0 21.7 %collective-permute-done.5 = bf16[256,2048]{1,0:T(8,128)(2,1)S(1)} collective-permute-done((bf16[256,2048]{1,0:T(8,128)(2,1)S(1)}, bf16[256,2048]{1,0:T(8,128)(2,1)S(1)}, u32[]{:S(2)}, u32[]{:S(2)}) %collective-permute-start.5) | collective-permute-done | bytes 1048608 | tf_op jit(solution)/shard_map/ppermute | solution.py:287
  206.4 22.2 %collective-permute-done.6 = bf16[256,2048]{1,0:T(8,128)(2,1)S(1)} collective-permute-done((bf16[256,2048]{1,0:T(8,128)(2,1)S(1)}, bf16[256,2048]{1,0:T(8,128)(2,1)S(1)}, u32[]{:S(2)}, u32[]{:S(2)}) %collective-permute-start.6) | collective-permute-done | bytes 1048608 | tf_op jit(solution)/shard_map/ppermute | solution.py:287
  261.5 16.7 %collective-permute-done.9 = bf16[256,2048]{1,0:T(8,128)(2,1)S(1)} collective-permute-done((bf16[256,2048]{1,0:T(8,128)(2,1)S(1)}, bf16[256,2048]{1,0:T(8,128)(2,1)S(1)}, u32[]{:S(2)}, u32[]{:S(2)}) %collective-permute-start.9) | collective-permute-done | bytes 1048608 | tf_op jit(solution)/shard_map/ppermute | solution.py:287
  281.1 19.6 %collective-permute-done.8 = bf16[256,2048]{1,0:T(8,128)(2,1)S(1)} collective-permute-done((bf16[256,2048]{1,0:T(8,128)(2,1)}, bf16[256,2048]{1,0:T(8,128)(2,1)S(1)}, u32[]{:S(2)}, u32[]{:S(2)}) %collective-permute-start.8) | collective-permute-done | bytes 1048608 | tf_op jit(solution)/shard_map/ppermute | solution.py:287
  325.2 14.2 %collective-permute-done.11 = bf16[256,2048]{1,0:T(8,128)(2,1)S(1)} collective-permute-done((bf16[256,2048]{1,0:T(8,128)(2,1)S(1)}, bf16[256,2048]{1,0:T(8,128)(2,1)S(1)}, u32[]{:S(2)}, u32[]{:S(2)}) %collective-permute-start.11) | collective-permute-done | bytes 1048608 | tf_op jit(solution)/shard_map/ppermute | solution.py:287
  346.3 23.3 %collective-permute-done.12 = bf16[256,2048]{1,0:T(8,128)(2,1)S(1)} collective-permute-done((bf16[256,2048]{1,0:T(8,128)(2,1)S(1)}, bf16[256,2048]{1,0:T(8,128)(2,1)S(1)}, u32[]{:S(2)}, u32[]{:S(2)}) %collective-permute-start.12) | collective-permute-done | bytes 1048608 | tf_op jit(solution)/shard_map/ppermute | solution.py:287
  369.6 23.3 %collective-permute-done.13 = bf16[256,2048]{1,0:T(8,128)(2,1)S(1)} collective-permute-done((bf16[256,2048]{1,0:T(8,128)(2,1)S(1)}, bf16[256,2048]{1,0:T(8,128)(2,1)S(1)}, u32[]{:S(2)}, u32[]{:S(2)}) %collective-permute-start.13) | collective-permute-done | bytes 1048608 | tf_op jit(solution)/shard_map/ppermute | solution.py:287
  393.0 18.2 %collective-permute-done.14 = bf16[256,2048]{1,0:T(8,128)(2,1)S(1)} collective-permute-done((bf16[256,2048]{1,0:T(8,128)(2,1)S(1)}, bf16[256,2048]{1,0:T(8,128)(2,1)S(1)}, u32[]{:S(2)}, u32[]{:S(2)}) %collective-permute-start.14) | collective-permute-done | bytes 1048608 | tf_op jit(solution)/shard_map/ppermute | solution.py:287
  412.1 11.3 %convolution_convert_fusion.2 = bf16[2048,2048]{1,0:T(8,128)(2,1)} fusion(bf16[256,2048]{1,0:T(8,128)(2,1)S(1)} %get-tuple-element.158, bf16[256,2048]{1,0:T(8,128)(2,1)S(1)} %get-tuple-element.160, bf16[256,2048]{1,0:T(8,128)(2,1)S(1)} %copy-done.76, bf16[256,2048]{1,0:T(8,128)(2,1)S(1)} %get-tuple-element.156, ...), kind=kOutput, calls=%fused_computation.18 | convolution fusion | flops 8627683328 | bytes 16777216 | tf_op jit(solution)/shard_map/dot_general | solution.py:31
  423.8 10.3 %multiply_convert_fusion.7 = (bf16[256,2048]{1,0:T(8,128)(2,1)}, bf16[256,2048]{1,0:T(8,128)(2,1)}) fusion(f32[256,2048]{1,0:T(8,128)} %copy-done.72, f32[256,2048]{1,0:T(8,128)} %get-tuple-element.157, bf16[256,2048]{1,0:T(8,128)(2,1)} %copy-done.32, bf16[2048,2048]{1,0:T(8,128)(2,1)} %all-gather.13.cloned.1.call-done), kind=kOutput, calls=%fused_computation.113 | convolution fusion | flops 2154299392 | bytes 15728640 | tf_op jit(solution)/shard_map/dot_general | solution.py:27
  434.1 8.8 %multiply_convert_fusion.1 = (bf16[256,2048]{1,0:T(8,128)(2,1)}, bf16[256,2048]{1,0:T(8,128)(2,1)}) fusion(f32[256,2048]{1,0:T(8,128)S(1)} %copy-done.67, f32[256,2048]{1,0:T(8,128)S(1)} %copy-done.73, bf16[256,2048]{1,0:T(8,128)(2,1)S(1)} %copy-done.55, bf16[2048,2048]{1,0:T(8,128)(2,1)} %all-gather.13.cloned.1.call-done), kind=kOutput, calls=%fused_computation.107 | convolution fusion | flops 2154299392 | bytes 15728640 | tf_op jit(solution)/shard_map/dot_general | solution.py:27
  451.7 26.3 %convolution_convert_fusion = bf16[2048,4096]{1,0:T(8,128)(2,1)} fusion(bf16[256,2048]{1,0:T(8,128)(2,1)} %get-tuple-element.105, bf16[256,2048]{1,0:T(8,128)(2,1)} %get-tuple-element.103, bf16[256,2048]{1,0:T(8,128)(2,1)} %get-tuple-element.101, bf16[256,2048]{1,0:T(8,128)(2,1)} %get-tuple-element.107, bf16[256,2048]{1,0:T(8,128)(2,1)} %get-tuple-element.106, ...), kind=kOutput, calls=%fused_computation | convolution fusion | flops 17272143872 | bytes 29360128 | tf_op jit(solution)/shard_map/dot_general | solution.py:31
  499.0 16.4 %collective-permute-done.15 = bf16[256,2048]{1,0:T(8,128)(2,1)S(1)} collective-permute-done((bf16[256,2048]{1,0:T(8,128)(2,1)S(1)}, bf16[256,2048]{1,0:T(8,128)(2,1)S(1)}, u32[]{:S(2)}, u32[]{:S(2)}) %collective-permute-start.15) | collective-permute-done | bytes 1048608 | tf_op jit(solution)/shard_map/ppermute | solution.py:287
  525.3 16.0 %collective-permute-done.16 = bf16[256,2048]{1,0:T(8,128)(2,1)S(1)} collective-permute-done((bf16[256,2048]{1,0:T(8,128)(2,1)S(1)}, bf16[256,2048]{1,0:T(8,128)(2,1)S(1)}, u32[]{:S(2)}, u32[]{:S(2)}) %collective-permute-start.16) | collective-permute-done | bytes 1048608 | tf_op jit(solution)/shard_map/ppermute | solution.py:287
  550.4 16.6 %collective-permute-done.17 = bf16[256,2048]{1,0:T(8,128)(2,1)S(1)} collective-permute-done((bf16[256,2048]{1,0:T(8,128)(2,1)S(1)}, bf16[256,2048]{1,0:T(8,128)(2,1)S(1)}, u32[]{:S(2)}, u32[]{:S(2)}) %collective-permute-start.17) | collective-permute-done | bytes 1048608 | tf_op jit(solution)/shard_map/ppermute | solution.py:287
  569.1 27.4 %collective-permute-done.18 = bf16[256,2048]{1,0:T(8,128)(2,1)S(1)} collective-permute-done((bf16[256,2048]{1,0:T(8,128)(2,1)S(1)}, bf16[256,2048]{1,0:T(8,128)(2,1)S(1)}, u32[]{:S(2)}, u32[]{:S(2)}) %collective-permute-start.18) | collective-permute-done | bytes 1048608 | tf_op jit(solution)/shard_map/ppermute | solution.py:287
  597.5 26.5 %collective-permute-done.19 = bf16[256,2048]{1,0:T(8,128)(2,1)} collective-permute-done((bf16[256,2048]{1,0:T(8,128)(2,1)S(1)}, bf16[256,2048]{1,0:T(8,128)(2,1)}, u32[]{:S(2)}, u32[]{:S(2)}) %collective-permute-start.19) | collective-permute-done | bytes 1048608 | tf_op jit(solution)/shard_map/ppermute | solution.py:287
  631.5 9.4 %collective-permute-done.20 = bf16[256,2048]{1,0:T(8,128)(2,1)S(1)} collective-permute-done((bf16[256,2048]{1,0:T(8,128)(2,1)}, bf16[256,2048]{1,0:T(8,128)(2,1)S(1)}, u32[]{:S(2)}, u32[]{:S(2)}) %collective-permute-start.20) | collective-permute-done | bytes 1048608 | tf_op jit(solution)/shard_map/ppermute | solution.py:287
  643.6 26.7 %attention_backward.1 = (f32[1024,512]{1,0:T(8,128)}, f32[1024,512]{1,0:T(8,128)}, bf16[1024,512]{1,0:T(8,128)(2,1)S(1)}, f32[2,8,1024]{2,1,0:T(8,128)S(1)}, f32[4,2,128]{2,1,0:T(2,128)S(1)}) custom-call(s32[1]{0:T(128)} %bitcast.me_ref, f32[256,1536]{1,0:T(8,128)} %copy-done.13, f32[256,1536]{1,0:T(8,128)} %copy-done.14, f32[256,1536]{1,0:T(8,128)} %copy-done.11, ...), custom_call_target="tpu_custom_call" | custom-call | flops 2684354560 | bytes 13631488 | tf_op jit(solution)/shard_map/attention_backward/pallas_call | solution.py:206
  670.5 15.9 %all-reduce = (f32[4,2,256]{2,0,1:T(4,128)S(1)}, f32[8,512]{1,0:T(8,128)S(1)}) all-reduce(f32[4,2,256]{2,0,1:T(4,128)S(1)} %fusion.142, f32[8,512]{1,0:T(8,128)S(1)} %bitcast.141), channel_id=1, replica_groups=mesh['dp'=8,'mp'=4] {'mp'}, use_global_device_ids=true, to_apply=%region_14.0 | all-reduce | flops 6144 | bytes 49152 | tf_op jit(solution)/shard_map/psum | solution.py:436
  698.6 11.5 %convolution_convert_fusion.1 = bf16[2048,1536]{0,1:T(8,128)(2,1)} fusion(bf16[256,2048]{1,0:T(8,128)(2,1)} %copy-done.44, bf16[256,2048]{1,0:T(8,128)(2,1)} %collective-permute-done.1, bf16[256,2048]{1,0:T(8,128)(2,1)} %collective-permute-done, bf16[256,2048]{1,0:T(8,128)(2,1)S(1)} %copy-done.24, bf16[256,512]{1,0:T(8,128)(2,1)} %get-tuple-element.128, ...), kind=kOutput, calls=%fused_computation.17 | convolution fusion | flops 6500122624 | bytes 13631488 | tf_op jit(solution)/shard_map/dot_general | solution.py:31
  724.3 26.5 %collective-permute-done.21 = bf16[256,2048]{1,0:T(8,128)(2,1)S(1)} collective-permute-done((bf16[256,2048]{1,0:T(8,128)(2,1)S(1)}, bf16[256,2048]{1,0:T(8,128)(2,1)S(1)}, u32[]{:S(2)}, u32[]{:S(2)}) %collective-permute-start.21) | collective-permute-done | bytes 1048608 | tf_op jit(solution)/shard_map/ppermute | solution.py:287
  763.2 14.9 %collective-permute-done.22 = bf16[256,2048]{1,0:T(8,128)(2,1)S(1)} collective-permute-done((bf16[256,2048]{1,0:T(8,128)(2,1)}, bf16[256,2048]{1,0:T(8,128)(2,1)S(1)}, u32[]{:S(2)}, u32[]{:S(2)}) %collective-permute-start.22) | collective-permute-done | bytes 1048608 | tf_op jit(solution)/shard_map/ppermute | solution.py:287
  779.4 23.6 %psum.31 = f32[8,640]{1,0:T(8,128)S(1)} all-reduce(f32[8,640]{1,0:T(8,128)S(1)} %pad_maximum_fusion.4), channel_id=1, replica_groups=mesh['dp'=8,'mp'=4] {'dp'}, use_global_device_ids=true, to_apply=%region_20.0 | all-reduce | flops 5120 | bytes 40960 | tf_op jit(solution)/shard_map/psum | solution.py:470
  (360 shorter events, 223.5 us)
Async XLA Ops:
  7.2 60.6 %all-gather.7.cloned.1.call-start = ((), (), s32[]{:S(2)}) async-start(), calls=%async_computation.3 | async-start | bytes 9437184 | tf_op jit(solution)/shard_map/all_gather | solution.py:316
  10.6 218.2 %all-gather.9.cloned.1.call-start = ((), (), s32[]{:S(2)}) async-start(), calls=%async_computation.4 | async-start | bytes 9437184 | tf_op jit(solution)/shard_map/all_gather | solution.py:339
  11.3 224.6 %all-gather.11.cloned.1.call-start = ((), (), s32[]{:S(2)}) async-start(), calls=%async_computation.5 | async-start | bytes 9437184 | tf_op jit(solution)/shard_map/all_gather | solution.py:340
  12.1 232.1 %all-gather.13.cloned.1.call-start = ((), (), s32[]{:S(2)}) async-start(), calls=%async_computation.6 | async-start | bytes 9437184 | tf_op jit(solution)/shard_map/all_gather | solution.py:341
  12.6 611.4 %reduce-scatter.4.cloned.1.call-start = ((), (), s32[]{:S(2)}) async-start(), calls=%async_computation.7 | async-start | bytes 9437184 | tf_op jit(solution)/shard_map/reduce_scatter | solution.py:405
  12.7 28.4 %collective-permute-start = (bf16[256,2048]{1,0:T(8,128)(2,1)S(1)}, bf16[256,2048]{1,0:T(8,128)(2,1)}, u32[]{:S(2)}, u32[]{:S(2)}) collective-permute-start(bf16[256,2048]{1,0:T(8,128)(2,1)S(1)} %copy-done.22), channel_id=1, source_target_pairs={{0,1},{1,2},{2,3},{3,0},{4,5},{5,6},{6,7},{7,4},{8,9},{9,10},{10,1... | collective-permute-start | bytes 3145736 | tf_op jit(solution)/shard_map/ppermute | solution.py:287
  41.1 26.4 %collective-permute-start.1 = (bf16[256,2048]{1,0:T(8,128)(2,1)}, bf16[256,2048]{1,0:T(8,128)(2,1)}, u32[]{:S(2)}, u32[]{:S(2)}) collective-permute-start(bf16[256,2048]{1,0:T(8,128)(2,1)} %collective-permute-done), channel_id=1, source_target_pairs={{0,1},{1,2},{2,3},{3,0},{4,5},{5,6},{6,7},{7,4},{8,9},{9,10},{10,1... | collective-permute-start | bytes 3145736 | tf_op jit(solution)/shard_map/ppermute | solution.py:287
  75.1 27.4 %collective-permute-start.2 = (bf16[256,2048]{1,0:T(8,128)(2,1)}, bf16[256,2048]{1,0:T(8,128)(2,1)S(1)}, u32[]{:S(2)}, u32[]{:S(2)}) collective-permute-start(bf16[256,2048]{1,0:T(8,128)(2,1)} %collective-permute-done.1), channel_id=1, source_target_pairs={{0,1},{1,2},{2,3},{3,0},{4,5},{5,6},{6,7},{7,4},{8,9},{9,10},{10,1... | collective-permute-start | bytes 3145736 | tf_op jit(solution)/shard_map/ppermute | solution.py:287
  132.3 24.3 %collective-permute-start.3 = (bf16[256,2048]{1,0:T(8,128)(2,1)S(1)}, bf16[256,2048]{1,0:T(8,128)(2,1)S(1)}, u32[]{:S(2)}, u32[]{:S(2)}) collective-permute-start(bf16[256,2048]{1,0:T(8,128)(2,1)S(1)} %convolution_convert_fusion.3), channel_id=1, source_target_pairs={{0,1},{1,2},{2,3},{3,0},{4,5},{5,6},{6,7},{7,4},{8,9},{9,10},{10,1... | collective-permute-start | bytes 3145736 | tf_op jit(solution)/shard_map/ppermute | solution.py:287
  157.4 23.4 %collective-permute-start.4 = (bf16[256,2048]{1,0:T(8,128)(2,1)S(1)}, bf16[256,2048]{1,0:T(8,128)(2,1)S(1)}, u32[]{:S(2)}, u32[]{:S(2)}) collective-permute-start(bf16[256,2048]{1,0:T(8,128)(2,1)S(1)} %add_convert_fusion.7), channel_id=1, source_target_pairs={{0,1},{1,2},{2,3},{3,0},{4,5},{5,6},{6,7},{7,4},{8,9},{9,10},{10,1... | collective-permute-start | bytes 3145736 | tf_op jit(solution)/shard_map/ppermute | solution.py:287
  181.1 22.6 %collective-permute-start.5 = (bf16[256,2048]{1,0:T(8,128)(2,1)S(1)}, bf16[256,2048]{1,0:T(8,128)(2,1)S(1)}, u32[]{:S(2)}, u32[]{:S(2)}) collective-permute-start(bf16[256,2048]{1,0:T(8,128)(2,1)S(1)} %add_convert_fusion.6), channel_id=1, source_target_pairs={{0,1},{1,2},{2,3},{3,0},{4,5},{5,6},{6,7},{7,4},{8,9},{9,10},{10,1... | collective-permute-start | bytes 3145736 | tf_op jit(solution)/shard_map/ppermute | solution.py:287
  205.4 23.2 %collective-permute-start.6 = (bf16[256,2048]{1,0:T(8,128)(2,1)S(1)}, bf16[256,2048]{1,0:T(8,128)(2,1)S(1)}, u32[]{:S(2)}, u32[]{:S(2)}) collective-permute-start(bf16[256,2048]{1,0:T(8,128)(2,1)S(1)} %fusion.88), channel_id=1, source_target_pairs={{0,1},{1,2},{2,3},{3,0},{4,5},{5,6},{6,7},{7,4},{8,9},{9,10},{10,1... | collective-permute-start | bytes 3145736 | tf_op jit(solution)/shard_map/ppermute | solution.py:287
  228.6 21.9 %collective-permute-start.7 = (bf16[256,2048]{1,0:T(8,128)(2,1)S(1)}, bf16[256,2048]{1,0:T(8,128)(2,1)}, u32[]{:S(2)}, u32[]{:S(2)}) collective-permute-start(bf16[256,2048]{1,0:T(8,128)(2,1)S(1)} %collective-permute-done.6), channel_id=1, source_target_pairs={{0,1},{1,2},{2,3},{3,0},{4,5},{5,6},{6,7},{7,4},{8,9},{9,10},{10,1... | collective-permute-start | bytes 3145736 | tf_op jit(solution)/shard_map/ppermute | solution.py:287
  250.3 27.9 %collective-permute-start.9 = (bf16[256,2048]{1,0:T(8,128)(2,1)S(1)}, bf16[256,2048]{1,0:T(8,128)(2,1)S(1)}, u32[]{:S(2)}, u32[]{:S(2)}) collective-permute-start(bf16[256,2048]{1,0:T(8,128)(2,1)S(1)} %convolution_convert_fusion.5), channel_id=1, source_target_pairs={{0,1},{1,2},{2,3},{3,0},{4,5},{5,6},{6,7},{7,4},{8,9},{9,10},{10,1... | collective-permute-start | bytes 3145736 | tf_op jit(solution)/shard_map/ppermute | solution.py:287
  250.5 50.2 %collective-permute-start.8 = (bf16[256,2048]{1,0:T(8,128)(2,1)}, bf16[256,2048]{1,0:T(8,128)(2,1)S(1)}, u32[]{:S(2)}, u32[]{:S(2)}) collective-permute-start(bf16[256,2048]{1,0:T(8,128)(2,1)} %collective-permute-done.7), channel_id=1, source_target_pairs={{0,1},{1,2},{2,3},{3,0},{4,5},{5,6},{6,7},{7,4},{8,9},{9,10},{10,1... | collective-permute-start | bytes 3145736 | tf_op jit(solution)/shard_map/ppermute | solution.py:287
  280.6 37.6 %collective-permute-start.10 = (bf16[256,2048]{1,0:T(8,128)(2,1)S(1)}, bf16[256,2048]{1,0:T(8,128)(2,1)S(1)}, u32[]{:S(2)}, u32[]{:S(2)}) collective-permute-start(bf16[256,2048]{1,0:T(8,128)(2,1)S(1)} %add_convert_fusion.5), channel_id=1, source_target_pairs={{0,1},{1,2},{2,3},{3,0},{4,5},{5,6},{6,7},{7,4},{8,9},{9,10},{10,1... | collective-permute-start | bytes 3145736 | tf_op jit(solution)/shard_map/ppermute | solution.py:287
  318.6 20.8 %collective-permute-start.11 = (bf16[256,2048]{1,0:T(8,128)(2,1)S(1)}, bf16[256,2048]{1,0:T(8,128)(2,1)S(1)}, u32[]{:S(2)}, u32[]{:S(2)}) collective-permute-start(bf16[256,2048]{1,0:T(8,128)(2,1)S(1)} %add_convert_fusion.4), channel_id=1, source_target_pairs={{0,1},{1,2},{2,3},{3,0},{4,5},{5,6},{6,7},{7,4},{8,9},{9,10},{10,1... | collective-permute-start | bytes 3145736 | tf_op jit(solution)/shard_map/ppermute | solution.py:287
  343.9 68.3 %copy-start.76 = (bf16[256,2048]{1,0:T(8,128)(2,1)S(1)}, bf16[256,2048]{1,0:T(8,128)(2,1)}, u32[]{:S(2)}) copy-start(bf16[256,2048]{1,0:T(8,128)(2,1)} %get-tuple-element.162) | copy-start | bytes 3145732
  346.3 23.3 %collective-permute-start.12 = (bf16[256,2048]{1,0:T(8,128)(2,1)S(1)}, bf16[256,2048]{1,0:T(8,128)(2,1)S(1)}, u32[]{:S(2)}, u32[]{:S(2)}) collective-permute-start(bf16[256,2048]{1,0:T(8,128)(2,1)S(1)} %get-tuple-element.109), channel_id=1, source_target_pairs={{0,1},{1,2},{2,3},{3,0},{4,5},{5,6},{6,7},{7,4},{8,9},{9,10},{10,1... | collective-permute-start | bytes 3145736 | tf_op jit(solution)/shard_map/ppermute | solution.py:287
  369.6 23.3 %collective-permute-start.13 = (bf16[256,2048]{1,0:T(8,128)(2,1)S(1)}, bf16[256,2048]{1,0:T(8,128)(2,1)S(1)}, u32[]{:S(2)}, u32[]{:S(2)}) collective-permute-start(bf16[256,2048]{1,0:T(8,128)(2,1)S(1)} %collective-permute-done.12), channel_id=1, source_target_pairs={{0,1},{1,2},{2,3},{3,0},{4,5},{5,6},{6,7},{7,4},{8,9},{9,10},{10,1... | collective-permute-start | bytes 3145736 | tf_op jit(solution)/shard_map/ppermute | solution.py:287
  393.0 18.2 %collective-permute-start.14 = (bf16[256,2048]{1,0:T(8,128)(2,1)S(1)}, bf16[256,2048]{1,0:T(8,128)(2,1)S(1)}, u32[]{:S(2)}, u32[]{:S(2)}) collective-permute-start(bf16[256,2048]{1,0:T(8,128)(2,1)S(1)} %collective-permute-done.13), channel_id=1, source_target_pairs={{0,1},{1,2},{2,3},{3,0},{4,5},{5,6},{6,7},{7,4},{8,9},{9,10},{10,1... | collective-permute-start | bytes 3145736 | tf_op jit(solution)/shard_map/ppermute | solution.py:287
  423.5 355.9 %reduce-scatter.6.cloned.1.call-start = ((), (), s32[]{:S(2)}) async-start(), calls=%async_computation.8 | async-start | bytes 18874368 | tf_op jit(solution)/shard_map/reduce_scatter | solution.py:418
  478.0 331.1 %reduce-scatter.8.cloned.1.call-start = ((), (), s32[]{:S(2)}) async-start(), calls=%async_computation.9 | async-start | bytes 9437184 | tf_op jit(solution)/shard_map/reduce_scatter | solution.py:452
  490.4 25.1 %collective-permute-start.15 = (bf16[256,2048]{1,0:T(8,128)(2,1)S(1)}, bf16[256,2048]{1,0:T(8,128)(2,1)S(1)}, u32[]{:S(2)}, u32[]{:S(2)}) collective-permute-start(bf16[256,2048]{1,0:T(8,128)(2,1)S(1)} %fusion.77), channel_id=1, source_target_pairs={{0,1},{1,2},{2,3},{3,0},{4,5},{5,6},{6,7},{7,4},{8,9},{9,10},{10,1... | collective-permute-start | bytes 3145736 | tf_op jit(solution)/shard_map/ppermute | solution.py:287
  515.7 25.6 %collective-permute-start.16 = (bf16[256,2048]{1,0:T(8,128)(2,1)S(1)}, bf16[256,2048]{1,0:T(8,128)(2,1)S(1)}, u32[]{:S(2)}, u32[]{:S(2)}) collective-permute-start(bf16[256,2048]{1,0:T(8,128)(2,1)S(1)} %add_convert_fusion.3), channel_id=1, source_target_pairs={{0,1},{1,2},{2,3},{3,0},{4,5},{5,6},{6,7},{7,4},{8,9},{9,10},{10,1... | collective-permute-start | bytes 3145736 | tf_op jit(solution)/shard_map/ppermute | solution.py:287
  541.7 25.3 %collective-permute-start.17 = (bf16[256,2048]{1,0:T(8,128)(2,1)S(1)}, bf16[256,2048]{1,0:T(8,128)(2,1)S(1)}, u32[]{:S(2)}, u32[]{:S(2)}) collective-permute-start(bf16[256,2048]{1,0:T(8,128)(2,1)S(1)} %add_convert_fusion.2), channel_id=1, source_target_pairs={{0,1},{1,2},{2,3},{3,0},{4,5},{5,6},{6,7},{7,4},{8,9},{9,10},{10,1... | collective-permute-start | bytes 3145736 | tf_op jit(solution)/shard_map/ppermute | solution.py:287
  569.1 27.4 %collective-permute-start.18 = (bf16[256,2048]{1,0:T(8,128)(2,1)S(1)}, bf16[256,2048]{1,0:T(8,128)(2,1)S(1)}, u32[]{:S(2)}, u32[]{:S(2)}) collective-permute-start(bf16[256,2048]{1,0:T(8,128)(2,1)S(1)} %multiply_convert_fusion), channel_id=1, source_target_pairs={{0,1},{1,2},{2,3},{3,0},{4,5},{5,6},{6,7},{7,4},{8,9},{9,10},{10,1... | collective-permute-start | bytes 3145736 | tf_op jit(solution)/shard_map/ppermute | solution.py:287
  597.5 26.5 %collective-permute-start.19 = (bf16[256,2048]{1,0:T(8,128)(2,1)S(1)}, bf16[256,2048]{1,0:T(8,128)(2,1)}, u32[]{:S(2)}, u32[]{:S(2)}) collective-permute-start(bf16[256,2048]{1,0:T(8,128)(2,1)S(1)} %collective-permute-done.18), channel_id=1, source_target_pairs={{0,1},{1,2},{2,3},{3,0},{4,5},{5,6},{6,7},{7,4},{8,9},{9,10},{10,1... | collective-permute-start | bytes 3145736 | tf_op jit(solution)/shard_map/ppermute | solution.py:287
  624.1 16.8 %collective-permute-start.20 = (bf16[256,2048]{1,0:T(8,128)(2,1)}, bf16[256,2048]{1,0:T(8,128)(2,1)S(1)}, u32[]{:S(2)}, u32[]{:S(2)}) collective-permute-start(bf16[256,2048]{1,0:T(8,128)(2,1)} %collective-permute-done.19), channel_id=1, source_target_pairs={{0,1},{1,2},{2,3},{3,0},{4,5},{5,6},{6,7},{7,4},{8,9},{9,10},{10,1... | collective-permute-start | bytes 3145736 | tf_op jit(solution)/shard_map/ppermute | solution.py:287
  724.2 26.6 %collective-permute-start.21 = (bf16[256,2048]{1,0:T(8,128)(2,1)S(1)}, bf16[256,2048]{1,0:T(8,128)(2,1)S(1)}, u32[]{:S(2)}, u32[]{:S(2)}) collective-permute-start(bf16[256,2048]{1,0:T(8,128)(2,1)S(1)} %convolution_convert_fusion.4), channel_id=1, source_target_pairs={{0,1},{1,2},{2,3},{3,0},{4,5},{5,6},{6,7},{7,4},{8,9},{9,10},{10,1... | collective-permute-start | bytes 3145736 | tf_op jit(solution)/shard_map/ppermute | solution.py:287
  756.6 21.5 %collective-permute-start.22 = (bf16[256,2048]{1,0:T(8,128)(2,1)}, bf16[256,2048]{1,0:T(8,128)(2,1)S(1)}, u32[]{:S(2)}, u32[]{:S(2)}) collective-permute-start(bf16[256,2048]{1,0:T(8,128)(2,1)} %add_convert_fusion.1), channel_id=1, source_target_pairs={{0,1},{1,2},{2,3},{3,0},{4,5},{5,6},{6,7},{7,4},{8,9},{9,10},{10,1... | collective-permute-start | bytes 3145736 | tf_op jit(solution)/shard_map/ppermute | solution.py:287
  779.4 36.3 %collective-permute-start.23 = (bf16[256,2048]{1,0:T(8,128)(2,1)}, bf16[256,2048]{1,0:T(8,128)(2,1)}, u32[]{:S(2)}, u32[]{:S(2)}) collective-permute-start(bf16[256,2048]{1,0:T(8,128)(2,1)} %add_convert_fusion), channel_id=1, source_target_pairs={{0,1},{1,2},{2,3},{3,0},{4,5},{5,6},{6,7},{7,4},{8,9},{9,10},{10,1... | collective-permute-start | bytes 3145736 | tf_op jit(solution)/shard_map/ppermute | solution.py:287
  (86 other events, 1151.9 us)
Sparse Core Ops, SparseCore 0:
  10.7 57.0 all-gather.6
  69.7 54.2 all-gather.8
  125.9 54.2 all-gather.10
  181.9 55.8 all-gather.12
  423.6 68.8 reduce-scatter.3
  496.0 116.1 reduce-scatter.5
  718.5 72.4 reduce-scatter.7
where the time goes:
time: 837 us; the launch traced here: 829 us
  waiting for transfers between devices  432 us (52%)
  matrix products  219 us (26%)
  blocking collectives  59.6 us (7%)
  Pallas kernels  41.1 us (5%)
  other arithmetic  34.6 us (4%)
  local copies, waits for them, and re-layouts  18.7 us (2%)
  between operations  16.1 us (2%)
    ppermute x24, waiting for transfers between devices, shift(): return lax.ppermute(value, 'mp', ring)  430 us
    dot_general x20, matrix products, dot_right_t(): lax.dot_general(left, right, (((1,), (1,)), ((), ())), preferred_element_...  91 us
    dot_general x20, matrix products, dot_plain(): return jnp.dot(left, right, preferred_element_type=F32)  73.9 us
    dot_general x4, matrix products, dot_left_t(): lax.dot_general(left, right, (((0,), (0,)), ((), ())), preferred_element_...  54.2 us
    pallas_call x1, Pallas kernels, attention_backward(): pl.pallas_call(functools.partial(backward_kernel, n, rows), grid_spec=plt...  26.7 us
    psum x1, blocking collectives, local(): totals = lax.psum(jnp.concatenate([own, post], axis=1), 'dp')  23.6 us
  transfers between devices with their start and end apart: 31, of which 24 were waited for; matrix products, arithmetic and copies ran while one was open for 29% of the time, Pallas kernels for 5%

commit v1 on v0

--- a/solution.py
+++ b/solution.py
@@ -46,17 +46,20 @@
     )
 
 
-def masked_scores(queries, keys, rows, last):
-    scores = dot_right_t(queries, keys) * (HD ** (-0.5))
-    row = lax.broadcasted_iota(jnp.int32, (rows, last), 0) + (last - rows)
-    col = lax.broadcasted_iota(jnp.int32, (rows, last), 1)
-    return jnp.where(col <= row, scores, -1e30)
+def masked_scores(keys, queries, last, rows):
+    scores = dot_right_t(keys, queries) * (HD ** (-0.5))
+    row = lax.broadcasted_iota(jnp.int32, (rows, rows), 0)
+    col = lax.broadcasted_iota(jnp.int32, (rows, rows), 1)
+    corner = jnp.where(row <= col, scores[last - rows :, :], -1e30)
+    if last == rows:
+        return corner
+    return jnp.concatenate([scores[: last - rows, :], corner], axis=0)
 
 
 def forward_kernel(n, rows, me_ref, *refs):
     q_in, k_in, v_in = refs[:n], refs[n : 2 * n], refs[2 * n : 3 * n]
     rate_q, rate_k, gain_q, gain_k, cosine, sine = refs[3 * n : 3 * n + 6]
-    attn, q_out, k_out, v_out, lse = refs[3 * n + 6 :]
+    attn, q_out, k_out, v_out, lse, turned_v = refs[3 * n + 6 :]
     me = me_ref[0]
 
     def place(s):
@@ -73,15 +76,17 @@
             turned = normed * c + pltpu.roll(normed, HD // 2, 1) * d
             dst[at, :] = turned.astype(BF)
         v_out[at, :] = v_in[s][...].astype(BF)
+    turned_v[...] = v_out[...].T
     for piece in range(n):
         first, last = piece * rows, (piece + 1) * rows
-        scores = masked_scores(q_out[first:last, :], k_out[:last, :], rows, last)
-        peak = jnp.max(scores, axis=1, keepdims=True)
+        scores = masked_scores(k_out[:last, :], q_out[first:last, :], last, rows)
+        peak = jnp.max(scores, axis=0, keepdims=True)
         grown = jnp.exp(scores - peak)
-        total = jnp.sum(grown, axis=1, keepdims=True)
-        lse[0, first:last, :] = peak + jnp.log(total)
+        total = jnp.sum(grown, axis=0, keepdims=True)
+        lse[0, :, first:last] = peak + jnp.log(total)
         probs = (grown * (1.0 / total)).astype(BF)
-        attn[pl.ds(place(piece), rows), :] = dot_plain(probs, v_out[:last, :]).astype(BF)
+        out = dot_plain(turned_v[:, :last], probs)
+        attn[pl.ds(place(piece), rows), :] = out.T.astype(BF)
 
 
 def backward_kernel(n, rows, me_ref, *refs):
@@ -90,7 +95,7 @@
         3 * n : 3 * n + 10
     ]
     t_q, t_k, d_v, sums, gains = refs[3 * n + 10 : 3 * n + 15]
-    grads, acc_q, acc_k, acc_v = refs[3 * n + 15 :]
+    grads, turned_k, acc_q, acc_k, acc_v = refs[3 * n + 15 :]
     me = me_ref[0]
     scale = HD ** (-0.5)
 
@@ -99,20 +104,25 @@
 
     for s in range(n):
         grads[pl.ds(place(s), rows), :] = g_in[s][...]
-    acc_k[...] = jnp.zeros_like(acc_k)
-    acc_v[...] = jnp.zeros_like(acc_v)
-    for piece in range(n):
+    turned_k[...] = k_rot[...].T
+    for piece in reversed(range(n)):
         first, last = piece * rows, (piece + 1) * rows
         queries, keys = q_rot[first:last, :], k_rot[:last, :]
         grad = grads[first:last, :]
-        scores = masked_scores(queries, keys, rows, last)
-        probs = jnp.exp(scores - lse[0, first:last, :])
-        d_probs = dot_right_t(grad, value[:last, :])
-        delta = jnp.sum(probs * d_probs, axis=1, keepdims=True)
+        scores = masked_scores(keys, queries, last, rows)
+        probs = jnp.exp(scores - lse[0, :, first:last])
+        d_probs = dot_right_t(value[:last, :], grad)
+        delta = jnp.sum(probs * d_probs, axis=0, keepdims=True)
         d_scores = (probs * (d_probs - delta) * scale).astype(BF)
-        acc_v[:last, :] += dot_left_t(probs.astype(BF), grad)
-        acc_q[first:last, :] = dot_plain(d_scores, keys)
-        acc_k[:last, :] += dot_left_t(d_scores, queries)
+        add_v = dot_plain(probs.astype(BF), grad)
+        add_k = dot_plain(d_scores, queries)
+        if piece == n - 1:
+            acc_v[...] = add_v
+            acc_k[...] = add_k
+        else:
+            acc_v[:last, :] += add_v
+            acc_k[:last, :] += add_k
+        acc_q[first:last, :] = dot_plain(turned_k[:, :last], d_scores).T
     ones = jnp.ones((8, HD), F32)
     head = pl.program_id(0)
     for which, (acc, src, rate, gain, out) in enumerate(
@@ -166,9 +176,10 @@
             num_scalar_prefetch=1,
             grid=(heads,),
             in_specs=part(0) + part(1) + part(2) + [whole, whole, gain, gain, whole, whole],
-            out_specs=[column] * 4 + [pl.BlockSpec((1, L, 1), lambda h, m: (h, 0, 0))],
+            out_specs=[column] * 4 + [pl.BlockSpec((1, 1, L), lambda h, m: (h, 0, 0))],
+            scratch_shapes=[pltpu.VMEM((HD, L), BF)],
         ),
-        out_shape=[low] * 4 + [jax.ShapeDtypeStruct((heads, L, 1), F32)],
+        out_shape=[low] * 4 + [jax.ShapeDtypeStruct((heads, 1, L), F32)],
         compiler_params=pltpu.CompilerParams(vmem_limit_bytes=48 << 20),
         cost_estimate=pl.CostEstimate(
             flops=2 * heads * L * L * HD,
@@ -213,7 +224,7 @@
             + part(0)
             + [whole, whole, gain, gain, whole, whole]
             + [column] * 3
-            + [pl.BlockSpec((1, L, 1), lambda h, m: (h, 0, 0))],
+            + [pl.BlockSpec((1, 1, L), lambda h, m: (h, 0, 0))],
             out_specs=[column] * 3
             + [
                 pl.BlockSpec((2, 8, L), lambda h, m: (0, 0, 0)),
@@ -221,6 +232,7 @@
             ],
             scratch_shapes=[
                 pltpu.VMEM((L, HD), BF),
+                pltpu.VMEM((HD, L), BF),
                 pltpu.VMEM((L, HD), F32),
                 pltpu.VMEM((L, HD), F32),
                 pltpu.VMEM((L, HD), F32),
@@ -258,6 +270,43 @@
     )
 
 
+def weight_kernel(n, *refs):
+    x_in, d_in, a_in = refs[:n], refs[n : 2 * n], refs[2 * n : 3 * n]
+    attn, out = refs[3 * n :]
+    rows, wide = d_in[0].shape
+    one = sum(dot_left_t(x_in[s][...], d_in[s][...]) for s in range(n))
+    out[:, :wide] = one.astype(BF)
+    two = sum(
+        dot_left_t(a_in[s][...], attn[s * rows : (s + 1) * rows, :]) for s in range(n)
+    )
+    out[:, wide:] = two.astype(BF)
+
+
+def attention_weights(held_x, d_qkv, held_a, attn):
+    n, (rows, wide) = len(held_x), d_qkv[0].shape
+    width, narrow = held_x[0].shape[1], attn.shape[1]
+    tile = min(256, width)
+    step = pl.BlockSpec((rows, tile), lambda i: (0, i))
+    once = [pl.BlockSpec((rows, wide), lambda i: (0, 0), pipeline_mode=pl.Buffered(1))]
+    return pl.pallas_call(
+        functools.partial(weight_kernel, n),
+        grid=(width // tile,),
+        in_specs=[step] * n
+        + once * n
+        + [step] * n
+        + [pl.BlockSpec((n * rows, narrow), lambda i: (0, 0), pipeline_mode=pl.Buffered(1))],
+        out_specs=pl.BlockSpec((tile, wide + narrow), lambda i: (i, 0)),
+        out_shape=jax.ShapeDtypeStruct((width, wide + narrow), BF),
+        compiler_params=pltpu.CompilerParams(vmem_limit_bytes=40 << 20),
+        cost_estimate=pl.CostEstimate(
+            flops=2 * n * rows * width * (wide + narrow),
+            bytes_accessed=2 * (width + n * rows) * (wide + narrow) + 4 * n * rows * width,
+            transcendentals=0,
+        ),
+        name="attention_weights",
+    )(*held_x, *d_qkv, *held_a, attn)
+
+
 def local(
     n,
     groups,
@@ -286,6 +335,12 @@
     def shift(value):
         return lax.ppermute(value, "mp", ring)
 
+    def sum_all(value):
+        total = value
+        for k in range(1, n):
+            total = total + lax.ppermute(value, "mp", [(i, (i + k) % n) for i in range(n)])
+        return total
+
     def reorder(stacked):
         turned = stacked[::-1]
         return lax.dynamic_slice_in_dim(
@@ -341,11 +396,10 @@
     full_down = lax.all_gather(w_down, "dp", axis=1, tiled=True)
     cosine, sine = rope_tables()
 
-    held_x = gather_ring(inputs, 1, n - 2)
-    pieces = [dot_plain(x, w_qkv) for x in held_x]
-    last, pieces[0] = lax.optimization_barrier((held_x[-1], pieces[0]))
-    held_x.append(gather_ring(last, n - 1)[1])
-    pieces.append(dot_plain(held_x[-1], w_qkv))
+    held_x = gather_ring(inputs)
+    pieces = []
+    for x in held_x:
+        pieces.append(dot_plain(x, w_qkv))
     squares = jnp.stack(
         [
             jnp.stack(
@@ -357,7 +411,7 @@
             for p in pieces
         ]
     )
-    squares = lax.psum(reorder(squares), "mp")
+    squares = sum_all(reorder(squares))
     rates = lax.rsqrt(squares / width + epsilon)
     rate_q = jnp.broadcast_to(rates[:, 0].reshape(L, 1), (L, HD))
     rate_k = jnp.broadcast_to(rates[:, 1].reshape(L, 1), (L, HD))
@@ -414,7 +468,7 @@
     d_attn_proj = (
         rate_a * (scaled_a - hat_a * jnp.mean(scaled_a * hat_a, axis=1, keepdims=True))
     ).astype(BF)
-    held_a = gather_ring(d_attn_proj, after={n - 1: grad_down})
+    held_a = gather_ring(d_attn_proj, after={max(n - 2, 1): grad_down})
     grad_gate_up = lax.psum_scatter(gate_up, "dp", scatter_dimension=0, tiled=True)
     d_attn = [dot_plain(a, out_t).astype(BF) for a in held_a]
     t_q, t_k, d_value, sums, head_gains = attention_backward(
@@ -433,7 +487,7 @@
         lse,
     )
     sums = reorder(sums[:, 0, :].reshape(2, n, rows).transpose(1, 0, 2))
-    sums = lax.psum(sums, "mp")
+    sums = sum_all(sums)
     back = reorder(jnp.concatenate([rates, sums / width], axis=1))
     d_qkv = []
     for s in range(n):
@@ -445,21 +499,17 @@
             parts.append((rate * (t[at] - raw * (rate * back[s, 2 + which][:, None]))).astype(BF))
         parts.append(d_value[at])
         d_qkv.append(jnp.concatenate(parts, axis=1))
-    all_x, all_d = jnp.concatenate(held_x, axis=0), jnp.concatenate(d_qkv, axis=0)
-    dw_qkv = dot_left_t(all_x, all_d).astype(BF)
-    all_a = jnp.concatenate(held_a, axis=0)
-    dw_out = dot_left_t(all_a, attn).astype(BF)
-    grad_attn = lax.psum_scatter(
-        jnp.concatenate([dw_qkv, dw_out], axis=1), "dp", scatter_dimension=0, tiled=True
-    )
+    dw_attn = attention_weights(held_x, d_qkv, held_a, attn)
+    grad_attn = lax.psum_scatter(dw_attn, "dp", scatter_dimension=0, tiled=True)
+    input_grad = d_resid + scatter_ring(
+        lambda s: dot_right_t(d_qkv[s], w_qkv), {n - 1: grad_gate_up}
+    )
+
+    grad_attn, input_grad = lax.optimization_barrier((grad_attn, input_grad))
     grad_query = grad_attn[:, :head_cols].astype(F32)
     grad_key = grad_attn[:, head_cols : 2 * head_cols].astype(F32)
     grad_value = grad_attn[:, 2 * head_cols : 3 * head_cols].astype(F32)
     grad_out = grad_attn[:, 3 * head_cols :].astype(F32).T
-    input_grad = d_resid + scatter_ring(
-        lambda s: dot_right_t(d_qkv[s], w_qkv), {n - 1: grad_gate_up}
-    )
-
     grad_gate = grad_gate_up[:, :units].astype(F32)
     grad_up = grad_gate_up[:, units:].astype(F32)
 

time: 837 us -> 832 us (level)
  matrix products: 219 us -> 201 us
  starting transfers between devices: 8.22 us -> 22.1 us
  Pallas kernels: 41.1 us -> 53.2 us
    dot_general x4 -> x2, matrix products: 54.2 us -> 37.6 us  [dot_left_t(): lax.dot_general(left, right, (((0,), (0,)), ((), ())), preferred_element_...]
    pallas_call x0 -> x1, Pallas kernels: none -> 13.1 us  [attention_weights(): pl.pallas_call(functools.partial(weight_kernel, n), grid=(width // tile,)...]
    psum x2 -> x1, blocking collectives: 26.5 us -> 26 us  [local(): post = lax.psum(jnp.stack([grad_gain_a, grad_gain_m]), 'mp')]
  transfers between devices with their start and end apart: 31 -> 37, of which waited for: 24 -> 24; matrix products, arithmetic and copies ran while one was open for 29% -> 26% of each run, Pallas kernels for 5% -> 6%
where the time goes in v1:
time: 832 us; the launch traced here: 823 us
  waiting for transfers between devices  426 us (51%)
  matrix products  201 us (24%)
  blocking collectives  58 us (7%)
  Pallas kernels  53.2 us (6%)
  other arithmetic  29.5 us (4%)
  starting transfers between devices  22.1 us (3%)
  local copies, waits for them, and re-layouts  17.2 us (2%)
  between operations  16.3 us (2%)
    ppermute x24, waiting for transfers between devices, shift(): return lax.ppermute(value, 'mp', ring)  423 us
    dot_general x20, matrix products, dot_right_t(): lax.dot_general(left, right, (((1,), (1,)), ((), ())), preferred_element_...  91 us
    dot_general x20, matrix products, dot_plain(): return jnp.dot(left, right, preferred_element_type=F32)  72.4 us
    dot_general x2, matrix products, dot_left_t(): lax.dot_general(left, right, (((0,), (0,)), ((), ())), preferred_element_...  37.6 us
    pallas_call x1, Pallas kernels, attention_backward(): pl.pallas_call(functools.partial(backward_kernel, n, rows), grid_spec=plt...  26.5 us
    psum x1, blocking collectives, local(): post = lax.psum(jnp.stack([grad_gain_a, grad_gain_m]), 'mp')  26 us
    psum x1, blocking collectives, local(): totals = lax.psum(jnp.concatenate([own, post], axis=1), 'dp')  23.1 us
  transfers between devices with their start and end apart: 37, of which 24 were waited for; matrix products, arithmetic and copies ran while one was open for 26% of the time, Pallas kernels for 6%

profile of v1, /device:TPU:0, one launch (start us, length us, event | category | flops | bytes accessed | tf_op | source)
XLA Modules:
  0.0 822.7 jit_solution(11274965984228811437)
XLA Ops:
  15.2 25.2 %collective-permute-done.refs_1_ = bf16[256,2048]{1,0:T(8,128)(2,1)S(1)} collective-permute-done((bf16[256,2048]{1,0:T(8,128)(2,1)S(1)}, bf16[256,2048]{1,0:T(8,128)(2,1)S(1)}, u32[]{:S(2)}, u32[]{:S(2)}) %collective-permute-start) | collective-permute-done | bytes 1048608 | tf_op jit(solution)/shard_map/ppermute | solution.py:336
  40.5 26.0 %collective-permute-done.1.refs_2_ = bf16[256,2048]{1,0:T(8,128)(2,1)S(1)} collective-permute-done((bf16[256,2048]{1,0:T(8,128)(2,1)S(1)}, bf16[256,2048]{1,0:T(8,128)(2,1)S(1)}, u32[]{:S(2)}, u32[]{:S(2)}) %collective-permute-start.1) | collective-permute-done | bytes 1048608 | tf_op jit(solution)/shard_map/ppermute | solution.py:336
  66.8 8.8 %all-gather.1 = bf16[8,1,640]{2,1,0:T(2,128)(2,1)S(1)} all-gather(bf16[1,1,640]{2,1,0:T(2,128)(2,1)S(1)} %reshape.219), channel_id=2, replica_groups=mesh['dp'=8,'mp'=4] {'dp'}, dimensions={0}, use_global_device_ids=true | all-gather | bytes 11520 | tf_op jit(solution)/shard_map/all_gather | solution.py:382
  78.9 13.0 %collective-permute-done.2.refs_3_ = bf16[256,2048]{1,0:T(8,128)(2,1)} collective-permute-done((bf16[256,2048]{1,0:T(8,128)(2,1)S(1)}, bf16[256,2048]{1,0:T(8,128)(2,1)}, u32[]{:S(2)}, u32[]{:S(2)}) %collective-permute-start.2) | collective-permute-done | bytes 1048608 | tf_op jit(solution)/shard_map/ppermute | solution.py:336
  111.4 13.5 %attention_forward.1 = (bf16[1024,512]{1,0:T(8,128)(2,1)S(1)}, bf16[1024,512]{1,0:T(8,128)(2,1)S(1)}, bf16[1024,512]{1,0:T(8,128)(2,1)S(1)}, bf16[1024,512]{1,0:T(8,128)(2,1)}, f32[4,1,1024]{2,1,0:T(1,128)S(1)}) custom-call(s32[1]{0:T(128)} %bitcast.me_ref, f32[256,1536]{1,0:T(8,128)} %copy-done.26, f32[256,1536]{1,0:T(8,128)} %copy-done.25, ...), custom_call_target="tpu_custom_call" | custom-call | flops 1073741824 | bytes 11534336 | tf_op jit(solution)/shard_map/attention_forward/pallas_call | solution.py:173
  128.2 21.5 %collective-permute-done.6 = bf16[256,2048]{1,0:T(8,128)(2,1)S(1)} collective-permute-done((bf16[256,2048]{1,0:T(8,128)(2,1)S(1)}, bf16[256,2048]{1,0:T(8,128)(2,1)S(1)}, u32[]{:S(2)}, u32[]{:S(2)}) %collective-permute-start.6) | collective-permute-done | bytes 1048608 | tf_op jit(solution)/shard_map/ppermute | solution.py:336
  151.4 22.2 %collective-permute-done.7 = bf16[256,2048]{1,0:T(8,128)(2,1)S(1)} collective-permute-done((bf16[256,2048]{1,0:T(8,128)(2,1)S(1)}, bf16[256,2048]{1,0:T(8,128)(2,1)S(1)}, u32[]{:S(2)}, u32[]{:S(2)}) %collective-permute-start.7) | collective-permute-done | bytes 1048608 | tf_op jit(solution)/shard_map/ppermute | solution.py:336
  174.7 21.0 %collective-permute-done.8 = bf16[256,2048]{1,0:T(8,128)(2,1)S(1)} collective-permute-done((bf16[256,2048]{1,0:T(8,128)(2,1)S(1)}, bf16[256,2048]{1,0:T(8,128)(2,1)S(1)}, u32[]{:S(2)}, u32[]{:S(2)}) %collective-permute-start.8) | collective-permute-done | bytes 1048608 | tf_op jit(solution)/shard_map/ppermute | solution.py:336
  197.5 23.1 %collective-permute-done.9 = bf16[256,2048]{1,0:T(8,128)(2,1)} collective-permute-done((bf16[256,2048]{1,0:T(8,128)(2,1)S(1)}, bf16[256,2048]{1,0:T(8,128)(2,1)}, u32[]{:S(2)}, u32[]{:S(2)}) %collective-permute-start.9) | collective-permute-done | bytes 1048608 | tf_op jit(solution)/shard_map/ppermute | solution.py:336
  256.6 15.2 %collective-permute-done.12 = bf16[256,2048]{1,0:T(8,128)(2,1)S(1)} collective-permute-done((bf16[256,2048]{1,0:T(8,128)(2,1)S(1)}, bf16[256,2048]{1,0:T(8,128)(2,1)S(1)}, u32[]{:S(2)}, u32[]{:S(2)}) %collective-permute-start.12) | collective-permute-done | bytes 1048608 | tf_op jit(solution)/shard_map/ppermute | solution.py:336
  274.3 20.0 %collective-permute-done.11 = bf16[256,2048]{1,0:T(8,128)(2,1)S(1)} collective-permute-done((bf16[256,2048]{1,0:T(8,128)(2,1)}, bf16[256,2048]{1,0:T(8,128)(2,1)S(1)}, u32[]{:S(2)}, u32[]{:S(2)}) %collective-permute-start.11) | collective-permute-done | bytes 1048608 | tf_op jit(solution)/shard_map/ppermute | solution.py:336
  303.2 12.8 %collective-permute-done.13 = bf16[256,2048]{1,0:T(8,128)(2,1)S(1)} collective-permute-done((bf16[256,2048]{1,0:T(8,128)(2,1)S(1)}, bf16[256,2048]{1,0:T(8,128)(2,1)S(1)}, u32[]{:S(2)}, u32[]{:S(2)}) %collective-permute-start.13) | collective-permute-done | bytes 1048608 | tf_op jit(solution)/shard_map/ppermute | solution.py:336
  323.1 19.7 %collective-permute-done.14 = bf16[256,2048]{1,0:T(8,128)(2,1)S(1)} collective-permute-done((bf16[256,2048]{1,0:T(8,128)(2,1)S(1)}, bf16[256,2048]{1,0:T(8,128)(2,1)S(1)}, u32[]{:S(2)}, u32[]{:S(2)}) %collective-permute-start.14) | collective-permute-done | bytes 1048608 | tf_op jit(solution)/shard_map/ppermute | solution.py:336
  349.4 25.4 %collective-permute-done.15 = bf16[256,2048]{1,0:T(8,128)(2,1)S(1)} collective-permute-done((bf16[256,2048]{1,0:T(8,128)(2,1)S(1)}, bf16[256,2048]{1,0:T(8,128)(2,1)S(1)}, u32[]{:S(2)}, u32[]{:S(2)}) %collective-permute-start.15) | collective-permute-done | bytes 1048608 | tf_op jit(solution)/shard_map/ppermute | solution.py:336
  374.8 24.5 %collective-permute-done.16 = bf16[256,2048]{1,0:T(8,128)(2,1)S(1)} collective-permute-done((bf16[256,2048]{1,0:T(8,128)(2,1)S(1)}, bf16[256,2048]{1,0:T(8,128)(2,1)S(1)}, u32[]{:S(2)}, u32[]{:S(2)}) %collective-permute-start.16) | collective-permute-done | bytes 1048608 | tf_op jit(solution)/shard_map/ppermute | solution.py:336
  399.4 23.7 %collective-permute-done.17 = bf16[256,2048]{1,0:T(8,128)(2,1)S(1)} collective-permute-done((bf16[256,2048]{1,0:T(8,128)(2,1)S(1)}, bf16[256,2048]{1,0:T(8,128)(2,1)S(1)}, u32[]{:S(2)}, u32[]{:S(2)}) %collective-permute-start.17) | collective-permute-done | bytes 1048608 | tf_op jit(solution)/shard_map/ppermute | solution.py:336
  424.1 11.2 %convolution_convert_fusion.1 = bf16[2048,2048]{1,0:T(8,128)(2,1)} fusion(bf16[256,2048]{1,0:T(8,128)(2,1)S(1)} %copy-done.84, bf16[256,2048]{1,0:T(8,128)(2,1)S(1)} %copy-done.89, bf16[256,2048]{1,0:T(8,128)(2,1)S(1)} %copy-done.90, bf16[256,2048]{1,0:T(8,128)(2,1)S(1)} %get-tuple-element.154, bf16[256,2048]{1,0:T(8,128)(2,1)S(1)} %collective-permute-done.17, ...), kind=kOutput, calls=%fused_computation.16 | convolution fusion | flops 8627683328 | bytes 16777216 | tf_op jit(solution)/shard_map/dot_general | solution.py:31
  435.6 10.6 %multiply_convert_fusion.7 = (bf16[256,2048]{1,0:T(8,128)(2,1)}, bf16[256,2048]{1,0:T(8,128)(2,1)}) fusion(f32[256,2048]{1,0:T(8,128)} %copy-done.82, f32[256,2048]{1,0:T(8,128)} %get-tuple-element.155, bf16[256,2048]{1,0:T(8,128)(2,1)} %copy-done.40, bf16[2048,2048]{1,0:T(8,128)(2,1)} %all-gather.13.cloned.1.call-done), kind=kOutput, calls=%fused_computation.73 | convolution fusion | flops 2154299392 | bytes 15728640 | tf_op jit(solution)/shard_map/dot_general | solution.py:27
  446.3 8.5 %multiply_convert_fusion.1 = (bf16[256,2048]{1,0:T(8,128)(2,1)}, bf16[256,2048]{1,0:T(8,128)(2,1)}) fusion(f32[256,2048]{1,0:T(8,128)S(1)} %copy-done.77, f32[256,2048]{1,0:T(8,128)S(1)} %copy-done.85, bf16[256,2048]{1,0:T(8,128)(2,1)S(1)} %copy-done.65, bf16[2048,2048]{1,0:T(8,128)(2,1)} %all-gather.13.cloned.1.call-done), kind=kOutput, calls=%fused_computation.67 | convolution fusion | flops 2154299392 | bytes 15728640 | tf_op jit(solution)/shard_map/dot_general | solution.py:27
  463.7 26.4 %convolution_convert_fusion = bf16[2048,4096]{1,0:T(8,128)(2,1)} fusion(bf16[256,2048]{1,0:T(8,128)(2,1)} %get-tuple-element.103, bf16[256,2048]{1,0:T(8,128)(2,1)} %get-tuple-element.101, bf16[256,2048]{1,0:T(8,128)(2,1)} %get-tuple-element.99, bf16[256,2048]{1,0:T(8,128)(2,1)} %get-tuple-element.105, bf16[256,2048]{1,0:T(8,128)(2,1)} %get-tuple-element.104, ...), kind=kOutput, calls=%fused_computation | convolution fusion | flops 17272143872 | bytes 29360128 | tf_op jit(solution)/shard_map/dot_general | solution.py:31
  510.9 14.8 %collective-permute-done.18 = bf16[256,2048]{1,0:T(8,128)(2,1)S(1)} collective-permute-done((bf16[256,2048]{1,0:T(8,128)(2,1)S(1)}, bf16[256,2048]{1,0:T(8,128)(2,1)S(1)}, u32[]{:S(2)}, u32[]{:S(2)}) %collective-permute-start.18) | collective-permute-done | bytes 1048608 | tf_op jit(solution)/shard_map/ppermute | solution.py:336
  535.6 13.2 %collective-permute-done.19 = bf16[256,2048]{1,0:T(8,128)(2,1)S(1)} collective-permute-done((bf16[256,2048]{1,0:T(8,128)(2,1)S(1)}, bf16[256,2048]{1,0:T(8,128)(2,1)S(1)}, u32[]{:S(2)}, u32[]{:S(2)}) %collective-permute-start.19) | collective-permute-done | bytes 1048608 | tf_op jit(solution)/shard_map/ppermute | solution.py:336
  557.9 12.6 %collective-permute-done.20 = bf16[256,2048]{1,0:T(8,128)(2,1)S(1)} collective-permute-done((bf16[256,2048]{1,0:T(8,128)(2,1)S(1)}, bf16[256,2048]{1,0:T(8,128)(2,1)S(1)}, u32[]{:S(2)}, u32[]{:S(2)}) %collective-permute-start.20) | collective-permute-done | bytes 1048608 | tf_op jit(solution)/shard_map/ppermute | solution.py:336
  572.7 23.1 %collective-permute-done.21.refs_9_ = bf16[256,2048]{1,0:T(8,128)(2,1)} collective-permute-done((bf16[256,2048]{1,0:T(8,128)(2,1)S(1)}, bf16[256,2048]{1,0:T(8,128)(2,1)}, u32[]{:S(2)}, u32[]{:S(2)}) %collective-permute-start.21) | collective-permute-done | bytes 1048608 | tf_op jit(solution)/shard_map/ppermute | solution.py:336
  595.8 23.5 %collective-permute-done.22.refs_10_ = bf16[256,2048]{1,0:T(8,128)(2,1)S(1)} collective-permute-done((bf16[256,2048]{1,0:T(8,128)(2,1)}, bf16[256,2048]{1,0:T(8,128)(2,1)S(1)}, u32[]{:S(2)}, u32[]{:S(2)}) %collective-permute-start.22) | collective-permute-done | bytes 1048608 | tf_op jit(solution)/shard_map/ppermute | solution.py:336
  627.1 10.0 %collective-permute-done.23.refs_11_ = bf16[256,2048]{1,0:T(8,128)(2,1)S(1)} collective-permute-done((bf16[256,2048]{1,0:T(8,128)(2,1)S(1)}, bf16[256,2048]{1,0:T(8,128)(2,1)S(1)}, u32[]{:S(2)}, u32[]{:S(2)}) %collective-permute-start.23) | collective-permute-done | bytes 1048608 | tf_op jit(solution)/shard_map/ppermute | solution.py:336
  639.8 26.5 %attention_backward.1 = (f32[1024,512]{1,0:T(8,128)}, f32[1024,512]{1,0:T(8,128)}, bf16[1024,512]{1,0:T(8,128)(2,1)S(1)}, f32[2,8,1024]{2,1,0:T(8,128)S(1)}, f32[4,2,128]{2,1,0:T(2,128)S(1)}) custom-call(s32[1]{0:T(128)} %bitcast.me_ref, f32[256,1536]{1,0:T(8,128)} %copy-done.26, f32[256,1536]{1,0:T(8,128)} %copy-done.25, f32[256,1536]{1,0:T(8,128)} %copy-done.24, ...), custom_call_target="tpu_custom_call" | custom-call | flops 2684354560 | bytes 13631488 | tf_op jit(solution)/shard_map/attention_backward/pallas_call | solution.py:217
  681.9 13.1 %attention_weights.1 = bf16[2048,2048]{1,0:T(8,128)(2,1)} custom-call(bf16[256,2048]{1,0:T(8,128)(2,1)S(1)} %copy-done.4, bf16[256,2048]{1,0:T(8,128)(2,1)S(1)} %copy-done.16, bf16[256,2048]{1,0:T(8,128)(2,1)S(1)} %copy-done.18, bf16[256,2048]{1,0:T(8,128)(2,1)} %collective-permute-done.2.refs_3_, bf16[256,1536]{1,0:T(8,128)(2,1)S(1)} %pad_maximum_fusion.1.refs_4_, ...), custom_call_target="tpu_custom_call" | custom-call | flops 8589934592 | bytes 20971520 | tf_op jit(solution)/shard_map/attention_weights/pallas_call | solution.py:291
  703.8 14.9 %collective-permute-done.27 = bf16[256,2048]{1,0:T(8,128)(2,1)} collective-permute-done((bf16[256,2048]{1,0:T(8,128)(2,1)}, bf16[256,2048]{1,0:T(8,128)(2,1)}, u32[]{:S(2)}, u32[]{:S(2)}) %collective-permute-start.27) | collective-permute-done | bytes 1048608 | tf_op jit(solution)/shard_map/ppermute | solution.py:336
  727.0 26.0 %psum.14 = f32[8,512]{1,0:T(8,128)S(1)} all-reduce(f32[8,512]{1,0:T(8,128)S(1)} %bitcast.143), channel_id=1, replica_groups=mesh['dp'=8,'mp'=4] {'mp'}, use_global_device_ids=true, to_apply=%region_17.0 | all-reduce | flops 4096 | bytes 32768 | tf_op jit(solution)/shard_map/psum | solution.py:516
  754.7 23.1 %psum.15 = f32[8,640]{1,0:T(8,128)S(1)} all-reduce(f32[8,640]{1,0:T(8,128)S(1)} %pad_maximum_fusion.7), channel_id=1, replica_groups=mesh['dp'=8,'mp'=4] {'dp'}, use_global_device_ids=true, to_apply=%region_18.0 | all-reduce | flops 5120 | bytes 40960 | tf_op jit(solution)/shard_map/psum | solution.py:520
  793.1 17.1 %collective-permute-done.29 = bf16[256,2048]{1,0:T(8,128)(2,1)S(1)} collective-permute-done((bf16[256,2048]{1,0:T(8,128)(2,1)}, bf16[256,2048]{1,0:T(8,128)(2,1)S(1)}, u32[]{:S(2)}, u32[]{:S(2)}) %collective-permute-start.29) | collective-permute-done | bytes 1048608 | tf_op jit(solution)/shard_map/ppermute | solution.py:336
  (400 shorter events, 216.0 us)
Async XLA Ops:
  7.2 84.7 %all-gather.7.cloned.1.call-start = ((), (), s32[]{:S(2)}) async-start(), calls=%async_computation.3 | async-start | bytes 9437184 | tf_op jit(solution)/shard_map/all_gather | solution.py:371
  10.6 210.0 %all-gather.9.cloned.1.call-start = ((), (), s32[]{:S(2)}) async-start(), calls=%async_computation.4 | async-start | bytes 9437184 | tf_op jit(solution)/shard_map/all_gather | solution.py:394
  11.3 216.6 %all-gather.11.cloned.1.call-start = ((), (), s32[]{:S(2)}) async-start(), calls=%async_computation.5 | async-start | bytes 9437184 | tf_op jit(solution)/shard_map/all_gather | solution.py:395
  12.1 225.6 %all-gather.13.cloned.1.call-start = ((), (), s32[]{:S(2)}) async-start(), calls=%async_computation.6 | async-start | bytes 9437184 | tf_op jit(solution)/shard_map/all_gather | solution.py:396
  12.1 28.3 %collective-permute-start = (bf16[256,2048]{1,0:T(8,128)(2,1)S(1)}, bf16[256,2048]{1,0:T(8,128)(2,1)S(1)}, u32[]{:S(2)}, u32[]{:S(2)}) collective-permute-start(bf16[256,2048]{1,0:T(8,128)(2,1)S(1)} %copy-done.4), channel_id=1, source_target_pairs={{0,1},{1,2},{2,3},{3,0},{4,5},{5,6},{6,7},{7,4},{8,9},{9,10},{10,1... | collective-permute-start | bytes 3145736 | tf_op jit(solution)/shard_map/ppermute | solution.py:336
  40.4 26.1 %collective-permute-start.1 = (bf16[256,2048]{1,0:T(8,128)(2,1)S(1)}, bf16[256,2048]{1,0:T(8,128)(2,1)S(1)}, u32[]{:S(2)}, u32[]{:S(2)}) collective-permute-start(bf16[256,2048]{1,0:T(8,128)(2,1)S(1)} %collective-permute-done.refs_1_), channel_id=1, source_target_pairs={{0,1},{1,2},{2,3},{3,0},{4,5},{5,6},{6,7},{7,4},{8,9},{9,10},{10,1... | collective-permute-start | bytes 3145736 | tf_op jit(solution)/shard_map/ppermute | solution.py:336
  40.4 555.3 %reduce-scatter.4.cloned.1.call-start = ((), (), s32[]{:S(2)}) async-start(), calls=%async_computation.7 | async-start | bytes 9437184 | tf_op jit(solution)/shard_map/reduce_scatter | solution.py:459
  66.5 25.4 %collective-permute-start.2 = (bf16[256,2048]{1,0:T(8,128)(2,1)S(1)}, bf16[256,2048]{1,0:T(8,128)(2,1)}, u32[]{:S(2)}, u32[]{:S(2)}) collective-permute-start(bf16[256,2048]{1,0:T(8,128)(2,1)S(1)} %collective-permute-done.1.refs_2_), channel_id=1, source_target_pairs={{0,1},{1,2},{2,3},{3,0},{4,5},{5,6},{6,7},{7,4},{8,9},{9,10},{10,1... | collective-permute-start | bytes 3145736 | tf_op jit(solution)/shard_map/ppermute | solution.py:336
  125.8 23.8 %collective-permute-start.6 = (bf16[256,2048]{1,0:T(8,128)(2,1)S(1)}, bf16[256,2048]{1,0:T(8,128)(2,1)S(1)}, u32[]{:S(2)}, u32[]{:S(2)}) collective-permute-start(bf16[256,2048]{1,0:T(8,128)(2,1)S(1)} %convolution_convert_fusion.2), channel_id=1, source_target_pairs={{0,1},{1,2},{2,3},{3,0},{4,5},{5,6},{6,7},{7,4},{8,9},{9,10},{10,1... | collective-permute-start | bytes 3145736 | tf_op jit(solution)/shard_map/ppermute | solution.py:336
  150.5 23.0 %collective-permute-start.7 = (bf16[256,2048]{1,0:T(8,128)(2,1)S(1)}, bf16[256,2048]{1,0:T(8,128)(2,1)S(1)}, u32[]{:S(2)}, u32[]{:S(2)}) collective-permute-start(bf16[256,2048]{1,0:T(8,128)(2,1)S(1)} %add_convert_fusion.7), channel_id=1, source_target_pairs={{0,1},{1,2},{2,3},{3,0},{4,5},{5,6},{6,7},{7,4},{8,9},{9,10},{10,1... | collective-permute-start | bytes 3145736 | tf_op jit(solution)/shard_map/ppermute | solution.py:336
  173.8 21.9 %collective-permute-start.8 = (bf16[256,2048]{1,0:T(8,128)(2,1)S(1)}, bf16[256,2048]{1,0:T(8,128)(2,1)S(1)}, u32[]{:S(2)}, u32[]{:S(2)}) collective-permute-start(bf16[256,2048]{1,0:T(8,128)(2,1)S(1)} %add_convert_fusion.6), channel_id=1, source_target_pairs={{0,1},{1,2},{2,3},{3,0},{4,5},{5,6},{6,7},{7,4},{8,9},{9,10},{10,1... | collective-permute-start | bytes 3145736 | tf_op jit(solution)/shard_map/ppermute | solution.py:336
  197.5 23.1 %collective-permute-start.9 = (bf16[256,2048]{1,0:T(8,128)(2,1)S(1)}, bf16[256,2048]{1,0:T(8,128)(2,1)}, u32[]{:S(2)}, u32[]{:S(2)}) collective-permute-start(bf16[256,2048]{1,0:T(8,128)(2,1)S(1)} %fusion.47), channel_id=1, source_target_pairs={{0,1},{1,2},{2,3},{3,0},{4,5},{5,6},{6,7},{7,4},{8,9},{9,10},{10,1... | collective-permute-start | bytes 3145736 | tf_op jit(solution)/shard_map/ppermute | solution.py:336
  220.6 24.8 %collective-permute-start.10 = (bf16[256,2048]{1,0:T(8,128)(2,1)}, bf16[256,2048]{1,0:T(8,128)(2,1)}, u32[]{:S(2)}, u32[]{:S(2)}) collective-permute-start(bf16[256,2048]{1,0:T(8,128)(2,1)} %collective-permute-done.9), channel_id=1, source_target_pairs={{0,1},{1,2},{2,3},{3,0},{4,5},{5,6},{6,7},{7,4},{8,9},{9,10},{10,1... | collective-permute-start | bytes 3145736 | tf_op jit(solution)/shard_map/ppermute | solution.py:336
  243.9 27.9 %collective-permute-start.12 = (bf16[256,2048]{1,0:T(8,128)(2,1)S(1)}, bf16[256,2048]{1,0:T(8,128)(2,1)S(1)}, u32[]{:S(2)}, u32[]{:S(2)}) collective-permute-start(bf16[256,2048]{1,0:T(8,128)(2,1)S(1)} %convolution_convert_fusion.4), channel_id=1, source_target_pairs={{0,1},{1,2},{2,3},{3,0},{4,5},{5,6},{6,7},{7,4},{8,9},{9,10},{10,1... | collective-permute-start | bytes 3145736 | tf_op jit(solution)/shard_map/ppermute | solution.py:336
  249.3 45.0 %collective-permute-start.11 = (bf16[256,2048]{1,0:T(8,128)(2,1)}, bf16[256,2048]{1,0:T(8,128)(2,1)S(1)}, u32[]{:S(2)}, u32[]{:S(2)}) collective-permute-start(bf16[256,2048]{1,0:T(8,128)(2,1)} %collective-permute-done.10), channel_id=1, source_target_pairs={{0,1},{1,2},{2,3},{3,0},{4,5},{5,6},{6,7},{7,4},{8,9},{9,10},{10,1... | collective-permute-start | bytes 3145736 | tf_op jit(solution)/shard_map/ppermute | solution.py:336
  274.2 41.8 %collective-permute-start.13 = (bf16[256,2048]{1,0:T(8,128)(2,1)S(1)}, bf16[256,2048]{1,0:T(8,128)(2,1)S(1)}, u32[]{:S(2)}, u32[]{:S(2)}) collective-permute-start(bf16[256,2048]{1,0:T(8,128)(2,1)S(1)} %add_convert_fusion.5), channel_id=1, source_target_pairs={{0,1},{1,2},{2,3},{3,0},{4,5},{5,6},{6,7},{7,4},{8,9},{9,10},{10,1... | collective-permute-start | bytes 3145736 | tf_op jit(solution)/shard_map/ppermute | solution.py:336
  316.3 26.5 %collective-permute-start.14 = (bf16[256,2048]{1,0:T(8,128)(2,1)S(1)}, bf16[256,2048]{1,0:T(8,128)(2,1)S(1)}, u32[]{:S(2)}, u32[]{:S(2)}) collective-permute-start(bf16[256,2048]{1,0:T(8,128)(2,1)S(1)} %add_convert_fusion.4), channel_id=1, source_target_pairs={{0,1},{1,2},{2,3},{3,0},{4,5},{5,6},{6,7},{7,4},{8,9},{9,10},{10,1... | collective-permute-start | bytes 3145736 | tf_op jit(solution)/shard_map/ppermute | solution.py:336
  349.4 25.4 %collective-permute-start.15 = (bf16[256,2048]{1,0:T(8,128)(2,1)S(1)}, bf16[256,2048]{1,0:T(8,128)(2,1)S(1)}, u32[]{:S(2)}, u32[]{:S(2)}) collective-permute-start(bf16[256,2048]{1,0:T(8,128)(2,1)S(1)} %get-tuple-element.107), channel_id=1, source_target_pairs={{0,1},{1,2},{2,3},{3,0},{4,5},{5,6},{6,7},{7,4},{8,9},{9,10},{10,1... | collective-permute-start | bytes 3145736 | tf_op jit(solution)/shard_map/ppermute | solution.py:336
  374.8 24.5 %collective-permute-start.16 = (bf16[256,2048]{1,0:T(8,128)(2,1)S(1)}, bf16[256,2048]{1,0:T(8,128)(2,1)S(1)}, u32[]{:S(2)}, u32[]{:S(2)}) collective-permute-start(bf16[256,2048]{1,0:T(8,128)(2,1)S(1)} %collective-permute-done.15), channel_id=1, source_target_pairs={{0,1},{1,2},{2,3},{3,0},{4,5},{5,6},{6,7},{7,4},{8,9},{9,10},{10,1... | collective-permute-start | bytes 3145736 | tf_op jit(solution)/shard_map/ppermute | solution.py:336
  399.4 23.7 %collective-permute-start.17 = (bf16[256,2048]{1,0:T(8,128)(2,1)S(1)}, bf16[256,2048]{1,0:T(8,128)(2,1)S(1)}, u32[]{:S(2)}, u32[]{:S(2)}) collective-permute-start(bf16[256,2048]{1,0:T(8,128)(2,1)S(1)} %collective-permute-done.16), channel_id=1, source_target_pairs={{0,1},{1,2},{2,3},{3,0},{4,5},{5,6},{6,7},{7,4},{8,9},{9,10},{10,1... | collective-permute-start | bytes 3145736 | tf_op jit(solution)/shard_map/ppermute | solution.py:336
  435.3 350.5 %reduce-scatter.8.cloned.1.call-start = ((), (), s32[]{:S(2)}) async-start(), calls=%async_computation.9 | async-start | bytes 18874368 | tf_op jit(solution)/shard_map/reduce_scatter | solution.py:472
  490.1 321.9 %reduce-scatter.6.cloned.1.call-start = ((), (), s32[]{:S(2)}) async-start(), calls=%async_computation.8 | async-start | bytes 9437184 | tf_op jit(solution)/shard_map/reduce_scatter | solution.py:503
  502.4 23.2 %collective-permute-start.18 = (bf16[256,2048]{1,0:T(8,128)(2,1)S(1)}, bf16[256,2048]{1,0:T(8,128)(2,1)S(1)}, u32[]{:S(2)}, u32[]{:S(2)}) collective-permute-start(bf16[256,2048]{1,0:T(8,128)(2,1)S(1)} %fusion.36), channel_id=1, source_target_pairs={{0,1},{1,2},{2,3},{3,0},{4,5},{5,6},{6,7},{7,4},{8,9},{9,10},{10,1... | collective-permute-start | bytes 3145736 | tf_op jit(solution)/shard_map/ppermute | solution.py:336
  525.9 22.8 %collective-permute-start.19 = (bf16[256,2048]{1,0:T(8,128)(2,1)S(1)}, bf16[256,2048]{1,0:T(8,128)(2,1)S(1)}, u32[]{:S(2)}, u32[]{:S(2)}) collective-permute-start(bf16[256,2048]{1,0:T(8,128)(2,1)S(1)} %add_convert_fusion.3), channel_id=1, source_target_pairs={{0,1},{1,2},{2,3},{3,0},{4,5},{5,6},{6,7},{7,4},{8,9},{9,10},{10,1... | collective-permute-start | bytes 3145736 | tf_op jit(solution)/shard_map/ppermute | solution.py:336
  549.1 21.4 %collective-permute-start.20 = (bf16[256,2048]{1,0:T(8,128)(2,1)S(1)}, bf16[256,2048]{1,0:T(8,128)(2,1)S(1)}, u32[]{:S(2)}, u32[]{:S(2)}) collective-permute-start(bf16[256,2048]{1,0:T(8,128)(2,1)S(1)} %add_convert_fusion.2), channel_id=1, source_target_pairs={{0,1},{1,2},{2,3},{3,0},{4,5},{5,6},{6,7},{7,4},{8,9},{9,10},{10,1... | collective-permute-start | bytes 3145736 | tf_op jit(solution)/shard_map/ppermute | solution.py:336
  572.7 23.1 %collective-permute-start.21 = (bf16[256,2048]{1,0:T(8,128)(2,1)S(1)}, bf16[256,2048]{1,0:T(8,128)(2,1)}, u32[]{:S(2)}, u32[]{:S(2)}) collective-permute-start(bf16[256,2048]{1,0:T(8,128)(2,1)S(1)} %multiply_convert_fusion.refs_8_), channel_id=1, source_target_pairs={{0,1},{1,2},{2,3},{3,0},{4,5},{5,6},{6,7},{7,4},{8,9},{9,10},{10,1... | collective-permute-start | bytes 3145736 | tf_op jit(solution)/shard_map/ppermute | solution.py:336
  595.8 23.5 %collective-permute-start.22 = (bf16[256,2048]{1,0:T(8,128)(2,1)}, bf16[256,2048]{1,0:T(8,128)(2,1)S(1)}, u32[]{:S(2)}, u32[]{:S(2)}) collective-permute-start(bf16[256,2048]{1,0:T(8,128)(2,1)} %collective-permute-done.21.refs_9_), channel_id=1, source_target_pairs={{0,1},{1,2},{2,3},{3,0},{4,5},{5,6},{6,7},{7,4},{8,9},{9,10},{10,1... | collective-permute-start | bytes 3145736 | tf_op jit(solution)/shard_map/ppermute | solution.py:336
  619.3 17.8 %collective-permute-start.23 = (bf16[256,2048]{1,0:T(8,128)(2,1)S(1)}, bf16[256,2048]{1,0:T(8,128)(2,1)S(1)}, u32[]{:S(2)}, u32[]{:S(2)}) collective-permute-start(bf16[256,2048]{1,0:T(8,128)(2,1)S(1)} %collective-permute-done.22.refs_10_), channel_id=1, source_target_pairs={{0,1},{1,2},{2,3},{3,0},{4,5},{5,6},{6,7},{7,4},{8,9},{9,10},{10,1... | collective-permute-start | bytes 3145736 | tf_op jit(solution)/shard_map/ppermute | solution.py:336
  667.5 6.3 collective-permute-start.24
  701.8 16.9 %collective-permute-start.27 = (bf16[256,2048]{1,0:T(8,128)(2,1)}, bf16[256,2048]{1,0:T(8,128)(2,1)}, u32[]{:S(2)}, u32[]{:S(2)}) collective-permute-start(bf16[256,2048]{1,0:T(8,128)(2,1)} %convolution_convert_fusion.3), channel_id=1, source_target_pairs={{0,1},{1,2},{2,3},{3,0},{4,5},{5,6},{6,7},{7,4},{8,9},{9,10},{10,1... | collective-permute-start | bytes 3145736 | tf_op jit(solution)/shard_map/ppermute | solution.py:336
  725.3 59.1 %collective-permute-start.28 = (bf16[256,2048]{1,0:T(8,128)(2,1)}, bf16[256,2048]{1,0:T(8,128)(2,1)S(1)}, u32[]{:S(2)}, u32[]{:S(2)}) collective-permute-start(bf16[256,2048]{1,0:T(8,128)(2,1)} %add_convert_fusion.1), channel_id=1, source_target_pairs={{0,1},{1,2},{2,3},{3,0},{4,5},{5,6},{6,7},{7,4},{8,9},{9,10},{10,1... | collective-permute-start | bytes 3145736 | tf_op jit(solution)/shard_map/ppermute | solution.py:336
  785.8 24.4 %collective-permute-start.29 = (bf16[256,2048]{1,0:T(8,128)(2,1)}, bf16[256,2048]{1,0:T(8,128)(2,1)S(1)}, u32[]{:S(2)}, u32[]{:S(2)}) collective-permute-start(bf16[256,2048]{1,0:T(8,128)(2,1)} %add_convert_fusion), channel_id=1, source_target_pairs={{0,1},{1,2},{2,3},{3,0},{4,5},{5,6},{6,7},{7,4},{8,9},{9,10},{10,1... | collective-permute-start | bytes 3145736 | tf_op jit(solution)/shard_map/ppermute | solution.py:336
  (106 other events, 1676.0 us)
Sparse Core Ops, SparseCore 0:
  10.7 56.9 all-gather.6
  69.6 54.2 all-gather.8
  125.8 54.2 all-gather.10
  181.8 55.8 all-gather.12
  435.5 68.5 reduce-scatter.3
  507.4 116.1 reduce-scatter.7
  695.1 71.7 reduce-scatter.5

commit v2 on v1

--- a/solution.py
+++ b/solution.py
@@ -95,7 +95,7 @@
         3 * n : 3 * n + 10
     ]
     t_q, t_k, d_v, sums, gains = refs[3 * n + 10 : 3 * n + 15]
-    grads, turned_k, acc_q, acc_k, acc_v = refs[3 * n + 15 :]
+    grads, turned_k, acc_q, acc_k, acc_v, acc_sums = refs[3 * n + 15 :]
     me = me_ref[0]
     scale = HD ** (-0.5)
 
@@ -123,8 +123,12 @@
             acc_v[:last, :] += add_v
             acc_k[:last, :] += add_k
         acc_q[first:last, :] = dot_plain(turned_k[:, :last], d_scores).T
-    ones = jnp.ones((8, HD), F32)
     head = pl.program_id(0)
+
+    @pl.when(head == 0)
+    def _():
+        acc_sums[...] = jnp.zeros_like(acc_sums)
+
     for which, (acc, src, rate, gain, out) in enumerate(
         ((acc_q, q_in, rate_q, gain_q, t_q), (acc_k, k_in, rate_k, gain_k, t_k))
     ):
@@ -136,27 +140,17 @@
             hat = src[s][...] * rate[at, :]
             column = column + jnp.sum(normed * hat, axis=0, keepdims=True)
             scaled = normed * gain[0]
-            out[s * rows : (s + 1) * rows, :] = scaled
-            line = lax.dot_general(
-                ones,
-                scaled * hat,
-                (((1,), (1,)), ((), ())),
-                precision=lax.Precision.HIGHEST,
-                preferred_element_type=F32,
-            )
-            here = (which, slice(None), slice(s * rows, (s + 1) * rows))
-
-            @pl.when(head == 0)
-            def _():
-                sums[here] = line
-
-            @pl.when(head > 0)
-            def _():
-                sums[here] += line
-
+            here = slice(s * rows, (s + 1) * rows)
+            out[here, :] = scaled
+            acc_sums[which, here, :] += scaled * hat
         gains[0, which : which + 1, :] = column
     for s in range(n):
         d_v[s * rows : (s + 1) * rows, :] = acc_v[pl.ds(place(s), rows), :].astype(BF)
+
+    @pl.when(head == pl.num_programs(0) - 1)
+    def _():
+        for which in range(2):
+            sums[which] = jnp.sum(acc_sums[which].T, axis=0, keepdims=True)
 
 
 def attention_forward(me, pieces, rate_q, rate_k, gain_q, gain_k, cosine, sine):
@@ -227,7 +221,7 @@
             + [pl.BlockSpec((1, 1, L), lambda h, m: (h, 0, 0))],
             out_specs=[column] * 3
             + [
-                pl.BlockSpec((2, 8, L), lambda h, m: (0, 0, 0)),
+                pl.BlockSpec((2, 1, L), lambda h, m: (0, 0, 0)),
                 pl.BlockSpec((1, 2, HD), lambda h, m: (h, 0, 0)),
             ],
             scratch_shapes=[
@@ -236,13 +230,14 @@
                 pltpu.VMEM((L, HD), F32),
                 pltpu.VMEM((L, HD), F32),
                 pltpu.VMEM((L, HD), F32),
+                pltpu.VMEM((2, L, HD), F32),
             ],
         ),
         out_shape=[
             wide,
             wide,
             jax.ShapeDtypeStruct((L, heads * HD), BF),
-            jax.ShapeDtypeStruct((2, 8, L), F32),
+            jax.ShapeDtypeStruct((2, 1, L), F32),
             jax.ShapeDtypeStruct((heads, 2, HD), F32),
         ],
         compiler_params=pltpu.CompilerParams(vmem_limit_bytes=48 << 20),
@@ -391,8 +386,10 @@
     own_cols = attn_gain.shape[0]
     gain_a = small[:, 2 * count : 2 * count + own_cols].reshape(width)
     gain_m = small[:, 2 * count + own_cols :].reshape(width)
-    full_gate = lax.all_gather(w_gate, "dp", axis=0, tiled=True)
-    full_up = lax.all_gather(w_up, "dp", axis=0, tiled=True)
+    full_gate_up = lax.all_gather(
+        jnp.concatenate([w_gate, w_up], axis=1), "dp", axis=0, tiled=True
+    )
+    full_gate, full_up = full_gate_up[:, :units], full_gate_up[:, units:]
     full_down = lax.all_gather(w_down, "dp", axis=1, tiled=True)
     cosine, sine = rope_tables()
 
@@ -468,7 +465,7 @@
     d_attn_proj = (
         rate_a * (scaled_a - hat_a * jnp.mean(scaled_a * hat_a, axis=1, keepdims=True))
     ).astype(BF)
-    held_a = gather_ring(d_attn_proj, after={max(n - 2, 1): grad_down})
+    held_a = gather_ring(d_attn_proj, after={n - 1: grad_down})
     grad_gate_up = lax.psum_scatter(gate_up, "dp", scatter_dimension=0, tiled=True)
     d_attn = [dot_plain(a, out_t).astype(BF) for a in held_a]
     t_q, t_k, d_value, sums, head_gains = attention_backward(
@@ -513,11 +510,17 @@
     grad_gate = grad_gate_up[:, :units].astype(F32)
     grad_up = grad_gate_up[:, units:].astype(F32)
 
-    post = lax.psum(jnp.stack([grad_gain_a, grad_gain_m]), "mp")
+    post = sum_all(jnp.stack([grad_gain_a, grad_gain_m]))
     post = post.reshape(2, groups, own_cols).transpose(1, 0, 2).reshape(groups, 2 * own_cols)
     own = head_gains.transpose(1, 0, 2).reshape(2, heads, groups, slice_q)
     own = own.transpose(2, 0, 1, 3).reshape(groups, 2 * count)
-    totals = lax.psum(jnp.concatenate([own, post], axis=1), "dp")
+    totals = jnp.concatenate([own, post], axis=1)
+    if groups & (groups - 1):
+        totals = lax.psum(totals, "dp")
+    else:
+        for k in range(groups.bit_length() - 1):
+            pairs = [(i, i ^ (1 << k)) for i in range(groups)]
+            totals = totals + lax.ppermute(totals, "dp", pairs)
     mine = lax.dynamic_index_in_dim(totals, lax.axis_index("dp"), 0, keepdims=False)
     return (
         output,

time: 832 us -> 789 us (0.948)
  blocking collectives: 58 us -> 8.84 us
  matrix products: 201 us -> 212 us
  Pallas kernels: 53.2 us -> 42.6 us
  waiting for transfers between devices: 426 us -> 417 us
    psum x2 -> x0, blocking collectives: 49.1 us -> none  [the longest x1 26 us: local(): post = lax.psum(jnp.stack([grad_gain_a, grad_gain_m]), 'mp')]
    pallas_call x1, Pallas kernels: 26.5 us -> 15.7 us  [attention_backward(): pl.pallas_call(functools.partial(backward_kernel, n, rows), grid_spec=plt...]
  transfers between devices with their start and end apart: 37 -> 42, of which waited for: 24 -> 22; matrix products, arithmetic and copies ran while one was open for 26% -> 29% of each run, Pallas kernels for 6% -> 5%
where the time goes in v2:
time: 789 us; the launch traced here: 780 us
  waiting for transfers between devices  417 us (53%)
  matrix products  212 us (27%)
  Pallas kernels  42.6 us (5%)
  other arithmetic  31.4 us (4%)
  starting transfers between devices  29.2 us (4%)
  local copies, waits for them, and re-layouts  22.2 us (3%)
  between operations  16.3 us (2%)
  blocking collectives  8.84 us (1%)
    ppermute x24, waiting for transfers between devices, shift(): return lax.ppermute(value, 'mp', ring)  417 us
    dot_general x20, matrix products, dot_right_t(): lax.dot_general(left, right, (((1,), (1,)), ((), ())), preferred_element_...  93.6 us
    dot_general x20, matrix products, dot_plain(): return jnp.dot(left, right, preferred_element_type=F32)  80.4 us
    dot_general x2, matrix products, dot_left_t(): lax.dot_general(left, right, (((0,), (0,)), ((), ())), preferred_element_...  38.1 us
    unnamed x221, local copies, waits for them, and re-layouts  16.6 us
  transfers between devices with their start and end apart: 42, of which 22 were waited for; matrix products, arithmetic and copies ran while one was open for 29% of the time, Pallas kernels for 5%

profile of v2, /device:TPU:0, one launch (start us, length us, event | category | flops | bytes accessed | tf_op | source)
XLA Modules:
  0.0 780.1 jit_solution(13080580389699405453)
XLA Ops:
  16.6 25.2 %collective-permute-done.refs_1_ = bf16[256,2048]{1,0:T(8,128)(2,1)S(1)} collective-permute-done((bf16[256,2048]{1,0:T(8,128)(2,1)S(1)}, bf16[256,2048]{1,0:T(8,128)(2,1)S(1)}, u32[]{:S(2)}, u32[]{:S(2)}) %collective-permute-start) | collective-permute-done | bytes 1048608 | tf_op jit(solution)/shard_map/ppermute | solution.py:331
  41.7 26.1 %collective-permute-done.1.refs_2_ = bf16[256,2048]{1,0:T(8,128)(2,1)S(1)} collective-permute-done((bf16[256,2048]{1,0:T(8,128)(2,1)S(1)}, bf16[256,2048]{1,0:T(8,128)(2,1)S(1)}, u32[]{:S(2)}, u32[]{:S(2)}) %collective-permute-start.1) | collective-permute-done | bytes 1048608 | tf_op jit(solution)/shard_map/ppermute | solution.py:331
  68.2 8.8 %all-gather.1 = bf16[8,1,640]{2,1,0:T(2,128)(2,1)S(1)} all-gather(bf16[1,1,640]{2,1,0:T(2,128)(2,1)S(1)} %reshape.219), channel_id=2, replica_groups=mesh['dp'=8,'mp'=4] {'dp'}, dimensions={0}, use_global_device_ids=true | all-gather | bytes 11520 | tf_op jit(solution)/shard_map/all_gather | solution.py:377
  80.3 13.0 %collective-permute-done.2.refs_3_ = bf16[256,2048]{1,0:T(8,128)(2,1)} collective-permute-done((bf16[256,2048]{1,0:T(8,128)(2,1)S(1)}, bf16[256,2048]{1,0:T(8,128)(2,1)}, u32[]{:S(2)}, u32[]{:S(2)}) %collective-permute-start.2) | collective-permute-done | bytes 1048608 | tf_op jit(solution)/shard_map/ppermute | solution.py:331
  113.1 13.8 %attention_forward.1 = (bf16[1024,512]{1,0:T(8,128)(2,1)S(1)}, bf16[1024,512]{1,0:T(8,128)(2,1)S(1)}, bf16[1024,512]{1,0:T(8,128)(2,1)S(1)}, bf16[1024,512]{1,0:T(8,128)(2,1)}, f32[4,1,1024]{2,1,0:T(1,128)S(1)}) custom-call(s32[1]{0:T(128)} %bitcast.me_ref, f32[256,1536]{1,0:T(8,128)} %copy-done.27, f32[256,1536]{1,0:T(8,128)} %copy-done.26, ...), custom_call_target="tpu_custom_call" | custom-call | flops 1073741824 | bytes 11534336 | tf_op jit(solution)/shard_map/attention_forward/pallas_call | solution.py:167
  129.6 23.0 %collective-permute-done.6 = bf16[256,2048]{1,0:T(8,128)(2,1)S(1)} collective-permute-done((bf16[256,2048]{1,0:T(8,128)(2,1)S(1)}, bf16[256,2048]{1,0:T(8,128)(2,1)S(1)}, u32[]{:S(2)}, u32[]{:S(2)}) %collective-permute-start.6) | collective-permute-done | bytes 1048608 | tf_op jit(solution)/shard_map/ppermute | solution.py:331
  154.3 22.9 %collective-permute-done.7 = bf16[256,2048]{1,0:T(8,128)(2,1)S(1)} collective-permute-done((bf16[256,2048]{1,0:T(8,128)(2,1)S(1)}, bf16[256,2048]{1,0:T(8,128)(2,1)S(1)}, u32[]{:S(2)}, u32[]{:S(2)}) %collective-permute-start.7) | collective-permute-done | bytes 1048608 | tf_op jit(solution)/shard_map/ppermute | solution.py:331
  178.3 22.0 %collective-permute-done.8 = bf16[256,2048]{1,0:T(8,128)(2,1)S(1)} collective-permute-done((bf16[256,2048]{1,0:T(8,128)(2,1)S(1)}, bf16[256,2048]{1,0:T(8,128)(2,1)S(1)}, u32[]{:S(2)}, u32[]{:S(2)}) %collective-permute-start.8) | collective-permute-done | bytes 1048608 | tf_op jit(solution)/shard_map/ppermute | solution.py:331
  202.0 23.3 %collective-permute-done.9 = bf16[256,2048]{1,0:T(8,128)(2,1)S(1)} collective-permute-done((bf16[256,2048]{1,0:T(8,128)(2,1)S(1)}, bf16[256,2048]{1,0:T(8,128)(2,1)S(1)}, u32[]{:S(2)}, u32[]{:S(2)}) %collective-permute-start.9) | collective-permute-done | bytes 1048608 | tf_op jit(solution)/shard_map/ppermute | solution.py:331
  226.3 22.1 %collective-permute-done.10 = bf16[256,2048]{1,0:T(8,128)(2,1)} collective-permute-done((bf16[256,2048]{1,0:T(8,128)(2,1)S(1)}, bf16[256,2048]{1,0:T(8,128)(2,1)}, u32[]{:S(2)}, u32[]{:S(2)}) %collective-permute-start.10) | collective-permute-done | bytes 1048608 | tf_op jit(solution)/shard_map/ppermute | solution.py:331
  255.9 7.8 multiply_convert_fusion.9
  270.3 6.4 fusion.69
  302.9 16.5 %collective-permute-done.13 = bf16[256,2048]{1,0:T(8,128)(2,1)S(1)} collective-permute-done((bf16[256,2048]{1,0:T(8,128)(2,1)S(1)}, bf16[256,2048]{1,0:T(8,128)(2,1)S(1)}, u32[]{:S(2)}, u32[]{:S(2)}) %collective-permute-start.13) | collective-permute-done | bytes 1048608 | tf_op jit(solution)/shard_map/ppermute | solution.py:331
  327.1 10.7 %collective-permute-done.14 = bf16[256,2048]{1,0:T(8,128)(2,1)S(1)} collective-permute-done((bf16[256,2048]{1,0:T(8,128)(2,1)S(1)}, bf16[256,2048]{1,0:T(8,128)(2,1)S(1)}, u32[]{:S(2)}, u32[]{:S(2)}) %collective-permute-start.14) | collective-permute-done | bytes 1048608 | tf_op jit(solution)/shard_map/ppermute | solution.py:331
  345.4 22.4 %collective-permute-done.15 = bf16[256,2048]{1,0:T(8,128)(2,1)S(1)} collective-permute-done((bf16[256,2048]{1,0:T(8,128)(2,1)S(1)}, bf16[256,2048]{1,0:T(8,128)(2,1)S(1)}, u32[]{:S(2)}, u32[]{:S(2)}) %collective-permute-start.15) | collective-permute-done | bytes 1048608 | tf_op jit(solution)/shard_map/ppermute | solution.py:331
  369.6 22.3 %collective-permute-done.16 = bf16[256,2048]{1,0:T(8,128)(2,1)S(1)} collective-permute-done((bf16[256,2048]{1,0:T(8,128)(2,1)S(1)}, bf16[256,2048]{1,0:T(8,128)(2,1)S(1)}, u32[]{:S(2)}, u32[]{:S(2)}) %collective-permute-start.16) | collective-permute-done | bytes 1048608 | tf_op jit(solution)/shard_map/ppermute | solution.py:331
  394.9 13.8 %collective-permute-done.17 = bf16[256,2048]{1,0:T(8,128)(2,1)S(1)} collective-permute-done((bf16[256,2048]{1,0:T(8,128)(2,1)S(1)}, bf16[256,2048]{1,0:T(8,128)(2,1)S(1)}, u32[]{:S(2)}, u32[]{:S(2)}) %collective-permute-start.17) | collective-permute-done | bytes 1048608 | tf_op jit(solution)/shard_map/ppermute | solution.py:331
  409.7 11.1 %convolution_convert_fusion.1 = bf16[2048,2048]{1,0:T(8,128)(2,1)} fusion(bf16[256,2048]{1,0:T(8,128)(2,1)S(1)} %copy-done.85, bf16[256,2048]{1,0:T(8,128)(2,1)S(1)} %copy-done.86, bf16[256,2048]{1,0:T(8,128)(2,1)S(1)} %copy-done.90, bf16[256,2048]{1,0:T(8,128)(2,1)S(1)} %get-tuple-element.154, bf16[256,2048]{1,0:T(8,128)(2,1)S(1)} %collective-permute-done.17, ...), kind=kOutput, calls=%fused_computation.16 | convolution fusion | flops 8627683328 | bytes 16777216 | tf_op jit(solution)/shard_map/dot_general | solution.py:31
  421.2 9.3 %multiply_convert_fusion.7 = (bf16[256,2048]{1,0:T(8,128)(2,1)}, bf16[256,2048]{1,0:T(8,128)(2,1)}) fusion(f32[256,2048]{1,0:T(8,128)} %fusion.73, f32[256,2048]{1,0:T(8,128)} %get-tuple-element.155, bf16[256,2048]{1,0:T(8,128)(2,1)} %copy-done.42, bf16[2048,2048]{1,0:T(8,128)(2,1)} %all-gather.10.cloned.1.call-done), kind=kOutput, calls=%fused_computation.74 | convolution fusion | flops 2154299392 | bytes 15728640 | tf_op jit(solution)/shard_map/dot_general | solution.py:27
  430.5 9.1 %multiply_convert_fusion.1 = (bf16[256,2048]{1,0:T(8,128)(2,1)}, bf16[256,2048]{1,0:T(8,128)(2,1)}) fusion(f32[256,2048]{1,0:T(8,128)S(1)} %copy-done.76, f32[256,2048]{1,0:T(8,128)S(1)} %copy-done.87, bf16[256,2048]{1,0:T(8,128)(2,1)S(1)} %copy-done.67, bf16[2048,2048]{1,0:T(8,128)(2,1)} %all-gather.10.cloned.1.call-done), kind=kOutput, calls=%fused_computation.68 | convolution fusion | flops 2154299392 | bytes 15728640 | tf_op jit(solution)/shard_map/dot_general | solution.py:27
  448.8 26.9 %convolution_convert_fusion = bf16[2048,4096]{1,0:T(8,128)(2,1)} fusion(bf16[256,2048]{1,0:T(8,128)(2,1)} %get-tuple-element.103, bf16[256,2048]{1,0:T(8,128)(2,1)} %get-tuple-element.101, bf16[256,2048]{1,0:T(8,128)(2,1)} %get-tuple-element.99, bf16[256,2048]{1,0:T(8,128)(2,1)} %get-tuple-element.105, bf16[256,2048]{1,0:T(8,128)(2,1)} %get-tuple-element.104, ...), kind=kOutput, calls=%fused_computation | convolution fusion | flops 17272143872 | bytes 29360128 | tf_op jit(solution)/shard_map/dot_general | solution.py:31
  497.8 18.2 %collective-permute-done.18 = bf16[256,2048]{1,0:T(8,128)(2,1)S(1)} collective-permute-done((bf16[256,2048]{1,0:T(8,128)(2,1)S(1)}, bf16[256,2048]{1,0:T(8,128)(2,1)S(1)}, u32[]{:S(2)}, u32[]{:S(2)}) %collective-permute-start.18) | collective-permute-done | bytes 1048608 | tf_op jit(solution)/shard_map/ppermute | solution.py:331
  524.5 19.3 %collective-permute-done.19 = bf16[256,2048]{1,0:T(8,128)(2,1)S(1)} collective-permute-done((bf16[256,2048]{1,0:T(8,128)(2,1)S(1)}, bf16[256,2048]{1,0:T(8,128)(2,1)S(1)}, u32[]{:S(2)}, u32[]{:S(2)}) %collective-permute-start.19) | collective-permute-done | bytes 1048608 | tf_op jit(solution)/shard_map/ppermute | solution.py:331
  556.6 15.2 %collective-permute-done.20 = bf16[256,2048]{1,0:T(8,128)(2,1)S(1)} collective-permute-done((bf16[256,2048]{1,0:T(8,128)(2,1)S(1)}, bf16[256,2048]{1,0:T(8,128)(2,1)S(1)}, u32[]{:S(2)}, u32[]{:S(2)}) %collective-permute-start.20) | collective-permute-done | bytes 1048608 | tf_op jit(solution)/shard_map/ppermute | solution.py:331
  574.0 25.8 %collective-permute-done.21.refs_9_ = bf16[256,2048]{1,0:T(8,128)(2,1)S(1)} collective-permute-done((bf16[256,2048]{1,0:T(8,128)(2,1)S(1)}, bf16[256,2048]{1,0:T(8,128)(2,1)S(1)}, u32[]{:S(2)}, u32[]{:S(2)}) %collective-permute-start.21) | collective-permute-done | bytes 1048608 | tf_op jit(solution)/shard_map/ppermute | solution.py:331
  600.8 24.3 %collective-permute-done.22.refs_10_ = bf16[256,2048]{1,0:T(8,128)(2,1)} collective-permute-done((bf16[256,2048]{1,0:T(8,128)(2,1)S(1)}, bf16[256,2048]{1,0:T(8,128)(2,1)}, u32[]{:S(2)}, u32[]{:S(2)}) %collective-permute-start.22) | collective-permute-done | bytes 1048608 | tf_op jit(solution)/shard_map/ppermute | solution.py:331
  632.5 9.4 %collective-permute-done.23.refs_11_ = bf16[256,2048]{1,0:T(8,128)(2,1)S(1)} collective-permute-done((bf16[256,2048]{1,0:T(8,128)(2,1)}, bf16[256,2048]{1,0:T(8,128)(2,1)S(1)}, u32[]{:S(2)}, u32[]{:S(2)}) %collective-permute-start.23) | collective-permute-done | bytes 1048608 | tf_op jit(solution)/shard_map/ppermute | solution.py:331
  644.7 15.7 %attention_backward.1 = (f32[1024,512]{1,0:T(8,128)}, f32[1024,512]{1,0:T(8,128)}, bf16[1024,512]{1,0:T(8,128)(2,1)S(1)}, f32[2,1,1024]{2,1,0:T(1,128)S(1)}, f32[4,2,128]{2,1,0:T(2,128)S(1)}) custom-call(s32[1]{0:T(128)} %bitcast.me_ref, f32[256,1536]{1,0:T(8,128)} %copy-done.27, f32[256,1536]{1,0:T(8,128)} %copy-done.26, f32[256,1536]{1,0:T(8,128)} %copy-done.25, ...), custom_call_target="tpu_custom_call" | custom-call | flops 2684354560 | bytes 13631488 | tf_op jit(solution)/shard_map/attention_backward/pallas_call | solution.py:211
  675.9 13.1 %attention_weights.1 = bf16[2048,2048]{1,0:T(8,128)(2,1)} custom-call(bf16[256,2048]{1,0:T(8,128)(2,1)S(1)} %copy-done.4, bf16[256,2048]{1,0:T(8,128)(2,1)S(1)} %copy-done.16, bf16[256,2048]{1,0:T(8,128)(2,1)S(1)} %copy-done.18, bf16[256,2048]{1,0:T(8,128)(2,1)} %collective-permute-done.2.refs_3_, bf16[256,1536]{1,0:T(8,128)(2,1)S(1)} %pad_maximum_fusion.2.refs_4_, ...), custom_call_target="tpu_custom_call" | custom-call | flops 8589934592 | bytes 20971520 | tf_op jit(solution)/shard_map/attention_weights/pallas_call | solution.py:286
  700.8 21.6 %collective-permute-done.27 = bf16[256,2048]{1,0:T(8,128)(2,1)S(1)} collective-permute-done((bf16[256,2048]{1,0:T(8,128)(2,1)S(1)}, bf16[256,2048]{1,0:T(8,128)(2,1)S(1)}, u32[]{:S(2)}, u32[]{:S(2)}) %collective-permute-start.27) | collective-permute-done | bytes 1048608 | tf_op jit(solution)/shard_map/ppermute | solution.py:331
  735.0 13.5 %collective-permute-done.28 = bf16[256,2048]{1,0:T(8,128)(2,1)S(1)} collective-permute-done((bf16[256,2048]{1,0:T(8,128)(2,1)}, bf16[256,2048]{1,0:T(8,128)(2,1)S(1)}, u32[]{:S(2)}, u32[]{:S(2)}) %collective-permute-start.28) | collective-permute-done | bytes 1048608 | tf_op jit(solution)/shard_map/ppermute | solution.py:331
  760.8 6.7 collective-permute-done.29
  (420 shorter events, 224.4 us)
Async XLA Ops:
  7.2 86.0 %all-gather.6.cloned.1.call-start = ((), (), s32[]{:S(2)}) async-start(), calls=%async_computation.3 | async-start | bytes 9437184 | tf_op jit(solution)/shard_map/all_gather | solution.py:366
  10.7 237.7 %all-gather.8.cloned.1.call-start = ((), (), s32[]{:S(2)}) async-start(), calls=%async_computation.4 | async-start | bytes 18874368 | tf_op jit(solution)/shard_map/all_gather | solution.py:389
  12.3 251.3 %all-gather.10.cloned.1.call-start = ((), (), s32[]{:S(2)}) async-start(), calls=%async_computation.5 | async-start | bytes 9437184 | tf_op jit(solution)/shard_map/all_gather | solution.py:393
  13.5 28.2 %collective-permute-start = (bf16[256,2048]{1,0:T(8,128)(2,1)S(1)}, bf16[256,2048]{1,0:T(8,128)(2,1)S(1)}, u32[]{:S(2)}, u32[]{:S(2)}) collective-permute-start(bf16[256,2048]{1,0:T(8,128)(2,1)S(1)} %copy-done.4), channel_id=1, source_target_pairs={{0,1},{1,2},{2,3},{3,0},{4,5},{5,6},{6,7},{7,4},{8,9},{9,10},{10,1... | collective-permute-start | bytes 3145736 | tf_op jit(solution)/shard_map/ppermute | solution.py:331
  41.7 26.1 %collective-permute-start.1 = (bf16[256,2048]{1,0:T(8,128)(2,1)S(1)}, bf16[256,2048]{1,0:T(8,128)(2,1)S(1)}, u32[]{:S(2)}, u32[]{:S(2)}) collective-permute-start(bf16[256,2048]{1,0:T(8,128)(2,1)S(1)} %collective-permute-done.refs_1_), channel_id=1, source_target_pairs={{0,1},{1,2},{2,3},{3,0},{4,5},{5,6},{6,7},{7,4},{8,9},{9,10},{10,1... | collective-permute-start | bytes 3145736 | tf_op jit(solution)/shard_map/ppermute | solution.py:331
  67.9 25.4 %collective-permute-start.2 = (bf16[256,2048]{1,0:T(8,128)(2,1)S(1)}, bf16[256,2048]{1,0:T(8,128)(2,1)}, u32[]{:S(2)}, u32[]{:S(2)}) collective-permute-start(bf16[256,2048]{1,0:T(8,128)(2,1)S(1)} %collective-permute-done.1.refs_2_), channel_id=1, source_target_pairs={{0,1},{1,2},{2,3},{3,0},{4,5},{5,6},{6,7},{7,4},{8,9},{9,10},{10,1... | collective-permute-start | bytes 3145736 | tf_op jit(solution)/shard_map/ppermute | solution.py:331
  67.9 557.2 %reduce-scatter.4.cloned.1.call-start = ((), (), s32[]{:S(2)}) async-start(), calls=%async_computation.6 | async-start | bytes 9437184 | tf_op jit(solution)/shard_map/reduce_scatter | solution.py:456
  127.8 24.8 %collective-permute-start.6 = (bf16[256,2048]{1,0:T(8,128)(2,1)S(1)}, bf16[256,2048]{1,0:T(8,128)(2,1)S(1)}, u32[]{:S(2)}, u32[]{:S(2)}) collective-permute-start(bf16[256,2048]{1,0:T(8,128)(2,1)S(1)} %convolution_convert_fusion.2), channel_id=1, source_target_pairs={{0,1},{1,2},{2,3},{3,0},{4,5},{5,6},{6,7},{7,4},{8,9},{9,10},{10,1... | collective-permute-start | bytes 3145736 | tf_op jit(solution)/shard_map/ppermute | solution.py:331
  153.4 23.7 %collective-permute-start.7 = (bf16[256,2048]{1,0:T(8,128)(2,1)S(1)}, bf16[256,2048]{1,0:T(8,128)(2,1)S(1)}, u32[]{:S(2)}, u32[]{:S(2)}) collective-permute-start(bf16[256,2048]{1,0:T(8,128)(2,1)S(1)} %add_convert_fusion.7), channel_id=1, source_target_pairs={{0,1},{1,2},{2,3},{3,0},{4,5},{5,6},{6,7},{7,4},{8,9},{9,10},{10,1... | collective-permute-start | bytes 3145736 | tf_op jit(solution)/shard_map/ppermute | solution.py:331
  177.4 22.8 %collective-permute-start.8 = (bf16[256,2048]{1,0:T(8,128)(2,1)S(1)}, bf16[256,2048]{1,0:T(8,128)(2,1)S(1)}, u32[]{:S(2)}, u32[]{:S(2)}) collective-permute-start(bf16[256,2048]{1,0:T(8,128)(2,1)S(1)} %add_convert_fusion.6), channel_id=1, source_target_pairs={{0,1},{1,2},{2,3},{3,0},{4,5},{5,6},{6,7},{7,4},{8,9},{9,10},{10,1... | collective-permute-start | bytes 3145736 | tf_op jit(solution)/shard_map/ppermute | solution.py:331
  202.0 23.3 %collective-permute-start.9 = (bf16[256,2048]{1,0:T(8,128)(2,1)S(1)}, bf16[256,2048]{1,0:T(8,128)(2,1)S(1)}, u32[]{:S(2)}, u32[]{:S(2)}) collective-permute-start(bf16[256,2048]{1,0:T(8,128)(2,1)S(1)} %fusion.75), channel_id=1, source_target_pairs={{0,1},{1,2},{2,3},{3,0},{4,5},{5,6},{6,7},{7,4},{8,9},{9,10},{10,1... | collective-permute-start | bytes 3145736 | tf_op jit(solution)/shard_map/ppermute | solution.py:331
  225.3 23.1 %collective-permute-start.10 = (bf16[256,2048]{1,0:T(8,128)(2,1)S(1)}, bf16[256,2048]{1,0:T(8,128)(2,1)}, u32[]{:S(2)}, u32[]{:S(2)}) collective-permute-start(bf16[256,2048]{1,0:T(8,128)(2,1)S(1)} %collective-permute-done.9), channel_id=1, source_target_pairs={{0,1},{1,2},{2,3},{3,0},{4,5},{5,6},{6,7},{7,4},{8,9},{9,10},{10,1... | collective-permute-start | bytes 3145736 | tf_op jit(solution)/shard_map/ppermute | solution.py:331
  248.5 28.3 %collective-permute-start.11 = (bf16[256,2048]{1,0:T(8,128)(2,1)}, bf16[256,2048]{1,0:T(8,128)(2,1)}, u32[]{:S(2)}, u32[]{:S(2)}) collective-permute-start(bf16[256,2048]{1,0:T(8,128)(2,1)} %collective-permute-done.10), channel_id=1, source_target_pairs={{0,1},{1,2},{2,3},{3,0},{4,5},{5,6},{6,7},{7,4},{8,9},{9,10},{10,1... | collective-permute-start | bytes 3145736 | tf_op jit(solution)/shard_map/ppermute | solution.py:331
  269.9 22.9 %collective-permute-start.12 = (bf16[256,2048]{1,0:T(8,128)(2,1)S(1)}, bf16[256,2048]{1,0:T(8,128)(2,1)S(1)}, u32[]{:S(2)}, u32[]{:S(2)}) collective-permute-start(bf16[256,2048]{1,0:T(8,128)(2,1)S(1)} %convolution_convert_fusion.4), channel_id=1, source_target_pairs={{0,1},{1,2},{2,3},{3,0},{4,5},{5,6},{6,7},{7,4},{8,9},{9,10},{10,1... | collective-permute-start | bytes 3145736 | tf_op jit(solution)/shard_map/ppermute | solution.py:331
  296.5 22.9 %collective-permute-start.13 = (bf16[256,2048]{1,0:T(8,128)(2,1)S(1)}, bf16[256,2048]{1,0:T(8,128)(2,1)S(1)}, u32[]{:S(2)}, u32[]{:S(2)}) collective-permute-start(bf16[256,2048]{1,0:T(8,128)(2,1)S(1)} %add_convert_fusion.5), channel_id=1, source_target_pairs={{0,1},{1,2},{2,3},{3,0},{4,5},{5,6},{6,7},{7,4},{8,9},{9,10},{10,1... | collective-permute-start | bytes 3145736 | tf_op jit(solution)/shard_map/ppermute | solution.py:331
  319.7 18.1 %collective-permute-start.14 = (bf16[256,2048]{1,0:T(8,128)(2,1)S(1)}, bf16[256,2048]{1,0:T(8,128)(2,1)S(1)}, u32[]{:S(2)}, u32[]{:S(2)}) collective-permute-start(bf16[256,2048]{1,0:T(8,128)(2,1)S(1)} %add_convert_fusion.4), channel_id=1, source_target_pairs={{0,1},{1,2},{2,3},{3,0},{4,5},{5,6},{6,7},{7,4},{8,9},{9,10},{10,1... | collective-permute-start | bytes 3145736 | tf_op jit(solution)/shard_map/ppermute | solution.py:331
  344.5 23.3 %collective-permute-start.15 = (bf16[256,2048]{1,0:T(8,128)(2,1)S(1)}, bf16[256,2048]{1,0:T(8,128)(2,1)S(1)}, u32[]{:S(2)}, u32[]{:S(2)}) collective-permute-start(bf16[256,2048]{1,0:T(8,128)(2,1)S(1)} %get-tuple-element.107), channel_id=1, source_target_pairs={{0,1},{1,2},{2,3},{3,0},{4,5},{5,6},{6,7},{7,4},{8,9},{9,10},{10,1... | collective-permute-start | bytes 3145736 | tf_op jit(solution)/shard_map/ppermute | solution.py:331
  367.8 24.0 %collective-permute-start.16 = (bf16[256,2048]{1,0:T(8,128)(2,1)S(1)}, bf16[256,2048]{1,0:T(8,128)(2,1)S(1)}, u32[]{:S(2)}, u32[]{:S(2)}) collective-permute-start(bf16[256,2048]{1,0:T(8,128)(2,1)S(1)} %collective-permute-done.15), channel_id=1, source_target_pairs={{0,1},{1,2},{2,3},{3,0},{4,5},{5,6},{6,7},{7,4},{8,9},{9,10},{10,1... | collective-permute-start | bytes 3145736 | tf_op jit(solution)/shard_map/ppermute | solution.py:331
  420.9 328.9 %reduce-scatter.8.cloned.1.call-start = ((), (), s32[]{:S(2)}) async-start(), calls=%async_computation.8 | async-start | bytes 18874368 | tf_op jit(solution)/shard_map/reduce_scatter | solution.py:469
  475.7 293.7 %reduce-scatter.6.cloned.1.call-start = ((), (), s32[]{:S(2)}) async-start(), calls=%async_computation.7 | async-start | bytes 9437184 | tf_op jit(solution)/shard_map/reduce_scatter | solution.py:500
  488.5 27.5 %collective-permute-start.18 = (bf16[256,2048]{1,0:T(8,128)(2,1)S(1)}, bf16[256,2048]{1,0:T(8,128)(2,1)S(1)}, u32[]{:S(2)}, u32[]{:S(2)}) collective-permute-start(bf16[256,2048]{1,0:T(8,128)(2,1)S(1)} %fusion.36), channel_id=1, source_target_pairs={{0,1},{1,2},{2,3},{3,0},{4,5},{5,6},{6,7},{7,4},{8,9},{9,10},{10,1... | collective-permute-start | bytes 3145736 | tf_op jit(solution)/shard_map/ppermute | solution.py:331
  516.3 27.5 %collective-permute-start.19 = (bf16[256,2048]{1,0:T(8,128)(2,1)S(1)}, bf16[256,2048]{1,0:T(8,128)(2,1)S(1)}, u32[]{:S(2)}, u32[]{:S(2)}) collective-permute-start(bf16[256,2048]{1,0:T(8,128)(2,1)S(1)} %add_convert_fusion.3), channel_id=1, source_target_pairs={{0,1},{1,2},{2,3},{3,0},{4,5},{5,6},{6,7},{7,4},{8,9},{9,10},{10,1... | collective-permute-start | bytes 3145736 | tf_op jit(solution)/shard_map/ppermute | solution.py:331
  544.1 27.8 %collective-permute-start.20 = (bf16[256,2048]{1,0:T(8,128)(2,1)S(1)}, bf16[256,2048]{1,0:T(8,128)(2,1)S(1)}, u32[]{:S(2)}, u32[]{:S(2)}) collective-permute-start(bf16[256,2048]{1,0:T(8,128)(2,1)S(1)} %add_convert_fusion.2), channel_id=1, source_target_pairs={{0,1},{1,2},{2,3},{3,0},{4,5},{5,6},{6,7},{7,4},{8,9},{9,10},{10,1... | collective-permute-start | bytes 3145736 | tf_op jit(solution)/shard_map/ppermute | solution.py:331
  574.0 25.8 %collective-permute-start.21 = (bf16[256,2048]{1,0:T(8,128)(2,1)S(1)}, bf16[256,2048]{1,0:T(8,128)(2,1)S(1)}, u32[]{:S(2)}, u32[]{:S(2)}) collective-permute-start(bf16[256,2048]{1,0:T(8,128)(2,1)S(1)} %multiply_convert_fusion.refs_8_), channel_id=1, source_target_pairs={{0,1},{1,2},{2,3},{3,0},{4,5},{5,6},{6,7},{7,4},{8,9},{9,10},{10,1... | collective-permute-start | bytes 3145736 | tf_op jit(solution)/shard_map/ppermute | solution.py:331
  600.8 24.3 %collective-permute-start.22 = (bf16[256,2048]{1,0:T(8,128)(2,1)S(1)}, bf16[256,2048]{1,0:T(8,128)(2,1)}, u32[]{:S(2)}, u32[]{:S(2)}) collective-permute-start(bf16[256,2048]{1,0:T(8,128)(2,1)S(1)} %collective-permute-done.21.refs_9_), channel_id=1, source_target_pairs={{0,1},{1,2},{2,3},{3,0},{4,5},{5,6},{6,7},{7,4},{8,9},{9,10},{10,1... | collective-permute-start | bytes 3145736 | tf_op jit(solution)/shard_map/ppermute | solution.py:331
  694.8 27.6 %collective-permute-start.27 = (bf16[256,2048]{1,0:T(8,128)(2,1)S(1)}, bf16[256,2048]{1,0:T(8,128)(2,1)S(1)}, u32[]{:S(2)}, u32[]{:S(2)}) collective-permute-start(bf16[256,2048]{1,0:T(8,128)(2,1)S(1)} %convolution_convert_fusion.3), channel_id=1, source_target_pairs={{0,1},{1,2},{2,3},{3,0},{4,5},{5,6},{6,7},{7,4},{8,9},{9,10},{10,1... | collective-permute-start | bytes 3145736 | tf_op jit(solution)/shard_map/ppermute | solution.py:331
  696.0 32.3 %collective-permute-start.31 = (f32[2,2048]{1,0:T(2,128)S(1)}, f32[2,2048]{1,0:T(2,128)S(1)}, u32[]{:S(2)}, u32[]{:S(2)}) collective-permute-start(f32[2,2048]{1,0:T(2,128)S(1)} %pad_maximum_fusion.10), channel_id=1, source_target_pairs={{0,2},{1,3},{2,0},{3,1},{4,6},{5,7},{6,4},{7,5},{8,10},{9,11},{10,... | collective-permute-start | bytes 49160 | tf_op jit(solution)/shard_map/ppermute | solution.py:336
  698.8 29.5 %collective-permute-start.32 = (f32[2,2048]{1,0:T(2,128)S(1)}, f32[2,2048]{1,0:T(2,128)S(1)}, u32[]{:S(2)}, u32[]{:S(2)}) collective-permute-start(f32[2,2048]{1,0:T(2,128)S(1)} %pad_maximum_fusion.10), channel_id=1, source_target_pairs={{0,3},{1,0},{2,1},{3,2},{4,7},{5,4},{6,5},{7,6},{8,11},{9,8},{10,9... | collective-permute-start | bytes 49160 | tf_op jit(solution)/shard_map/ppermute | solution.py:336
  699.0 29.3 %collective-permute-start.30 = (f32[2,2048]{1,0:T(2,128)S(1)}, f32[2,2048]{1,0:T(2,128)S(1)}, u32[]{:S(2)}, u32[]{:S(2)}) collective-permute-start(f32[2,2048]{1,0:T(2,128)S(1)} %pad_maximum_fusion.10), channel_id=1, source_target_pairs={{0,1},{1,2},{2,3},{3,0},{4,5},{5,6},{6,7},{7,4},{8,9},{9,10},{10,1... | collective-permute-start | bytes 49160 | tf_op jit(solution)/shard_map/ppermute | solution.py:336
  728.2 20.2 %collective-permute-start.28 = (bf16[256,2048]{1,0:T(8,128)(2,1)}, bf16[256,2048]{1,0:T(8,128)(2,1)S(1)}, u32[]{:S(2)}, u32[]{:S(2)}) collective-permute-start(bf16[256,2048]{1,0:T(8,128)(2,1)} %add_convert_fusion.1), channel_id=1, source_target_pairs={{0,1},{1,2},{2,3},{3,0},{4,5},{5,6},{6,7},{7,4},{8,9},{9,10},{10,1... | collective-permute-start | bytes 3145736 | tf_op jit(solution)/shard_map/ppermute | solution.py:331
  734.9 21.3 %collective-permute-start.35 = (f32[8,640]{1,0:T(8,128)S(1)}, f32[8,640]{1,0:T(8,128)S(1)}, u32[]{:S(2)}, u32[]{:S(2)}) collective-permute-start(f32[8,640]{1,0:T(8,128)S(1)} %add.205), channel_id=1, source_target_pairs={{0,16},{4,20},{8,24},{12,28},{16,0},{20,4},{24,8},{28,12},{1,17},{... | collective-permute-start | bytes 61448 | tf_op jit(solution)/shard_map/ppermute | solution.py:523
  749.8 17.7 %collective-permute-start.29 = (bf16[256,2048]{1,0:T(8,128)(2,1)}, bf16[256,2048]{1,0:T(8,128)(2,1)S(1)}, u32[]{:S(2)}, u32[]{:S(2)}) collective-permute-start(bf16[256,2048]{1,0:T(8,128)(2,1)} %add_convert_fusion), channel_id=1, source_target_pairs={{0,1},{1,2},{2,3},{3,0},{4,5},{5,6},{6,7},{7,4},{8,9},{9,10},{10,1... | collective-permute-start | bytes 3145736 | tf_op jit(solution)/shard_map/ppermute | solution.py:331
  (115 other events, 1576.4 us)
Sparse Core Ops, SparseCore 0:
  10.8 56.9 all-gather.5
  70.3 89.7 all-gather.7
  161.9 55.8 all-gather.9
  421.0 76.4 reduce-scatter.3
  501.0 116.1 reduce-scatter.7
  689.2 70.9 reduce-scatter.5

commit v3 on v2

--- a/solution.py
+++ b/solution.py
@@ -302,6 +302,34 @@
     )(*held_x, *d_qkv, *held_a, attn)
 
 
+def half_kernel(n, *refs):
+    x_in, d_in, out = refs[:n], refs[n : 2 * n], refs[-1]
+    out[...] = sum(dot_left_t(x_in[s][...], d_in[s][...]) for s in range(n)).astype(BF)
+
+
+def half_weights(held, grads, which, buffer=None):
+    n, (rows, wide) = len(held), grads[0].shape
+    width = held[0].shape[1]
+    tile = min(256, width)
+    step = pl.BlockSpec((rows, tile), lambda i: (0, i))
+    once = pl.BlockSpec((rows, wide), lambda i: (0, 0), pipeline_mode=pl.Buffered(1))
+    rest = () if buffer is None else (buffer,)
+    return pl.pallas_call(
+        functools.partial(half_kernel, n),
+        grid=(width // tile,),
+        in_specs=[step] * n + [once] * n + [pl.BlockSpec(memory_space=pl.ANY)] * len(rest),
+        out_specs=pl.BlockSpec((tile, wide), lambda i: (i, which)),
+        out_shape=jax.ShapeDtypeStruct((width, 2 * wide), BF),
+        input_output_aliases={2 * n: 0} if rest else {},
+        compiler_params=pltpu.CompilerParams(vmem_limit_bytes=40 << 20),
+        cost_estimate=pl.CostEstimate(
+            flops=2 * n * rows * width * wide,
+            bytes_accessed=2 * (width * wide + n * rows * (wide + width)),
+            transcendentals=0,
+        ),
+    )(*held, *grads, *rest)
+
+
 def local(
     n,
     groups,
@@ -386,10 +414,11 @@
     own_cols = attn_gain.shape[0]
     gain_a = small[:, 2 * count : 2 * count + own_cols].reshape(width)
     gain_m = small[:, 2 * count + own_cols :].reshape(width)
-    full_gate_up = lax.all_gather(
-        jnp.concatenate([w_gate, w_up], axis=1), "dp", axis=0, tiled=True
-    )
-    full_gate, full_up = full_gate_up[:, :units], full_gate_up[:, units:]
+    shard_gate_up = jnp.concatenate([w_gate, w_up], axis=1)
+    full_gate_up = lax.all_gather(shard_gate_up, "dp", axis=0, tiled=True)
+    full_gate, full_up = lax.optimization_barrier(
+        (full_gate_up[:, :units], full_gate_up[:, units:])
+    )
     full_down = lax.all_gather(w_down, "dp", axis=1, tiled=True)
     cosine, sine = rope_tables()
 
@@ -454,11 +483,8 @@
         {1: held_m[-1]},
     )
     grad_down = lax.psum_scatter(down, "dp", scatter_dimension=1, tiled=True)
-    d_gate_up = jnp.concatenate(
-        [jnp.concatenate(d_gates, axis=0), jnp.concatenate(d_ups, axis=0)], axis=1
-    )
-    all_r = jnp.concatenate(held_r, axis=0)
-    gate_up = dot_left_t(all_r, d_gate_up).astype(BF)
+    gate_up = half_weights(held_r, d_gates, 0)
+    gate_up = half_weights(held_r, d_ups, 1, gate_up)
 
     grad_gain_a = jnp.sum(d_resid * hat_a, axis=0)
     scaled_a = d_resid * gain_a

time: 789 us -> 786 us (level)
  matrix products: 212 us -> 169 us
  Pallas kernels: 42.6 us -> 68.8 us
  waiting for transfers between devices: 417 us -> 429 us
  local copies, waits for them, and re-layouts: 22.2 us -> 32.8 us
  starting transfers between devices: 29.2 us -> 21.2 us
    dot_general x2 -> x1, matrix products: 38.1 us -> 11.2 us  [dot_left_t(): lax.dot_general(left, right, (((0,), (0,)), ((), ())), preferred_element_...]
    pallas_call x0 -> x2, Pallas kernels: none -> 26.1 us  [half_weights(): pl.pallas_call(functools.partial(half_kernel, n), grid=(width // tile,),...]
    dot_general x20, matrix products: 80.4 us -> 65.9 us  [dot_plain(): return jnp.dot(left, right, preferred_element_type=F32)]
    ppermute x24, waiting for transfers between devices: 417 us -> 429 us  [shift(): return lax.ppermute(value, 'mp', ring)]
    unnamed x221 -> x227, local copies, waits for them, and re-layouts: 16.6 us -> 20.2 us
  transfers between devices with their start and end apart: 42 -> 42, of which waited for: 22 -> 23; matrix products, arithmetic and copies ran while one was open for 29% -> 24% of each run, Pallas kernels for 5% -> 9%
where the time goes in v3:
time: 786 us; the launch traced here: 777 us
  waiting for transfers between devices  429 us (55%)
  matrix products  169 us (22%)
  Pallas kernels  68.8 us (9%)
  local copies, waits for them, and re-layouts  32.8 us (4%)
  other arithmetic  30.9 us (4%)
  starting transfers between devices  21.2 us (3%)
  between operations  16.5 us (2%)
  blocking collectives  8.84 us (1%)
    ppermute x24, waiting for transfers between devices, shift(): return lax.ppermute(value, 'mp', ring)  429 us
    dot_general x20, matrix products, dot_right_t(): lax.dot_general(left, right, (((1,), (1,)), ((), ())), preferred_element_...  91.5 us
    dot_general x20, matrix products, dot_plain(): return jnp.dot(left, right, preferred_element_type=F32)  65.9 us
    pallas_call x2, Pallas kernels, half_weights(): pl.pallas_call(functools.partial(half_kernel, n), grid=(width // tile,),...  26.1 us
    unnamed x227, local copies, waits for them, and re-layouts  20.2 us
  transfers between devices with their start and end apart: 42, of which 23 were waited for; matrix products, arithmetic and copies ran while one was open for 24% of the time, Pallas kernels for 9%

profile of v3, /device:TPU:0, one launch (start us, length us, event | category | flops | bytes accessed | tf_op | source)
XLA Modules:
  0.0 777.0 jit_solution(14682044603323213295)
XLA Ops:
  16.6 25.2 %collective-permute-done.refs_1_ = bf16[256,2048]{1,0:T(8,128)(2,1)S(1)} collective-permute-done((bf16[256,2048]{1,0:T(8,128)(2,1)S(1)}, bf16[256,2048]{1,0:T(8,128)(2,1)S(1)}, u32[]{:S(2)}, u32[]{:S(2)}) %collective-permute-start) | collective-permute-done | bytes 1048608 | tf_op jit(solution)/shard_map/ppermute | solution.py:359
  41.7 26.1 %collective-permute-done.1.refs_2_ = bf16[256,2048]{1,0:T(8,128)(2,1)S(1)} collective-permute-done((bf16[256,2048]{1,0:T(8,128)(2,1)S(1)}, bf16[256,2048]{1,0:T(8,128)(2,1)S(1)}, u32[]{:S(2)}, u32[]{:S(2)}) %collective-permute-start.1) | collective-permute-done | bytes 1048608 | tf_op jit(solution)/shard_map/ppermute | solution.py:359
  68.2 8.8 %all-gather.1 = bf16[8,1,640]{2,1,0:T(2,128)(2,1)S(1)} all-gather(bf16[1,1,640]{2,1,0:T(2,128)(2,1)S(1)} %reshape.219), channel_id=2, replica_groups=mesh['dp'=8,'mp'=4] {'dp'}, dimensions={0}, use_global_device_ids=true | all-gather | bytes 11520 | tf_op jit(solution)/shard_map/all_gather | solution.py:405
  80.3 13.0 %collective-permute-done.2.refs_3_ = bf16[256,2048]{1,0:T(8,128)(2,1)} collective-permute-done((bf16[256,2048]{1,0:T(8,128)(2,1)S(1)}, bf16[256,2048]{1,0:T(8,128)(2,1)}, u32[]{:S(2)}, u32[]{:S(2)}) %collective-permute-start.2) | collective-permute-done | bytes 1048608 | tf_op jit(solution)/shard_map/ppermute | solution.py:359
  113.1 13.8 %attention_forward.1 = (bf16[1024,512]{1,0:T(8,128)(2,1)S(1)}, bf16[1024,512]{1,0:T(8,128)(2,1)S(1)}, bf16[1024,512]{1,0:T(8,128)(2,1)S(1)}, bf16[1024,512]{1,0:T(8,128)(2,1)}, f32[4,1,1024]{2,1,0:T(1,128)S(1)}) custom-call(s32[1]{0:T(128)} %bitcast.me_ref, f32[256,1536]{1,0:T(8,128)} %copy-done.45, f32[256,1536]{1,0:T(8,128)} %copy-done.44, ...), custom_call_target="tpu_custom_call" | custom-call | flops 1073741824 | bytes 11534336 | tf_op jit(solution)/shard_map/attention_forward/pallas_call | solution.py:167
  129.6 23.0 %collective-permute-done.6 = bf16[256,2048]{1,0:T(8,128)(2,1)S(1)} collective-permute-done((bf16[256,2048]{1,0:T(8,128)(2,1)S(1)}, bf16[256,2048]{1,0:T(8,128)(2,1)S(1)}, u32[]{:S(2)}, u32[]{:S(2)}) %collective-permute-start.6) | collective-permute-done | bytes 1048608 | tf_op jit(solution)/shard_map/ppermute | solution.py:359
  154.3 22.9 %collective-permute-done.7 = bf16[256,2048]{1,0:T(8,128)(2,1)S(1)} collective-permute-done((bf16[256,2048]{1,0:T(8,128)(2,1)S(1)}, bf16[256,2048]{1,0:T(8,128)(2,1)S(1)}, u32[]{:S(2)}, u32[]{:S(2)}) %collective-permute-start.7) | collective-permute-done | bytes 1048608 | tf_op jit(solution)/shard_map/ppermute | solution.py:359
  178.3 22.0 %collective-permute-done.8 = bf16[256,2048]{1,0:T(8,128)(2,1)S(1)} collective-permute-done((bf16[256,2048]{1,0:T(8,128)(2,1)S(1)}, bf16[256,2048]{1,0:T(8,128)(2,1)S(1)}, u32[]{:S(2)}, u32[]{:S(2)}) %collective-permute-start.8) | collective-permute-done | bytes 1048608 | tf_op jit(solution)/shard_map/ppermute | solution.py:359
  202.1 22.4 %collective-permute-done.9.refs_1_ = bf16[256,2048]{1,0:T(8,128)(2,1)S(1)} collective-permute-done((bf16[256,2048]{1,0:T(8,128)(2,1)S(1)}, bf16[256,2048]{1,0:T(8,128)(2,1)S(1)}, u32[]{:S(2)}, u32[]{:S(2)}) %collective-permute-start.9) | collective-permute-done | bytes 1048608 | tf_op jit(solution)/shard_map/ppermute | solution.py:359
  225.4 23.1 %collective-permute-done.10.refs_2_ = bf16[256,2048]{1,0:T(8,128)(2,1)} collective-permute-done((bf16[256,2048]{1,0:T(8,128)(2,1)S(1)}, bf16[256,2048]{1,0:T(8,128)(2,1)}, u32[]{:S(2)}, u32[]{:S(2)}) %collective-permute-start.10) | collective-permute-done | bytes 1048608 | tf_op jit(solution)/shard_map/ppermute | solution.py:359
  248.5 7.0 fusion.62
  304.6 15.3 %collective-permute-done.13 = bf16[256,2048]{1,0:T(8,128)(2,1)S(1)} collective-permute-done((bf16[256,2048]{1,0:T(8,128)(2,1)S(1)}, bf16[256,2048]{1,0:T(8,128)(2,1)S(1)}, u32[]{:S(2)}, u32[]{:S(2)}) %collective-permute-start.13) | collective-permute-done | bytes 1048608 | tf_op jit(solution)/shard_map/ppermute | solution.py:359
  326.7 10.6 %collective-permute-done.14 = bf16[256,2048]{1,0:T(8,128)(2,1)S(1)} collective-permute-done((bf16[256,2048]{1,0:T(8,128)(2,1)S(1)}, bf16[256,2048]{1,0:T(8,128)(2,1)S(1)}, u32[]{:S(2)}, u32[]{:S(2)}) %collective-permute-start.14) | collective-permute-done | bytes 1048608 | tf_op jit(solution)/shard_map/ppermute | solution.py:359
  344.1 25.3 %collective-permute-done.15 = bf16[256,2048]{1,0:T(8,128)(2,1)S(1)} collective-permute-done((bf16[256,2048]{1,0:T(8,128)(2,1)S(1)}, bf16[256,2048]{1,0:T(8,128)(2,1)S(1)}, u32[]{:S(2)}, u32[]{:S(2)}) %collective-permute-start.15) | collective-permute-done | bytes 1048608 | tf_op jit(solution)/shard_map/ppermute | solution.py:359
  369.3 26.2 %collective-permute-done.16 = bf16[256,2048]{1,0:T(8,128)(2,1)S(1)} collective-permute-done((bf16[256,2048]{1,0:T(8,128)(2,1)S(1)}, bf16[256,2048]{1,0:T(8,128)(2,1)S(1)}, u32[]{:S(2)}, u32[]{:S(2)}) %collective-permute-start.16) | collective-permute-done | bytes 1048608 | tf_op jit(solution)/shard_map/ppermute | solution.py:359
  395.5 16.6 %collective-permute-done.17 = bf16[256,2048]{1,0:T(8,128)(2,1)S(1)} collective-permute-done((bf16[256,2048]{1,0:T(8,128)(2,1)S(1)}, bf16[256,2048]{1,0:T(8,128)(2,1)S(1)}, u32[]{:S(2)}, u32[]{:S(2)}) %collective-permute-start.17) | collective-permute-done | bytes 1048608 | tf_op jit(solution)/shard_map/ppermute | solution.py:359
  413.1 11.2 %convolution_convert_fusion = bf16[2048,2048]{1,0:T(8,128)(2,1)} fusion(bf16[256,2048]{1,0:T(8,128)(2,1)S(1)} %get-tuple-element.162, bf16[256,2048]{1,0:T(8,128)(2,1)S(1)} %get-tuple-element.164, bf16[256,2048]{1,0:T(8,128)(2,1)S(1)} %copy-done.95, bf16[256,2048]{1,0:T(8,128)(2,1)S(1)} %get-tuple-element.160, ...), kind=kOutput, calls=%fused_computation | convolution fusion | flops 8627683328 | bytes 16777216 | tf_op jit(solution)/shard_map/dot_general | solution.py:31
  424.7 7.9 %multiply_convert_fusion.7 = (bf16[256,2048]{1,0:T(8,128)(2,1)S(1)}, bf16[256,2048]{1,0:T(8,128)(2,1)S(1)}) fusion(f32[256,2048]{1,0:T(8,128)} %copy-done.94, f32[256,2048]{1,0:T(8,128)} %get-tuple-element.161, bf16[256,2048]{1,0:T(8,128)(2,1)} %copy-done.63, bf16[2048,2048]{1,0:T(8,128)(2,1)} %all-gather.10.cloned.1.call-done), kind=kOutput, calls=%fused_computation.51 | convolution fusion | flops 2154299392 | bytes 15728640 | tf_op jit(solution)/shard_map/dot_general | solution.py:27
  432.6 9.1 %multiply_convert_fusion.1 = (bf16[256,2048]{1,0:T(8,128)(2,1)S(1)}, bf16[256,2048]{1,0:T(8,128)(2,1)S(1)}) fusion(f32[256,2048]{1,0:T(8,128)S(1)} %copy-done.91, f32[256,2048]{1,0:T(8,128)} %get-tuple-element.167, bf16[256,2048]{1,0:T(8,128)(2,1)S(1)} %copy-done.85, bf16[2048,2048]{1,0:T(8,128)(2,1)} %all-gather.10.cloned.1.call-done), kind=kOutput, calls=%fused_computation.45 | convolution fusion | flops 2154299392 | bytes 15728640 | tf_op jit(solution)/shard_map/dot_general | solution.py:27
  454.4 13.4 %shard_map.228.refs_8_ = bf16[2048,4096]{1,0:T(8,128)(2,1)} custom-call(bf16[256,2048]{1,0:T(8,128)(2,1)S(1)} %fusion.25.refs_0_, bf16[256,2048]{1,0:T(8,128)(2,1)S(1)} %copy-done.7, bf16[256,2048]{1,0:T(8,128)(2,1)} %collective-permute-done.10.refs_2_, bf16[256,2048]{1,0:T(8,128)(2,1)} %collective-permute-done.11.refs_3_, ...), custom_call_target="tpu_custom_call" | custom-call | flops 8589934592 | bytes 16777216 | tf_op jit(solution)/shard_map/pallas_call | solution.py:317
  467.9 12.7 %shard_map.229 = bf16[2048,4096]{1,0:T(8,128)(2,1)} custom-call(bf16[256,2048]{1,0:T(8,128)(2,1)S(1)} %fusion.25.refs_0_, bf16[256,2048]{1,0:T(8,128)(2,1)S(1)} %copy-done.7, bf16[256,2048]{1,0:T(8,128)(2,1)} %collective-permute-done.10.refs_2_, bf16[256,2048]{1,0:T(8,128)(2,1)} %collective-permute-done.11.refs_3_, ...), custom_call_target="tpu_custom_call", output_to_operand_aliasing={{}: (8, {})} | custom-call | flops 8589934592 | bytes 16777216 | tf_op jit(solution)/shard_map/pallas_call | solution.py:317
  480.7 7.5 fusion.75
  502.5 18.5 %collective-permute-done.18 = bf16[256,2048]{1,0:T(8,128)(2,1)S(1)} collective-permute-done((bf16[256,2048]{1,0:T(8,128)(2,1)S(1)}, bf16[256,2048]{1,0:T(8,128)(2,1)S(1)}, u32[]{:S(2)}, u32[]{:S(2)}) %collective-permute-start.18) | collective-permute-done | bytes 1048608 | tf_op jit(solution)/shard_map/ppermute | solution.py:359
  529.6 17.1 %collective-permute-done.19 = bf16[256,2048]{1,0:T(8,128)(2,1)S(1)} collective-permute-done((bf16[256,2048]{1,0:T(8,128)(2,1)S(1)}, bf16[256,2048]{1,0:T(8,128)(2,1)S(1)}, u32[]{:S(2)}, u32[]{:S(2)}) %collective-permute-start.19) | collective-permute-done | bytes 1048608 | tf_op jit(solution)/shard_map/ppermute | solution.py:359
  554.9 18.3 %collective-permute-done.20 = bf16[256,2048]{1,0:T(8,128)(2,1)S(1)} collective-permute-done((bf16[256,2048]{1,0:T(8,128)(2,1)S(1)}, bf16[256,2048]{1,0:T(8,128)(2,1)S(1)}, u32[]{:S(2)}, u32[]{:S(2)}) %collective-permute-start.20) | collective-permute-done | bytes 1048608 | tf_op jit(solution)/shard_map/ppermute | solution.py:359
  575.4 24.1 %collective-permute-done.21.refs_9_ = bf16[256,2048]{1,0:T(8,128)(2,1)S(1)} collective-permute-done((bf16[256,2048]{1,0:T(8,128)(2,1)S(1)}, bf16[256,2048]{1,0:T(8,128)(2,1)S(1)}, u32[]{:S(2)}, u32[]{:S(2)}) %collective-permute-start.21) | collective-permute-done | bytes 1048608 | tf_op jit(solution)/shard_map/ppermute | solution.py:359
  600.5 22.8 %collective-permute-done.22.refs_10_ = bf16[256,2048]{1,0:T(8,128)(2,1)} collective-permute-done((bf16[256,2048]{1,0:T(8,128)(2,1)S(1)}, bf16[256,2048]{1,0:T(8,128)(2,1)}, u32[]{:S(2)}, u32[]{:S(2)}) %collective-permute-start.22) | collective-permute-done | bytes 1048608 | tf_op jit(solution)/shard_map/ppermute | solution.py:359
  630.9 9.5 %collective-permute-done.23.refs_11_ = bf16[256,2048]{1,0:T(8,128)(2,1)S(1)} collective-permute-done((bf16[256,2048]{1,0:T(8,128)(2,1)}, bf16[256,2048]{1,0:T(8,128)(2,1)S(1)}, u32[]{:S(2)}, u32[]{:S(2)}) %collective-permute-start.23) | collective-permute-done | bytes 1048608 | tf_op jit(solution)/shard_map/ppermute | solution.py:359
  643.1 15.7 %attention_backward.1 = (f32[1024,512]{1,0:T(8,128)}, f32[1024,512]{1,0:T(8,128)}, bf16[1024,512]{1,0:T(8,128)(2,1)S(1)}, f32[2,1,1024]{2,1,0:T(1,128)S(1)}, f32[4,2,128]{2,1,0:T(2,128)S(1)}) custom-call(s32[1]{0:T(128)} %bitcast.me_ref, f32[256,1536]{1,0:T(8,128)} %copy-done.45, f32[256,1536]{1,0:T(8,128)} %copy-done.44, f32[256,1536]{1,0:T(8,128)} %copy-done.43, ...), custom_call_target="tpu_custom_call" | custom-call | flops 2684354560 | bytes 13631488 | tf_op jit(solution)/shard_map/attention_backward/pallas_call | solution.py:211
  674.2 13.1 %attention_weights.1 = bf16[2048,2048]{1,0:T(8,128)(2,1)} custom-call(bf16[256,2048]{1,0:T(8,128)(2,1)S(1)} %copy-done.4, bf16[256,2048]{1,0:T(8,128)(2,1)S(1)} %copy-done.27, bf16[256,2048]{1,0:T(8,128)(2,1)S(1)} %copy-done.29, bf16[256,2048]{1,0:T(8,128)(2,1)} %collective-permute-done.2.refs_3_, bf16[256,1536]{1,0:T(8,128)(2,1)S(1)} %pad_maximum_fusion.2.refs_4_, ...), custom_call_target="tpu_custom_call" | custom-call | flops 8589934592 | bytes 20971520 | tf_op jit(solution)/shard_map/attention_weights/pallas_call | solution.py:286
  699.0 20.1 %collective-permute-done.27 = bf16[256,2048]{1,0:T(8,128)(2,1)S(1)} collective-permute-done((bf16[256,2048]{1,0:T(8,128)(2,1)S(1)}, bf16[256,2048]{1,0:T(8,128)(2,1)S(1)}, u32[]{:S(2)}, u32[]{:S(2)}) %collective-permute-start.27) | collective-permute-done | bytes 1048608 | tf_op jit(solution)/shard_map/ppermute | solution.py:359
  731.9 13.5 %collective-permute-done.28 = bf16[256,2048]{1,0:T(8,128)(2,1)S(1)} collective-permute-done((bf16[256,2048]{1,0:T(8,128)(2,1)}, bf16[256,2048]{1,0:T(8,128)(2,1)S(1)}, u32[]{:S(2)}, u32[]{:S(2)}) %collective-permute-start.28) | collective-permute-done | bytes 1048608 | tf_op jit(solution)/shard_map/ppermute | solution.py:359
  (429 shorter events, 224.6 us)
Async XLA Ops:
  7.2 86.0 %all-gather.6.cloned.1.call-start = ((), (), s32[]{:S(2)}) async-start(), calls=%async_computation.3 | async-start | bytes 9437184 | tf_op jit(solution)/shard_map/all_gather | solution.py:394
  10.7 237.8 %all-gather.8.cloned.1.call-start = ((), (), s32[]{:S(2)}) async-start(), calls=%async_computation.4 | async-start | bytes 18874368 | tf_op jit(solution)/shard_map/all_gather | solution.py:418
  12.3 254.9 %all-gather.10.cloned.1.call-start = ((), (), s32[]{:S(2)}) async-start(), calls=%async_computation.5 | async-start | bytes 9437184 | tf_op jit(solution)/shard_map/all_gather | solution.py:422
  13.5 28.2 %collective-permute-start = (bf16[256,2048]{1,0:T(8,128)(2,1)S(1)}, bf16[256,2048]{1,0:T(8,128)(2,1)S(1)}, u32[]{:S(2)}, u32[]{:S(2)}) collective-permute-start(bf16[256,2048]{1,0:T(8,128)(2,1)S(1)} %copy-done.4), channel_id=1, source_target_pairs={{0,1},{1,2},{2,3},{3,0},{4,5},{5,6},{6,7},{7,4},{8,9},{9,10},{10,1... | collective-permute-start | bytes 3145736 | tf_op jit(solution)/shard_map/ppermute | solution.py:359
  41.7 26.1 %collective-permute-start.1 = (bf16[256,2048]{1,0:T(8,128)(2,1)S(1)}, bf16[256,2048]{1,0:T(8,128)(2,1)S(1)}, u32[]{:S(2)}, u32[]{:S(2)}) collective-permute-start(bf16[256,2048]{1,0:T(8,128)(2,1)S(1)} %collective-permute-done.refs_1_), channel_id=1, source_target_pairs={{0,1},{1,2},{2,3},{3,0},{4,5},{5,6},{6,7},{7,4},{8,9},{9,10},{10,1... | collective-permute-start | bytes 3145736 | tf_op jit(solution)/shard_map/ppermute | solution.py:359
  67.9 25.4 %collective-permute-start.2 = (bf16[256,2048]{1,0:T(8,128)(2,1)S(1)}, bf16[256,2048]{1,0:T(8,128)(2,1)}, u32[]{:S(2)}, u32[]{:S(2)}) collective-permute-start(bf16[256,2048]{1,0:T(8,128)(2,1)S(1)} %collective-permute-done.1.refs_2_), channel_id=1, source_target_pairs={{0,1},{1,2},{2,3},{3,0},{4,5},{5,6},{6,7},{7,4},{8,9},{9,10},{10,1... | collective-permute-start | bytes 3145736 | tf_op jit(solution)/shard_map/ppermute | solution.py:359
  67.9 555.4 %reduce-scatter.4.cloned.1.call-start = ((), (), s32[]{:S(2)}) async-start(), calls=%async_computation.6 | async-start | bytes 9437184 | tf_op jit(solution)/shard_map/reduce_scatter | solution.py:485
  127.8 24.8 %collective-permute-start.6 = (bf16[256,2048]{1,0:T(8,128)(2,1)S(1)}, bf16[256,2048]{1,0:T(8,128)(2,1)S(1)}, u32[]{:S(2)}, u32[]{:S(2)}) collective-permute-start(bf16[256,2048]{1,0:T(8,128)(2,1)S(1)} %convolution_convert_fusion.1), channel_id=1, source_target_pairs={{0,1},{1,2},{2,3},{3,0},{4,5},{5,6},{6,7},{7,4},{8,9},{9,10},{10,1... | collective-permute-start | bytes 3145736 | tf_op jit(solution)/shard_map/ppermute | solution.py:359
  153.5 23.7 %collective-permute-start.7 = (bf16[256,2048]{1,0:T(8,128)(2,1)S(1)}, bf16[256,2048]{1,0:T(8,128)(2,1)S(1)}, u32[]{:S(2)}, u32[]{:S(2)}) collective-permute-start(bf16[256,2048]{1,0:T(8,128)(2,1)S(1)} %add_convert_fusion.7), channel_id=1, source_target_pairs={{0,1},{1,2},{2,3},{3,0},{4,5},{5,6},{6,7},{7,4},{8,9},{9,10},{10,1... | collective-permute-start | bytes 3145736 | tf_op jit(solution)/shard_map/ppermute | solution.py:359
  177.5 22.9 %collective-permute-start.8 = (bf16[256,2048]{1,0:T(8,128)(2,1)S(1)}, bf16[256,2048]{1,0:T(8,128)(2,1)S(1)}, u32[]{:S(2)}, u32[]{:S(2)}) collective-permute-start(bf16[256,2048]{1,0:T(8,128)(2,1)S(1)} %add_convert_fusion.6), channel_id=1, source_target_pairs={{0,1},{1,2},{2,3},{3,0},{4,5},{5,6},{6,7},{7,4},{8,9},{9,10},{10,1... | collective-permute-start | bytes 3145736 | tf_op jit(solution)/shard_map/ppermute | solution.py:359
  202.1 22.4 %collective-permute-start.9 = (bf16[256,2048]{1,0:T(8,128)(2,1)S(1)}, bf16[256,2048]{1,0:T(8,128)(2,1)S(1)}, u32[]{:S(2)}, u32[]{:S(2)}) collective-permute-start(bf16[256,2048]{1,0:T(8,128)(2,1)S(1)} %fusion.25.refs_0_), channel_id=1, source_target_pairs={{0,1},{1,2},{2,3},{3,0},{4,5},{5,6},{6,7},{7,4},{8,9},{9,10},{10,1... | collective-permute-start | bytes 3145736 | tf_op jit(solution)/shard_map/ppermute | solution.py:359
  225.4 23.1 %collective-permute-start.10 = (bf16[256,2048]{1,0:T(8,128)(2,1)S(1)}, bf16[256,2048]{1,0:T(8,128)(2,1)}, u32[]{:S(2)}, u32[]{:S(2)}) collective-permute-start(bf16[256,2048]{1,0:T(8,128)(2,1)S(1)} %collective-permute-done.9.refs_1_), channel_id=1, source_target_pairs={{0,1},{1,2},{2,3},{3,0},{4,5},{5,6},{6,7},{7,4},{8,9},{9,10},{10,1... | collective-permute-start | bytes 3145736 | tf_op jit(solution)/shard_map/ppermute | solution.py:359
  248.5 29.1 %collective-permute-start.11 = (bf16[256,2048]{1,0:T(8,128)(2,1)}, bf16[256,2048]{1,0:T(8,128)(2,1)}, u32[]{:S(2)}, u32[]{:S(2)}) collective-permute-start(bf16[256,2048]{1,0:T(8,128)(2,1)} %collective-permute-done.10.refs_2_), channel_id=1, source_target_pairs={{0,1},{1,2},{2,3},{3,0},{4,5},{5,6},{6,7},{7,4},{8,9},{9,10},{10,1... | collective-permute-start | bytes 3145736 | tf_op jit(solution)/shard_map/ppermute | solution.py:359
  273.4 21.4 %collective-permute-start.12 = (bf16[256,2048]{1,0:T(8,128)(2,1)S(1)}, bf16[256,2048]{1,0:T(8,128)(2,1)S(1)}, u32[]{:S(2)}, u32[]{:S(2)}) collective-permute-start(bf16[256,2048]{1,0:T(8,128)(2,1)S(1)} %convolution_convert_fusion.3), channel_id=1, source_target_pairs={{0,1},{1,2},{2,3},{3,0},{4,5},{5,6},{6,7},{7,4},{8,9},{9,10},{10,1... | collective-permute-start | bytes 3145736 | tf_op jit(solution)/shard_map/ppermute | solution.py:359
  297.1 22.8 %collective-permute-start.13 = (bf16[256,2048]{1,0:T(8,128)(2,1)S(1)}, bf16[256,2048]{1,0:T(8,128)(2,1)S(1)}, u32[]{:S(2)}, u32[]{:S(2)}) collective-permute-start(bf16[256,2048]{1,0:T(8,128)(2,1)S(1)} %add_convert_fusion.5), channel_id=1, source_target_pairs={{0,1},{1,2},{2,3},{3,0},{4,5},{5,6},{6,7},{7,4},{8,9},{9,10},{10,1... | collective-permute-start | bytes 3145736 | tf_op jit(solution)/shard_map/ppermute | solution.py:359
  343.8 25.5 %collective-permute-start.15 = (bf16[256,2048]{1,0:T(8,128)(2,1)S(1)}, bf16[256,2048]{1,0:T(8,128)(2,1)S(1)}, u32[]{:S(2)}, u32[]{:S(2)}) collective-permute-start(bf16[256,2048]{1,0:T(8,128)(2,1)S(1)} %get-tuple-element.113), channel_id=1, source_target_pairs={{0,1},{1,2},{2,3},{3,0},{4,5},{5,6},{6,7},{7,4},{8,9},{9,10},{10,1... | collective-permute-start | bytes 3145736 | tf_op jit(solution)/shard_map/ppermute | solution.py:359
  369.3 26.2 %collective-permute-start.16 = (bf16[256,2048]{1,0:T(8,128)(2,1)S(1)}, bf16[256,2048]{1,0:T(8,128)(2,1)S(1)}, u32[]{:S(2)}, u32[]{:S(2)}) collective-permute-start(bf16[256,2048]{1,0:T(8,128)(2,1)S(1)} %collective-permute-done.15), channel_id=1, source_target_pairs={{0,1},{1,2},{2,3},{3,0},{4,5},{5,6},{6,7},{7,4},{8,9},{9,10},{10,1... | collective-permute-start | bytes 3145736 | tf_op jit(solution)/shard_map/ppermute | solution.py:359
  424.4 322.3 %reduce-scatter.8.cloned.1.call-start = ((), (), s32[]{:S(2)}) async-start(), calls=%async_computation.8 | async-start | bytes 18874368 | tf_op jit(solution)/shard_map/reduce_scatter | solution.py:495
  480.6 285.7 %reduce-scatter.6.cloned.1.call-start = ((), (), s32[]{:S(2)}) async-start(), calls=%async_computation.7 | async-start | bytes 9437184 | tf_op jit(solution)/shard_map/reduce_scatter | solution.py:526
  494.7 26.3 %collective-permute-start.18 = (bf16[256,2048]{1,0:T(8,128)(2,1)S(1)}, bf16[256,2048]{1,0:T(8,128)(2,1)S(1)}, u32[]{:S(2)}, u32[]{:S(2)}) collective-permute-start(bf16[256,2048]{1,0:T(8,128)(2,1)S(1)} %fusion.14), channel_id=1, source_target_pairs={{0,1},{1,2},{2,3},{3,0},{4,5},{5,6},{6,7},{7,4},{8,9},{9,10},{10,1... | collective-permute-start | bytes 3145736 | tf_op jit(solution)/shard_map/ppermute | solution.py:359
  521.3 25.4 %collective-permute-start.19 = (bf16[256,2048]{1,0:T(8,128)(2,1)S(1)}, bf16[256,2048]{1,0:T(8,128)(2,1)S(1)}, u32[]{:S(2)}, u32[]{:S(2)}) collective-permute-start(bf16[256,2048]{1,0:T(8,128)(2,1)S(1)} %add_convert_fusion.3), channel_id=1, source_target_pairs={{0,1},{1,2},{2,3},{3,0},{4,5},{5,6},{6,7},{7,4},{8,9},{9,10},{10,1... | collective-permute-start | bytes 3145736 | tf_op jit(solution)/shard_map/ppermute | solution.py:359
  547.0 26.2 %collective-permute-start.20 = (bf16[256,2048]{1,0:T(8,128)(2,1)S(1)}, bf16[256,2048]{1,0:T(8,128)(2,1)S(1)}, u32[]{:S(2)}, u32[]{:S(2)}) collective-permute-start(bf16[256,2048]{1,0:T(8,128)(2,1)S(1)} %add_convert_fusion.2), channel_id=1, source_target_pairs={{0,1},{1,2},{2,3},{3,0},{4,5},{5,6},{6,7},{7,4},{8,9},{9,10},{10,1... | collective-permute-start | bytes 3145736 | tf_op jit(solution)/shard_map/ppermute | solution.py:359
  575.4 24.1 %collective-permute-start.21 = (bf16[256,2048]{1,0:T(8,128)(2,1)S(1)}, bf16[256,2048]{1,0:T(8,128)(2,1)S(1)}, u32[]{:S(2)}, u32[]{:S(2)}) collective-permute-start(bf16[256,2048]{1,0:T(8,128)(2,1)S(1)} %multiply_convert_fusion.refs_8_), channel_id=1, source_target_pairs={{0,1},{1,2},{2,3},{3,0},{4,5},{5,6},{6,7},{7,4},{8,9},{9,10},{10,1... | collective-permute-start | bytes 3145736 | tf_op jit(solution)/shard_map/ppermute | solution.py:359
  600.5 22.8 %collective-permute-start.22 = (bf16[256,2048]{1,0:T(8,128)(2,1)S(1)}, bf16[256,2048]{1,0:T(8,128)(2,1)}, u32[]{:S(2)}, u32[]{:S(2)}) collective-permute-start(bf16[256,2048]{1,0:T(8,128)(2,1)S(1)} %collective-permute-done.21.refs_9_), channel_id=1, source_target_pairs={{0,1},{1,2},{2,3},{3,0},{4,5},{5,6},{6,7},{7,4},{8,9},{9,10},{10,1... | collective-permute-start | bytes 3145736 | tf_op jit(solution)/shard_map/ppermute | solution.py:359
  623.3 17.1 %collective-permute-start.23 = (bf16[256,2048]{1,0:T(8,128)(2,1)}, bf16[256,2048]{1,0:T(8,128)(2,1)S(1)}, u32[]{:S(2)}, u32[]{:S(2)}) collective-permute-start(bf16[256,2048]{1,0:T(8,128)(2,1)} %collective-permute-done.22.refs_10_), channel_id=1, source_target_pairs={{0,1},{1,2},{2,3},{3,0},{4,5},{5,6},{6,7},{7,4},{8,9},{9,10},{10,1... | collective-permute-start | bytes 3145736 | tf_op jit(solution)/shard_map/ppermute | solution.py:359
  693.0 26.1 %collective-permute-start.27 = (bf16[256,2048]{1,0:T(8,128)(2,1)S(1)}, bf16[256,2048]{1,0:T(8,128)(2,1)S(1)}, u32[]{:S(2)}, u32[]{:S(2)}) collective-permute-start(bf16[256,2048]{1,0:T(8,128)(2,1)S(1)} %convolution_convert_fusion.2), channel_id=1, source_target_pairs={{0,1},{1,2},{2,3},{3,0},{4,5},{5,6},{6,7},{7,4},{8,9},{9,10},{10,1... | collective-permute-start | bytes 3145736 | tf_op jit(solution)/shard_map/ppermute | solution.py:359
  694.2 31.0 %collective-permute-start.31 = (f32[2,2048]{1,0:T(2,128)S(1)}, f32[2,2048]{1,0:T(2,128)S(1)}, u32[]{:S(2)}, u32[]{:S(2)}) collective-permute-start(f32[2,2048]{1,0:T(2,128)S(1)} %pad_maximum_fusion.10), channel_id=1, source_target_pairs={{0,2},{1,3},{2,0},{3,1},{4,6},{5,7},{6,4},{7,5},{8,10},{9,11},{10,... | collective-permute-start | bytes 49160 | tf_op jit(solution)/shard_map/ppermute | solution.py:364
  697.0 28.2 %collective-permute-start.32 = (f32[2,2048]{1,0:T(2,128)S(1)}, f32[2,2048]{1,0:T(2,128)S(1)}, u32[]{:S(2)}, u32[]{:S(2)}) collective-permute-start(f32[2,2048]{1,0:T(2,128)S(1)} %pad_maximum_fusion.10), channel_id=1, source_target_pairs={{0,3},{1,0},{2,1},{3,2},{4,7},{5,4},{6,5},{7,6},{8,11},{9,8},{10,9... | collective-permute-start | bytes 49160 | tf_op jit(solution)/shard_map/ppermute | solution.py:364
  697.2 28.1 %collective-permute-start.30 = (f32[2,2048]{1,0:T(2,128)S(1)}, f32[2,2048]{1,0:T(2,128)S(1)}, u32[]{:S(2)}, u32[]{:S(2)}) collective-permute-start(f32[2,2048]{1,0:T(2,128)S(1)} %pad_maximum_fusion.10), channel_id=1, source_target_pairs={{0,1},{1,2},{2,3},{3,0},{4,5},{5,6},{6,7},{7,4},{8,9},{9,10},{10,1... | collective-permute-start | bytes 49160 | tf_op jit(solution)/shard_map/ppermute | solution.py:364
  725.0 20.4 %collective-permute-start.28 = (bf16[256,2048]{1,0:T(8,128)(2,1)}, bf16[256,2048]{1,0:T(8,128)(2,1)S(1)}, u32[]{:S(2)}, u32[]{:S(2)}) collective-permute-start(bf16[256,2048]{1,0:T(8,128)(2,1)} %add_convert_fusion.1), channel_id=1, source_target_pairs={{0,1},{1,2},{2,3},{3,0},{4,5},{5,6},{6,7},{7,4},{8,9},{9,10},{10,1... | collective-permute-start | bytes 3145736 | tf_op jit(solution)/shard_map/ppermute | solution.py:359
  731.8 21.2 %collective-permute-start.35 = (f32[8,640]{1,0:T(8,128)S(1)}, f32[8,640]{1,0:T(8,128)S(1)}, u32[]{:S(2)}, u32[]{:S(2)}) collective-permute-start(f32[8,640]{1,0:T(8,128)S(1)} %add.205), channel_id=1, source_target_pairs={{0,16},{4,20},{8,24},{12,28},{16,0},{20,4},{24,8},{28,12},{1,17},{... | collective-permute-start | bytes 61448 | tf_op jit(solution)/shard_map/ppermute | solution.py:549
  746.7 17.8 %collective-permute-start.29 = (bf16[256,2048]{1,0:T(8,128)(2,1)}, bf16[256,2048]{1,0:T(8,128)(2,1)S(1)}, u32[]{:S(2)}, u32[]{:S(2)}) collective-permute-start(bf16[256,2048]{1,0:T(8,128)(2,1)} %add_convert_fusion), channel_id=1, source_target_pairs={{0,1},{1,2},{2,3},{3,0},{4,5},{5,6},{6,7},{7,4},{8,9},{9,10},{10,1... | collective-permute-start | bytes 3145736 | tf_op jit(solution)/shard_map/ppermute | solution.py:359
  (118 other events, 1475.9 us)
Sparse Core Ops, SparseCore 0:
  10.8 56.9 all-gather.5
  70.3 89.7 all-gather.7
  161.9 55.8 all-gather.9
  424.5 76.0 reduce-scatter.3
  504.0 116.2 reduce-scatter.7
  687.4 70.9 reduce-scatter.5

commit v4 on v3

--- a/solution.py
+++ b/solution.py
@@ -267,14 +267,16 @@
 
 def weight_kernel(n, *refs):
     x_in, d_in, a_in = refs[:n], refs[n : 2 * n], refs[2 * n : 3 * n]
-    attn, out = refs[3 * n :]
-    rows, wide = d_in[0].shape
+    attn, first, second = refs[3 * n :]
+    rows = d_in[0].shape[0]
+    cut, narrow = first.shape[1], attn.shape[1]
     one = sum(dot_left_t(x_in[s][...], d_in[s][...]) for s in range(n))
-    out[:, :wide] = one.astype(BF)
+    first[...] = one[:, :cut].astype(BF)
+    second[:, : second.shape[1] - narrow] = one[:, cut:].astype(BF)
     two = sum(
         dot_left_t(a_in[s][...], attn[s * rows : (s + 1) * rows, :]) for s in range(n)
     )
-    out[:, wide:] = two.astype(BF)
+    second[:, second.shape[1] - narrow :] = two.astype(BF)
 
 
 def attention_weights(held_x, d_qkv, held_a, attn):
@@ -290,8 +292,8 @@
         + once * n
         + [step] * n
         + [pl.BlockSpec((n * rows, narrow), lambda i: (0, 0), pipeline_mode=pl.Buffered(1))],
-        out_specs=pl.BlockSpec((tile, wide + narrow), lambda i: (i, 0)),
-        out_shape=jax.ShapeDtypeStruct((width, wide + narrow), BF),
+        out_specs=[pl.BlockSpec((tile, 2 * narrow), lambda i: (i, 0))] * 2,
+        out_shape=[jax.ShapeDtypeStruct((width, 2 * narrow), BF)] * 2,
         compiler_params=pltpu.CompilerParams(vmem_limit_bytes=40 << 20),
         cost_estimate=pl.CostEstimate(
             flops=2 * n * rows * width * (wide + narrow),
@@ -364,6 +366,22 @@
             total = total + lax.ppermute(value, "mp", [(i, (i + k) % n) for i in range(n)])
         return total
 
+    def halve(whole):
+        if groups & (groups - 1):
+            return lax.psum_scatter(whole, "dp", scatter_dimension=0, tiled=True).astype(F32)
+        place = lax.axis_index("dp")
+        left = whole.reshape(groups, whole.shape[0] // groups, whole.shape[1])
+        for k in range(groups.bit_length() - 1):
+            bit = (place >> k) & 1
+            paired = left.reshape(left.shape[0] // 2, 2, *left.shape[1:])
+            kept = lax.dynamic_index_in_dim(paired, bit, 1, keepdims=False)
+            sent = lax.dynamic_index_in_dim(paired, 1 - bit, 1, keepdims=False)
+            got = lax.ppermute(sent.astype(BF), "dp", [(i, i ^ (1 << k)) for i in range(groups)])
+            left = kept.astype(F32) + got.astype(F32)
+            if left.shape[0] > 1:
+                left = left.astype(BF)
+        return left[0]
+
     def reorder(stacked):
         turned = stacked[::-1]
         return lax.dynamic_slice_in_dim(
@@ -522,17 +540,18 @@
             parts.append((rate * (t[at] - raw * (rate * back[s, 2 + which][:, None]))).astype(BF))
         parts.append(d_value[at])
         d_qkv.append(jnp.concatenate(parts, axis=1))
-    dw_attn = attention_weights(held_x, d_qkv, held_a, attn)
+    dw_attn, dw_rest = attention_weights(held_x, d_qkv, held_a, attn)
     grad_attn = lax.psum_scatter(dw_attn, "dp", scatter_dimension=0, tiled=True)
     input_grad = d_resid + scatter_ring(
         lambda s: dot_right_t(d_qkv[s], w_qkv), {n - 1: grad_gate_up}
     )
 
+    grad_rest = halve(dw_rest)
     grad_attn, input_grad = lax.optimization_barrier((grad_attn, input_grad))
     grad_query = grad_attn[:, :head_cols].astype(F32)
     grad_key = grad_attn[:, head_cols : 2 * head_cols].astype(F32)
-    grad_value = grad_attn[:, 2 * head_cols : 3 * head_cols].astype(F32)
-    grad_out = grad_attn[:, 3 * head_cols :].astype(F32).T
+    grad_value = grad_rest[:, :head_cols]
+    grad_out = grad_rest[:, head_cols:].T
     grad_gate = grad_gate_up[:, :units].astype(F32)
     grad_up = grad_gate_up[:, units:].astype(F32)
 

time: 786 us -> 810 us (1.031)
  waiting for transfers between devices: 429 us -> 444 us
  other arithmetic: 30.9 us -> 39.1 us
    ppermute x0 -> x3, waiting for transfers between devices: none -> 34.5 us  [halve(): lax.ppermute(sent.astype(BF), 'dp', [(i, i ^ 1 << k) for i in range(group...]
    ppermute x24, waiting for transfers between devices: 429 us -> 409 us  [shift(): return lax.ppermute(value, 'mp', ring)]
    unnamed x227 -> x247, local copies, waits for them, and re-layouts: 20.2 us -> 20.2 us
  transfers between devices with their start and end apart: 42 -> 45, of which waited for: 23 -> 25; matrix products, arithmetic and copies ran while one was open for 24% -> 25% of each run, Pallas kernels for 9% -> 9%
where the time goes in v4:
time: 810 us; the launch traced here: 800 us
  waiting for transfers between devices  444 us (55%)
  matrix products  166 us (20%)
  Pallas kernels  68.7 us (8%)
  other arithmetic  39.1 us (5%)
  local copies, waits for them, and re-layouts  34.9 us (4%)
  starting transfers between devices  22 us (3%)
  between operations  16.7 us (2%)
  blocking collectives  8.84 us (1%)
    ppermute x24, waiting for transfers between devices, shift(): return lax.ppermute(value, 'mp', ring)  409 us
    dot_general x20, matrix products, dot_right_t(): lax.dot_general(left, right, (((1,), (1,)), ((), ())), preferred_element_...  88.6 us
    dot_general x20, matrix products, dot_plain(): return jnp.dot(left, right, preferred_element_type=F32)  66.1 us
    ppermute x3, waiting for transfers between devices, halve(): lax.ppermute(sent.astype(BF), 'dp', [(i, i ^ 1 << k) for i in range(group...  34.5 us
    pallas_call x2, Pallas kernels, half_weights(): pl.pallas_call(functools.partial(half_kernel, n), grid=(width // tile,),...  26.2 us
    unnamed x247, local copies, waits for them, and re-layouts  20.2 us
  transfers between devices with their start and end apart: 45, of which 25 were waited for; matrix products, arithmetic and copies ran while one was open for 25% of the time, Pallas kernels for 9%

profile of v4, /device:TPU:0, one launch (start us, length us, event | category | flops | bytes accessed | tf_op | source)
XLA Modules:
  0.0 800.2 jit_solution(13876929087098309567)
XLA Ops:
  16.6 25.2 %collective-permute-done.refs_1_ = bf16[256,2048]{1,0:T(8,128)(2,1)S(1)} collective-permute-done((bf16[256,2048]{1,0:T(8,128)(2,1)S(1)}, bf16[256,2048]{1,0:T(8,128)(2,1)S(1)}, u32[]{:S(2)}, u32[]{:S(2)}) %collective-permute-start) | collective-permute-done | bytes 1048608 | tf_op jit(solution)/shard_map/ppermute | solution.py:361
  41.7 26.1 %collective-permute-done.1.refs_2_ = bf16[256,2048]{1,0:T(8,128)(2,1)S(1)} collective-permute-done((bf16[256,2048]{1,0:T(8,128)(2,1)S(1)}, bf16[256,2048]{1,0:T(8,128)(2,1)S(1)}, u32[]{:S(2)}, u32[]{:S(2)}) %collective-permute-start.1) | collective-permute-done | bytes 1048608 | tf_op jit(solution)/shard_map/ppermute | solution.py:361
  68.2 8.8 %all-gather.1 = bf16[8,1,640]{2,1,0:T(2,128)(2,1)S(1)} all-gather(bf16[1,1,640]{2,1,0:T(2,128)(2,1)S(1)} %reshape.236), channel_id=2, replica_groups=mesh['dp'=8,'mp'=4] {'dp'}, dimensions={0}, use_global_device_ids=true | all-gather | bytes 11520 | tf_op jit(solution)/shard_map/all_gather | solution.py:423
  80.3 13.0 %collective-permute-done.2.refs_3_ = bf16[256,2048]{1,0:T(8,128)(2,1)} collective-permute-done((bf16[256,2048]{1,0:T(8,128)(2,1)S(1)}, bf16[256,2048]{1,0:T(8,128)(2,1)}, u32[]{:S(2)}, u32[]{:S(2)}) %collective-permute-start.2) | collective-permute-done | bytes 1048608 | tf_op jit(solution)/shard_map/ppermute | solution.py:361
  113.1 13.8 %attention_forward.1 = (bf16[1024,512]{1,0:T(8,128)(2,1)S(1)}, bf16[1024,512]{1,0:T(8,128)(2,1)S(1)}, bf16[1024,512]{1,0:T(8,128)(2,1)S(1)}, bf16[1024,512]{1,0:T(8,128)(2,1)}, f32[4,1,1024]{2,1,0:T(1,128)S(1)}) custom-call(s32[1]{0:T(128)} %bitcast.me_ref, f32[256,1536]{1,0:T(8,128)} %copy-done.42, f32[256,1536]{1,0:T(8,128)} %copy-done.41, ...), custom_call_target="tpu_custom_call" | custom-call | flops 1073741824 | bytes 11534336 | tf_op jit(solution)/shard_map/attention_forward/pallas_call | solution.py:167
  129.6 23.0 %collective-permute-done.6 = bf16[256,2048]{1,0:T(8,128)(2,1)S(1)} collective-permute-done((bf16[256,2048]{1,0:T(8,128)(2,1)S(1)}, bf16[256,2048]{1,0:T(8,128)(2,1)S(1)}, u32[]{:S(2)}, u32[]{:S(2)}) %collective-permute-start.6) | collective-permute-done | bytes 1048608 | tf_op jit(solution)/shard_map/ppermute | solution.py:361
  154.2 22.8 %collective-permute-done.7 = bf16[256,2048]{1,0:T(8,128)(2,1)S(1)} collective-permute-done((bf16[256,2048]{1,0:T(8,128)(2,1)S(1)}, bf16[256,2048]{1,0:T(8,128)(2,1)S(1)}, u32[]{:S(2)}, u32[]{:S(2)}) %collective-permute-start.7) | collective-permute-done | bytes 1048608 | tf_op jit(solution)/shard_map/ppermute | solution.py:361
  178.2 21.9 %collective-permute-done.8 = bf16[256,2048]{1,0:T(8,128)(2,1)S(1)} collective-permute-done((bf16[256,2048]{1,0:T(8,128)(2,1)S(1)}, bf16[256,2048]{1,0:T(8,128)(2,1)S(1)}, u32[]{:S(2)}, u32[]{:S(2)}) %collective-permute-start.8) | collective-permute-done | bytes 1048608 | tf_op jit(solution)/shard_map/ppermute | solution.py:361
  201.8 22.3 %collective-permute-done.9.refs_1_ = bf16[256,2048]{1,0:T(8,128)(2,1)S(1)} collective-permute-done((bf16[256,2048]{1,0:T(8,128)(2,1)S(1)}, bf16[256,2048]{1,0:T(8,128)(2,1)S(1)}, u32[]{:S(2)}, u32[]{:S(2)}) %collective-permute-start.9) | collective-permute-done | bytes 1048608 | tf_op jit(solution)/shard_map/ppermute | solution.py:361
  225.2 23.1 %collective-permute-done.10.refs_2_ = bf16[256,2048]{1,0:T(8,128)(2,1)} collective-permute-done((bf16[256,2048]{1,0:T(8,128)(2,1)S(1)}, bf16[256,2048]{1,0:T(8,128)(2,1)}, u32[]{:S(2)}, u32[]{:S(2)}) %collective-permute-start.10) | collective-permute-done | bytes 1048608 | tf_op jit(solution)/shard_map/ppermute | solution.py:361
  304.2 15.3 %collective-permute-done.13 = bf16[256,2048]{1,0:T(8,128)(2,1)S(1)} collective-permute-done((bf16[256,2048]{1,0:T(8,128)(2,1)S(1)}, bf16[256,2048]{1,0:T(8,128)(2,1)S(1)}, u32[]{:S(2)}, u32[]{:S(2)}) %collective-permute-start.13) | collective-permute-done | bytes 1048608 | tf_op jit(solution)/shard_map/ppermute | solution.py:361
  326.3 10.9 %collective-permute-done.14 = bf16[256,2048]{1,0:T(8,128)(2,1)S(1)} collective-permute-done((bf16[256,2048]{1,0:T(8,128)(2,1)S(1)}, bf16[256,2048]{1,0:T(8,128)(2,1)S(1)}, u32[]{:S(2)}, u32[]{:S(2)}) %collective-permute-start.14) | collective-permute-done | bytes 1048608 | tf_op jit(solution)/shard_map/ppermute | solution.py:361
  343.8 25.4 %collective-permute-done.15 = bf16[256,2048]{1,0:T(8,128)(2,1)S(1)} collective-permute-done((bf16[256,2048]{1,0:T(8,128)(2,1)S(1)}, bf16[256,2048]{1,0:T(8,128)(2,1)S(1)}, u32[]{:S(2)}, u32[]{:S(2)}) %collective-permute-start.15) | collective-permute-done | bytes 1048608 | tf_op jit(solution)/shard_map/ppermute | solution.py:361
  369.1 26.3 %collective-permute-done.16 = bf16[256,2048]{1,0:T(8,128)(2,1)S(1)} collective-permute-done((bf16[256,2048]{1,0:T(8,128)(2,1)S(1)}, bf16[256,2048]{1,0:T(8,128)(2,1)S(1)}, u32[]{:S(2)}, u32[]{:S(2)}) %collective-permute-start.16) | collective-permute-done | bytes 1048608 | tf_op jit(solution)/shard_map/ppermute | solution.py:361
  395.4 16.6 %collective-permute-done.17 = bf16[256,2048]{1,0:T(8,128)(2,1)S(1)} collective-permute-done((bf16[256,2048]{1,0:T(8,128)(2,1)S(1)}, bf16[256,2048]{1,0:T(8,128)(2,1)S(1)}, u32[]{:S(2)}, u32[]{:S(2)}) %collective-permute-start.17) | collective-permute-done | bytes 1048608 | tf_op jit(solution)/shard_map/ppermute | solution.py:361
  413.0 11.3 %convolution_convert_fusion = bf16[2048,2048]{1,0:T(8,128)(2,1)} fusion(bf16[256,2048]{1,0:T(8,128)(2,1)S(1)} %get-tuple-element.166, bf16[256,2048]{1,0:T(8,128)(2,1)S(1)} %get-tuple-element.168, bf16[256,2048]{1,0:T(8,128)(2,1)S(1)} %copy-done.101, bf16[256,2048]{1,0:T(8,128)(2,1)S(1)} %get-tuple-element.164, ...), kind=kOutput, calls=%fused_computation | convolution fusion | flops 8627683328 | bytes 16777216 | tf_op jit(solution)/shard_map/dot_general | solution.py:31
  424.6 7.9 multiply_convert_fusion.7
  432.6 9.2 %multiply_convert_fusion.1 = (bf16[256,2048]{1,0:T(8,128)(2,1)S(1)}, bf16[256,2048]{1,0:T(8,128)(2,1)S(1)}) fusion(f32[256,2048]{1,0:T(8,128)S(1)} %copy-done.97, f32[256,2048]{1,0:T(8,128)} %get-tuple-element.171, bf16[256,2048]{1,0:T(8,128)(2,1)S(1)} %copy-done.91, bf16[2048,2048]{1,0:T(8,128)(2,1)} %all-gather.10.cloned.1.call-done), kind=kOutput, calls=%fused_computation.50 | convolution fusion | flops 2154299392 | bytes 15728640 | tf_op jit(solution)/shard_map/dot_general | solution.py:27
  454.3 13.4 %shard_map.228.refs_8_ = bf16[2048,4096]{1,0:T(8,128)(2,1)} custom-call(bf16[256,2048]{1,0:T(8,128)(2,1)S(1)} %fusion.27.refs_0_, bf16[256,2048]{1,0:T(8,128)(2,1)S(1)} %copy-done.7, bf16[256,2048]{1,0:T(8,128)(2,1)} %collective-permute-done.10.refs_2_, bf16[256,2048]{1,0:T(8,128)(2,1)} %collective-permute-done.11.refs_3_, ...), custom_call_target="tpu_custom_call" | custom-call | flops 8589934592 | bytes 16777216 | tf_op jit(solution)/shard_map/pallas_call | solution.py:319
  467.7 12.7 %shard_map.229 = bf16[2048,4096]{1,0:T(8,128)(2,1)} custom-call(bf16[256,2048]{1,0:T(8,128)(2,1)S(1)} %fusion.27.refs_0_, bf16[256,2048]{1,0:T(8,128)(2,1)S(1)} %copy-done.7, bf16[256,2048]{1,0:T(8,128)(2,1)} %collective-permute-done.10.refs_2_, bf16[256,2048]{1,0:T(8,128)(2,1)} %collective-permute-done.11.refs_3_, ...), custom_call_target="tpu_custom_call", output_to_operand_aliasing={{}: (8, {})} | custom-call | flops 8589934592 | bytes 16777216 | tf_op jit(solution)/shard_map/pallas_call | solution.py:319
  480.6 7.5 fusion.78
  502.4 18.4 %collective-permute-done.18 = bf16[256,2048]{1,0:T(8,128)(2,1)S(1)} collective-permute-done((bf16[256,2048]{1,0:T(8,128)(2,1)S(1)}, bf16[256,2048]{1,0:T(8,128)(2,1)S(1)}, u32[]{:S(2)}, u32[]{:S(2)}) %collective-permute-start.18) | collective-permute-done | bytes 1048608 | tf_op jit(solution)/shard_map/ppermute | solution.py:361
  529.5 17.0 %collective-permute-done.19 = bf16[256,2048]{1,0:T(8,128)(2,1)S(1)} collective-permute-done((bf16[256,2048]{1,0:T(8,128)(2,1)S(1)}, bf16[256,2048]{1,0:T(8,128)(2,1)S(1)}, u32[]{:S(2)}, u32[]{:S(2)}) %collective-permute-start.19) | collective-permute-done | bytes 1048608 | tf_op jit(solution)/shard_map/ppermute | solution.py:361
  554.7 18.2 %collective-permute-done.20 = bf16[256,2048]{1,0:T(8,128)(2,1)S(1)} collective-permute-done((bf16[256,2048]{1,0:T(8,128)(2,1)S(1)}, bf16[256,2048]{1,0:T(8,128)(2,1)S(1)}, u32[]{:S(2)}, u32[]{:S(2)}) %collective-permute-start.20) | collective-permute-done | bytes 1048608 | tf_op jit(solution)/shard_map/ppermute | solution.py:361
  575.0 23.5 %collective-permute-done.21.refs_9_ = bf16[256,2048]{1,0:T(8,128)(2,1)} collective-permute-done((bf16[256,2048]{1,0:T(8,128)(2,1)S(1)}, bf16[256,2048]{1,0:T(8,128)(2,1)}, u32[]{:S(2)}, u32[]{:S(2)}) %collective-permute-start.21) | collective-permute-done | bytes 1048608 | tf_op jit(solution)/shard_map/ppermute | solution.py:361
  598.5 23.0 %collective-permute-done.22.refs_10_ = bf16[256,2048]{1,0:T(8,128)(2,1)} collective-permute-done((bf16[256,2048]{1,0:T(8,128)(2,1)}, bf16[256,2048]{1,0:T(8,128)(2,1)}, u32[]{:S(2)}, u32[]{:S(2)}) %collective-permute-start.22) | collective-permute-done | bytes 1048608 | tf_op jit(solution)/shard_map/ppermute | solution.py:361
  641.2 15.7 %attention_backward.1 = (f32[1024,512]{1,0:T(8,128)}, f32[1024,512]{1,0:T(8,128)}, bf16[1024,512]{1,0:T(8,128)(2,1)S(1)}, f32[2,1,1024]{2,1,0:T(1,128)S(1)}, f32[4,2,128]{2,1,0:T(2,128)S(1)}) custom-call(s32[1]{0:T(128)} %bitcast.me_ref, f32[256,1536]{1,0:T(8,128)} %copy-done.42, f32[256,1536]{1,0:T(8,128)} %copy-done.41, f32[256,1536]{1,0:T(8,128)} %copy-done.40, ...), custom_call_target="tpu_custom_call" | custom-call | flops 2684354560 | bytes 13631488 | tf_op jit(solution)/shard_map/attention_backward/pallas_call | solution.py:211
  671.7 13.0 %attention_weights.1 = (bf16[2048,1024]{1,0:T(8,128)(2,1)}, bf16[2048,1024]{1,0:T(8,128)(2,1)}) custom-call(bf16[256,2048]{1,0:T(8,128)(2,1)S(1)} %copy-done.4, bf16[256,2048]{1,0:T(8,128)(2,1)S(1)} %copy-done.27, bf16[256,2048]{1,0:T(8,128)(2,1)S(1)} %copy-done.29, bf16[256,2048]{1,0:T(8,128)(2,1)} %collective-permute-done.2.refs_3_, ...), custom_call_target="tpu_custom_call" | custom-call | flops 8589934592 | bytes 20971520 | tf_op jit(solution)/shard_map/attention_weights/pallas_call | solution.py:288
  701.7 15.9 %collective-permute-done.27 = bf16[256,2048]{1,0:T(8,128)(2,1)} collective-permute-done((bf16[256,2048]{1,0:T(8,128)(2,1)}, bf16[256,2048]{1,0:T(8,128)(2,1)}, u32[]{:S(2)}, u32[]{:S(2)}) %collective-permute-start.27) | collective-permute-done | bytes 1048608 | tf_op jit(solution)/shard_map/ppermute | solution.py:361
  732.5 24.5 %collective-permute-done.31 = bf16[2,256,1024]{2,1,0:T(8,128)(2,1)} collective-permute-done((bf16[2,256,1024]{2,1,0:T(8,128)(2,1)S(1)}, bf16[2,256,1024]{2,1,0:T(8,128)(2,1)}, u32[]{:S(2)}, u32[]{:S(2)}) %collective-permute-start.31) | collective-permute-done | bytes 1048608 | tf_op jit(solution)/shard_map/ppermute | solution.py:379
  761.6 10.0 %collective-permute-done.32 = bf16[1,256,1024]{2,1,0:T(8,128)(2,1)S(1)} collective-permute-done((bf16[1,256,1024]{2,1,0:T(8,128)(2,1)S(1)}, bf16[1,256,1024]{2,1,0:T(8,128)(2,1)S(1)}, u32[]{:S(2)}, u32[]{:S(2)}) %collective-permute-start.32) | collective-permute-done | bytes 524320 | tf_op jit(solution)/shard_map/ppermute | solution.py:379
  778.5 9.2 %collective-permute-done.29 = bf16[256,2048]{1,0:T(8,128)(2,1)} collective-permute-done((bf16[256,2048]{1,0:T(8,128)(2,1)}, bf16[256,2048]{1,0:T(8,128)(2,1)}, u32[]{:S(2)}, u32[]{:S(2)}) %collective-permute-start.29) | collective-permute-done | bytes 1048608 | tf_op jit(solution)/shard_map/ppermute | solution.py:361
  (464 shorter events, 238.4 us)
Async XLA Ops:
  7.2 86.0 %all-gather.6.cloned.1.call-start = ((), (), s32[]{:S(2)}) async-start(), calls=%async_computation.3 | async-start | bytes 9437184 | tf_op jit(solution)/shard_map/all_gather | solution.py:412
  10.7 237.6 %all-gather.8.cloned.1.call-start = ((), (), s32[]{:S(2)}) async-start(), calls=%async_computation.4 | async-start | bytes 18874368 | tf_op jit(solution)/shard_map/all_gather | solution.py:436
  12.3 254.4 %all-gather.10.cloned.1.call-start = ((), (), s32[]{:S(2)}) async-start(), calls=%async_computation.5 | async-start | bytes 9437184 | tf_op jit(solution)/shard_map/all_gather | solution.py:440
  13.5 28.2 %collective-permute-start = (bf16[256,2048]{1,0:T(8,128)(2,1)S(1)}, bf16[256,2048]{1,0:T(8,128)(2,1)S(1)}, u32[]{:S(2)}, u32[]{:S(2)}) collective-permute-start(bf16[256,2048]{1,0:T(8,128)(2,1)S(1)} %copy-done.4), channel_id=1, source_target_pairs={{0,1},{1,2},{2,3},{3,0},{4,5},{5,6},{6,7},{7,4},{8,9},{9,10},{10,1... | collective-permute-start | bytes 3145736 | tf_op jit(solution)/shard_map/ppermute | solution.py:361
  41.7 26.1 %collective-permute-start.1 = (bf16[256,2048]{1,0:T(8,128)(2,1)S(1)}, bf16[256,2048]{1,0:T(8,128)(2,1)S(1)}, u32[]{:S(2)}, u32[]{:S(2)}) collective-permute-start(bf16[256,2048]{1,0:T(8,128)(2,1)S(1)} %collective-permute-done.refs_1_), channel_id=1, source_target_pairs={{0,1},{1,2},{2,3},{3,0},{4,5},{5,6},{6,7},{7,4},{8,9},{9,10},{10,1... | collective-permute-start | bytes 3145736 | tf_op jit(solution)/shard_map/ppermute | solution.py:361
  67.9 25.4 %collective-permute-start.2 = (bf16[256,2048]{1,0:T(8,128)(2,1)S(1)}, bf16[256,2048]{1,0:T(8,128)(2,1)}, u32[]{:S(2)}, u32[]{:S(2)}) collective-permute-start(bf16[256,2048]{1,0:T(8,128)(2,1)S(1)} %collective-permute-done.1.refs_2_), channel_id=1, source_target_pairs={{0,1},{1,2},{2,3},{3,0},{4,5},{5,6},{6,7},{7,4},{8,9},{9,10},{10,1... | collective-permute-start | bytes 3145736 | tf_op jit(solution)/shard_map/ppermute | solution.py:361
  67.9 553.6 %reduce-scatter.4.cloned.1.call-start = ((), (), s32[]{:S(2)}) async-start(), calls=%async_computation.6 | async-start | bytes 9437184 | tf_op jit(solution)/shard_map/reduce_scatter | solution.py:503
  127.8 24.7 %collective-permute-start.6 = (bf16[256,2048]{1,0:T(8,128)(2,1)S(1)}, bf16[256,2048]{1,0:T(8,128)(2,1)S(1)}, u32[]{:S(2)}, u32[]{:S(2)}) collective-permute-start(bf16[256,2048]{1,0:T(8,128)(2,1)S(1)} %convolution_convert_fusion.1), channel_id=1, source_target_pairs={{0,1},{1,2},{2,3},{3,0},{4,5},{5,6},{6,7},{7,4},{8,9},{9,10},{10,1... | collective-permute-start | bytes 3145736 | tf_op jit(solution)/shard_map/ppermute | solution.py:361
  153.4 23.7 %collective-permute-start.7 = (bf16[256,2048]{1,0:T(8,128)(2,1)S(1)}, bf16[256,2048]{1,0:T(8,128)(2,1)S(1)}, u32[]{:S(2)}, u32[]{:S(2)}) collective-permute-start(bf16[256,2048]{1,0:T(8,128)(2,1)S(1)} %add_convert_fusion.7), channel_id=1, source_target_pairs={{0,1},{1,2},{2,3},{3,0},{4,5},{5,6},{6,7},{7,4},{8,9},{9,10},{10,1... | collective-permute-start | bytes 3145736 | tf_op jit(solution)/shard_map/ppermute | solution.py:361
  177.3 22.8 %collective-permute-start.8 = (bf16[256,2048]{1,0:T(8,128)(2,1)S(1)}, bf16[256,2048]{1,0:T(8,128)(2,1)S(1)}, u32[]{:S(2)}, u32[]{:S(2)}) collective-permute-start(bf16[256,2048]{1,0:T(8,128)(2,1)S(1)} %add_convert_fusion.6), channel_id=1, source_target_pairs={{0,1},{1,2},{2,3},{3,0},{4,5},{5,6},{6,7},{7,4},{8,9},{9,10},{10,1... | collective-permute-start | bytes 3145736 | tf_op jit(solution)/shard_map/ppermute | solution.py:361
  201.8 22.4 %collective-permute-start.9 = (bf16[256,2048]{1,0:T(8,128)(2,1)S(1)}, bf16[256,2048]{1,0:T(8,128)(2,1)S(1)}, u32[]{:S(2)}, u32[]{:S(2)}) collective-permute-start(bf16[256,2048]{1,0:T(8,128)(2,1)S(1)} %fusion.27.refs_0_), channel_id=1, source_target_pairs={{0,1},{1,2},{2,3},{3,0},{4,5},{5,6},{6,7},{7,4},{8,9},{9,10},{10,1... | collective-permute-start | bytes 3145736 | tf_op jit(solution)/shard_map/ppermute | solution.py:361
  225.2 23.1 %collective-permute-start.10 = (bf16[256,2048]{1,0:T(8,128)(2,1)S(1)}, bf16[256,2048]{1,0:T(8,128)(2,1)}, u32[]{:S(2)}, u32[]{:S(2)}) collective-permute-start(bf16[256,2048]{1,0:T(8,128)(2,1)S(1)} %collective-permute-done.9.refs_1_), channel_id=1, source_target_pairs={{0,1},{1,2},{2,3},{3,0},{4,5},{5,6},{6,7},{7,4},{8,9},{9,10},{10,1... | collective-permute-start | bytes 3145736 | tf_op jit(solution)/shard_map/ppermute | solution.py:361
  248.3 28.9 %collective-permute-start.11 = (bf16[256,2048]{1,0:T(8,128)(2,1)}, bf16[256,2048]{1,0:T(8,128)(2,1)}, u32[]{:S(2)}, u32[]{:S(2)}) collective-permute-start(bf16[256,2048]{1,0:T(8,128)(2,1)} %collective-permute-done.10.refs_2_), channel_id=1, source_target_pairs={{0,1},{1,2},{2,3},{3,0},{4,5},{5,6},{6,7},{7,4},{8,9},{9,10},{10,1... | collective-permute-start | bytes 3145736 | tf_op jit(solution)/shard_map/ppermute | solution.py:361
  296.7 22.8 %collective-permute-start.13 = (bf16[256,2048]{1,0:T(8,128)(2,1)S(1)}, bf16[256,2048]{1,0:T(8,128)(2,1)S(1)}, u32[]{:S(2)}, u32[]{:S(2)}) collective-permute-start(bf16[256,2048]{1,0:T(8,128)(2,1)S(1)} %add_convert_fusion.5), channel_id=1, source_target_pairs={{0,1},{1,2},{2,3},{3,0},{4,5},{5,6},{6,7},{7,4},{8,9},{9,10},{10,1... | collective-permute-start | bytes 3145736 | tf_op jit(solution)/shard_map/ppermute | solution.py:361
  343.8 25.4 %collective-permute-start.15 = (bf16[256,2048]{1,0:T(8,128)(2,1)S(1)}, bf16[256,2048]{1,0:T(8,128)(2,1)S(1)}, u32[]{:S(2)}, u32[]{:S(2)}) collective-permute-start(bf16[256,2048]{1,0:T(8,128)(2,1)S(1)} %get-tuple-element.117), channel_id=1, source_target_pairs={{0,1},{1,2},{2,3},{3,0},{4,5},{5,6},{6,7},{7,4},{8,9},{9,10},{10,1... | collective-permute-start | bytes 3145736 | tf_op jit(solution)/shard_map/ppermute | solution.py:361
  369.1 26.3 %collective-permute-start.16 = (bf16[256,2048]{1,0:T(8,128)(2,1)S(1)}, bf16[256,2048]{1,0:T(8,128)(2,1)S(1)}, u32[]{:S(2)}, u32[]{:S(2)}) collective-permute-start(bf16[256,2048]{1,0:T(8,128)(2,1)S(1)} %collective-permute-done.15), channel_id=1, source_target_pairs={{0,1},{1,2},{2,3},{3,0},{4,5},{5,6},{6,7},{7,4},{8,9},{9,10},{10,1... | collective-permute-start | bytes 3145736 | tf_op jit(solution)/shard_map/ppermute | solution.py:361
  424.3 337.3 %reduce-scatter.8.cloned.1.call-start = ((), (), s32[]{:S(2)}) async-start(), calls=%async_computation.8 | async-start | bytes 18874368 | tf_op jit(solution)/shard_map/reduce_scatter | solution.py:513
  480.5 310.2 %reduce-scatter.6.cloned.1.call-start = ((), (), s32[]{:S(2)}) async-start(), calls=%async_computation.7 | async-start | bytes 4718592 | tf_op jit(solution)/shard_map/reduce_scatter | solution.py:544
  494.6 26.2 %collective-permute-start.18 = (bf16[256,2048]{1,0:T(8,128)(2,1)S(1)}, bf16[256,2048]{1,0:T(8,128)(2,1)S(1)}, u32[]{:S(2)}, u32[]{:S(2)}) collective-permute-start(bf16[256,2048]{1,0:T(8,128)(2,1)S(1)} %fusion.15), channel_id=1, source_target_pairs={{0,1},{1,2},{2,3},{3,0},{4,5},{5,6},{6,7},{7,4},{8,9},{9,10},{10,1... | collective-permute-start | bytes 3145736 | tf_op jit(solution)/shard_map/ppermute | solution.py:361
  521.1 25.4 %collective-permute-start.19 = (bf16[256,2048]{1,0:T(8,128)(2,1)S(1)}, bf16[256,2048]{1,0:T(8,128)(2,1)S(1)}, u32[]{:S(2)}, u32[]{:S(2)}) collective-permute-start(bf16[256,2048]{1,0:T(8,128)(2,1)S(1)} %add_convert_fusion.3), channel_id=1, source_target_pairs={{0,1},{1,2},{2,3},{3,0},{4,5},{5,6},{6,7},{7,4},{8,9},{9,10},{10,1... | collective-permute-start | bytes 3145736 | tf_op jit(solution)/shard_map/ppermute | solution.py:361
  546.8 26.1 %collective-permute-start.20 = (bf16[256,2048]{1,0:T(8,128)(2,1)S(1)}, bf16[256,2048]{1,0:T(8,128)(2,1)S(1)}, u32[]{:S(2)}, u32[]{:S(2)}) collective-permute-start(bf16[256,2048]{1,0:T(8,128)(2,1)S(1)} %add_convert_fusion.2), channel_id=1, source_target_pairs={{0,1},{1,2},{2,3},{3,0},{4,5},{5,6},{6,7},{7,4},{8,9},{9,10},{10,1... | collective-permute-start | bytes 3145736 | tf_op jit(solution)/shard_map/ppermute | solution.py:361
  575.0 23.5 %collective-permute-start.21 = (bf16[256,2048]{1,0:T(8,128)(2,1)S(1)}, bf16[256,2048]{1,0:T(8,128)(2,1)}, u32[]{:S(2)}, u32[]{:S(2)}) collective-permute-start(bf16[256,2048]{1,0:T(8,128)(2,1)S(1)} %multiply_convert_fusion.refs_8_), channel_id=1, source_target_pairs={{0,1},{1,2},{2,3},{3,0},{4,5},{5,6},{6,7},{7,4},{8,9},{9,10},{10,1... | collective-permute-start | bytes 3145736 | tf_op jit(solution)/shard_map/ppermute | solution.py:361
  598.5 23.0 %collective-permute-start.22 = (bf16[256,2048]{1,0:T(8,128)(2,1)}, bf16[256,2048]{1,0:T(8,128)(2,1)}, u32[]{:S(2)}, u32[]{:S(2)}) collective-permute-start(bf16[256,2048]{1,0:T(8,128)(2,1)} %collective-permute-done.21.refs_9_), channel_id=1, source_target_pairs={{0,1},{1,2},{2,3},{3,0},{4,5},{5,6},{6,7},{7,4},{8,9},{9,10},{10,1... | collective-permute-start | bytes 3145736 | tf_op jit(solution)/shard_map/ppermute | solution.py:361
  621.5 69.8 %collective-permute-start.34 = (f32[2,2048]{1,0:T(2,128)S(1)}, f32[2,2048]{1,0:T(2,128)S(1)}, u32[]{:S(2)}, u32[]{:S(2)}) collective-permute-start(f32[2,2048]{1,0:T(2,128)S(1)} %pad_maximum_fusion.10), channel_id=1, source_target_pairs={{0,2},{1,3},{2,0},{3,1},{4,6},{5,7},{6,4},{7,5},{8,10},{9,11},{10,... | collective-permute-start | bytes 49160 | tf_op jit(solution)/shard_map/ppermute | solution.py:366
  621.7 69.7 %collective-permute-start.35 = (f32[2,2048]{1,0:T(2,128)S(1)}, f32[2,2048]{1,0:T(2,128)S(1)}, u32[]{:S(2)}, u32[]{:S(2)}) collective-permute-start(f32[2,2048]{1,0:T(2,128)S(1)} %pad_maximum_fusion.10), channel_id=1, source_target_pairs={{0,3},{1,0},{2,1},{3,2},{4,7},{5,4},{6,5},{7,6},{8,11},{9,8},{10,9... | collective-permute-start | bytes 49160 | tf_op jit(solution)/shard_map/ppermute | solution.py:366
  663.4 28.0 %collective-permute-start.33 = (f32[2,2048]{1,0:T(2,128)S(1)}, f32[2,2048]{1,0:T(2,128)S(1)}, u32[]{:S(2)}, u32[]{:S(2)}) collective-permute-start(f32[2,2048]{1,0:T(2,128)S(1)} %pad_maximum_fusion.10), channel_id=1, source_target_pairs={{0,1},{1,2},{2,3},{3,0},{4,5},{5,6},{6,7},{7,4},{8,9},{9,10},{10,1... | collective-permute-start | bytes 49160 | tf_op jit(solution)/shard_map/ppermute | solution.py:366
  686.6 37.0 %collective-permute-start.30 = (bf16[4,256,1024]{2,1,0:T(8,128)(2,1)S(1)}, bf16[4,256,1024]{2,1,0:T(8,128)(2,1)}, u32[]{:S(2)}, u32[]{:S(2)}) collective-permute-start(bf16[4,256,1024]{2,1,0:T(8,128)(2,1)S(1)} %dynamic-slice_bitcast_fusion), channel_id=1, source_target_pairs={{0,4},{4,0},{8,12},{12,8},{16,20},{20,16},{24,28},{28,24},{1,5},{5... | collective-permute-start | bytes 6291464 | tf_op jit(solution)/shard_map/ppermute | solution.py:379
  689.5 28.2 %collective-permute-start.27 = (bf16[256,2048]{1,0:T(8,128)(2,1)}, bf16[256,2048]{1,0:T(8,128)(2,1)}, u32[]{:S(2)}, u32[]{:S(2)}) collective-permute-start(bf16[256,2048]{1,0:T(8,128)(2,1)} %convolution_convert_fusion.2), channel_id=1, source_target_pairs={{0,1},{1,2},{2,3},{3,0},{4,5},{5,6},{6,7},{7,4},{8,9},{9,10},{10,1... | collective-permute-start | bytes 3145736 | tf_op jit(solution)/shard_map/ppermute | solution.py:361
  700.8 29.7 %collective-permute-start.38 = (f32[8,640]{1,0:T(8,128)S(1)}, f32[8,640]{1,0:T(8,128)S(1)}, u32[]{:S(2)}, u32[]{:S(2)}) collective-permute-start(f32[8,640]{1,0:T(8,128)S(1)} %add.247), channel_id=1, source_target_pairs={{0,16},{4,20},{8,24},{12,28},{16,0},{20,4},{24,8},{28,12},{1,17},{... | collective-permute-start | bytes 61448 | tf_op jit(solution)/shard_map/ppermute | solution.py:568
  723.6 35.2 %collective-permute-start.28 = (bf16[256,2048]{1,0:T(8,128)(2,1)}, bf16[256,2048]{1,0:T(8,128)(2,1)}, u32[]{:S(2)}, u32[]{:S(2)}) collective-permute-start(bf16[256,2048]{1,0:T(8,128)(2,1)} %add_convert_fusion.1), channel_id=1, source_target_pairs={{0,1},{1,2},{2,3},{3,0},{4,5},{5,6},{6,7},{7,4},{8,9},{9,10},{10,1... | collective-permute-start | bytes 3145736 | tf_op jit(solution)/shard_map/ppermute | solution.py:361
  726.3 30.7 %collective-permute-start.31 = (bf16[2,256,1024]{2,1,0:T(8,128)(2,1)S(1)}, bf16[2,256,1024]{2,1,0:T(8,128)(2,1)}, u32[]{:S(2)}, u32[]{:S(2)}) collective-permute-start(bf16[2,256,1024]{2,1,0:T(8,128)(2,1)S(1)} %dynamic-slice_bitcast_fusion.1), channel_id=1, source_target_pairs={{0,8},{4,12},{8,0},{12,4},{16,24},{20,28},{24,16},{28,20},{1,9},{5... | collective-permute-start | bytes 3145736 | tf_op jit(solution)/shard_map/ppermute | solution.py:379
  761.6 26.1 %collective-permute-start.29 = (bf16[256,2048]{1,0:T(8,128)(2,1)}, bf16[256,2048]{1,0:T(8,128)(2,1)}, u32[]{:S(2)}, u32[]{:S(2)}) collective-permute-start(bf16[256,2048]{1,0:T(8,128)(2,1)} %add_convert_fusion), channel_id=1, source_target_pairs={{0,1},{1,2},{2,3},{3,0},{4,5},{5,6},{6,7},{7,4},{8,9},{9,10},{10,1... | collective-permute-start | bytes 3145736 | tf_op jit(solution)/shard_map/ppermute | solution.py:361
  (131 other events, 1681.5 us)
Sparse Core Ops, SparseCore 0:
  10.8 56.9 all-gather.5
  70.3 89.7 all-gather.7
  161.9 55.8 all-gather.9
  424.4 75.9 reduce-scatter.3
  503.8 116.1 reduce-scatter.7
  691.5 55.3 reduce-scatter.5
